TPU v7x, 32 devices: a whole 2x2x4 slice. The times are simulated.
32 devices in a mesh: stream: 2 (over x), dp: 16 (over z, y, core).
Axes of the slice: x: 2, y: 2, z: 4, core: 2. Of those that a mesh axis runs over, the one named last changes fastest.
Arguments:
- inputs: bfloat16 [2, 6144, 768], P('stream', 'dp'), may hold values from -6 to 6
- lengths: int32 [2, 16, 2], P(None, 'dp'), may hold values from 64 to 256, as said below
- cotangent: bfloat16 [6144, 768], P('dp'), may hold values from -6 to 6
- attn_in: bfloat16 [2, 3, 768, 768], P('stream'), may hold values from -0.21875 to 0.21875
- attn_out: bfloat16 [2, 768, 768], P('stream'), may hold values from -0.875 to 0.875
- cross_first: bfloat16 [2, 768, 768], P('stream'), may hold values from -0.21875 to 0.21875
- cross_second: bfloat16 [2, 768, 768], P('stream'), may hold values from -0.875 to 0.875
- ffn_in: bfloat16 [2, 768, 3072], P('stream'), may hold values from -0.21875 to 0.21875
- ffn_out: bfloat16 [2, 3072, 768], P('stream'), may hold values from -0.109375 to 0.109375
- gains: bfloat16 [5, 768], replicated, may hold values from 0.5 to 1.5
- biases: bfloat16 [24, 768], replicated, may hold values from -1.25 to 1.25
Outputs:
- layer_out: bfloat16 [2, 6144, 768], P('stream', 'dp')
- grad_inputs: float32 [2, 6144, 768], P('stream', 'dp')
- grad_attn_in: float32 [2, 3, 768, 768], P('stream', None, 'dp')
- grad_attn_out: float32 [2, 768, 768], P('stream', 'dp')
- grad_cross_first: float32 [2, 768, 768], P('stream', 'dp')
- grad_cross_second: float32 [2, 768, 768], P('stream', 'dp')
- grad_ffn_in: float32 [2, 768, 3072], P('stream', 'dp')
- grad_ffn_out: float32 [2, 3072, 768], P('stream', 'dp')
- grad_gains: float32 [5, 768], P(None, 'dp')
- grad_biases: float32 [24, 768], P(None, 'dp')
Inputs may be any that keep to these rules, and one draw needn't show every extreme that they name: lengths[s, i, 0] lies between 64 and 128, lengths[s, i, 1] between 129 and 256; some pair group has full-length sequences in both buckets on both sides.
All inputs are finite; a program needn't handle non-finite values.
Results may differ from a plain program's by a relative error of at most 0.025.
Values may be sent and summed in bfloat16 or wider, within the bound.
A program may use at most 384 MiB of HBM per device.

v0:
```python
import jax
import jax.numpy as jnp
from jax import lax
from jax.sharding import PartitionSpec as P

HDIM = 64
SHORT = 128
LONG = 256


eps_norm = 1e-05
low_type = jnp.bfloat16
wide_type = jnp.float32


def as_sent(shard):
    return jax.tree.map(lambda a: a.astype(jnp.bfloat16) if a.dtype == jnp.float32 else a, shard)


def shifted(shard, axis, by):
    count = lax.axis_size(axis)
    pairs = [(i, i + by) for i in range(count) if 0 <= i + by < count]
    return lax.ppermute(shard, axis, pairs)


def matmul(left_mat, right_mat):
    return jnp.dot(left_mat, right_mat, preferred_element_type=wide_type)


def matmul_tn(left_mat, right_mat):
    return lax.dot_general(
        left_mat, right_mat, (((0,), (0,)), ((), ())), preferred_element_type=wide_type
    )


def matmul_nt(left_mat, right_mat):
    return lax.dot_general(
        left_mat, right_mat, (((1,), (1,)), ((), ())), preferred_element_type=wide_type
    )


def column_sum(tensor):
    return jnp.sum(tensor.astype(wide_type), axis=0)


def norm_rows(tensor, norm_gain, norm_shift):
    centre = tensor - jnp.mean(tensor, axis=-1, keepdims=True)
    spread = jnp.mean(centre * centre, axis=-1, keepdims=True)
    return centre * lax.rsqrt(spread + eps_norm) * norm_gain + norm_shift


def norm_back(tensor, norm_gain, norm_shift, upstream):
    unused, pullback = jax.vjp(norm_rows, tensor, norm_gain, norm_shift)
    return pullback(upstream)


def gelu_exact(tensor):
    return jax.nn.gelu(tensor, approximate=False)


def key_mask(row_count, key_count, length, causal):
    columns = lax.broadcasted_iota(jnp.int32, (row_count, key_count), 1)
    allowed = columns < length
    if causal:
        allowed = allowed & (columns <= lax.broadcasted_iota(jnp.int32, (row_count, key_count), 0))
    return allowed


def split_heads(tensor):
    return tensor.reshape(tensor.shape[0], -1, HDIM)


def attend_scores(queries, key_rows, allowed):
    scores = jnp.einsum(
        "qhd,khd->hqk",
        split_heads(queries),
        split_heads(key_rows),
        preferred_element_type=wide_type,
    )
    return jnp.where(allowed[None], scores * HDIM ** (-0.5), -1e30)


def attend_forward(queries, key_rows, values, allowed):
    scores = attend_scores(queries, key_rows, allowed)
    row_max = jnp.max(scores, axis=-1, keepdims=True)
    log_total = row_max + jnp.log(jnp.sum(jnp.exp(scores - row_max), axis=-1, keepdims=True))
    softmaxed = jnp.exp(scores - log_total).astype(low_type)
    attended = jnp.einsum(
        "hqk,khd->qhd", softmaxed, split_heads(values), preferred_element_type=wide_type
    )
    return (attended.reshape(queries.shape[0], -1), log_total)


def attend_backward(queries, key_rows, values, allowed, log_total, upstream):
    softmaxed = jnp.exp(attend_scores(queries, key_rows, allowed) - log_total)
    grad_heads = split_heads(upstream)
    grad_values = jnp.einsum(
        "hqk,qhd->khd", softmaxed.astype(low_type), grad_heads, preferred_element_type=wide_type
    )
    grad_probs = jnp.einsum(
        "qhd,khd->hqk", grad_heads, split_heads(values), preferred_element_type=wide_type
    )
    grad_scores = (
        softmaxed * (grad_probs - jnp.sum(softmaxed * grad_probs, axis=-1, keepdims=True))
    ).astype(low_type)
    scale_factor = HDIM ** (-0.5)
    grad_queries = (
        jnp.einsum(
            "hqk,khd->qhd", grad_scores, split_heads(key_rows), preferred_element_type=wide_type
        )
        * scale_factor
    )
    grad_keys = (
        jnp.einsum(
            "hqk,qhd->khd", grad_scores, split_heads(queries), preferred_element_type=wide_type
        )
        * scale_factor
    )
    key_count = key_rows.shape[0]
    return (
        grad_queries.reshape(queries.shape[0], -1),
        grad_keys.reshape(key_count, -1),
        grad_values.reshape(key_count, -1),
    )


def self_forward(row_block, length, causal, w_proj, w_out, vectors):
    bias_q, bias_v, bias_o, norm_gain, norm_shift = vectors
    row_count = row_block.shape[0]
    offsets = jnp.stack([bias_q, jnp.zeros_like(bias_q), bias_v])[:, None, :]
    projected = (
        jnp.einsum("rd,cde->cre", row_block, w_proj, preferred_element_type=wide_type) + offsets
    ).astype(low_type)
    allowed = key_mask(row_count, row_count, length, causal)
    attended, log_total = attend_forward(projected[0], projected[1], projected[2], allowed)
    attended = attended.astype(low_type)
    summed = row_block.astype(wide_type) + matmul(attended, w_out) + bias_o
    return (norm_rows(summed, norm_gain, norm_shift), (projected, log_total, attended, summed))


def self_backward(row_block, length, causal, w_proj, w_out, vectors, saved_fwd, upstream):
    projected, log_total, attended, summed = saved_fwd
    row_count = row_block.shape[0]
    grad_sum, grad_gain, grad_shift = norm_back(summed, vectors[3], vectors[4], upstream)
    grad_branch = grad_sum.astype(low_type)
    grad_attended = matmul_nt(grad_branch, w_out).astype(low_type)
    allowed = key_mask(row_count, row_count, length, causal)
    grad_q, grad_k, grad_v = attend_backward(
        projected[0], projected[1], projected[2], allowed, log_total, grad_attended
    )
    grad_proj = jnp.stack([grad_q, grad_k, grad_v]).astype(low_type)
    grad_rows = grad_sum + jnp.einsum(
        "cre,cde->rd", grad_proj, w_proj, preferred_element_type=wide_type
    )
    weight_grads = (
        jnp.einsum("rd,cre->cde", row_block, grad_proj, preferred_element_type=wide_type),
        matmul_tn(attended, grad_branch),
    )
    vector_grads = (
        column_sum(grad_proj[0]),
        column_sum(grad_proj[2]),
        column_sum(grad_branch),
        grad_gain,
        grad_shift,
    )
    return (grad_rows, weight_grads, vector_grads)


def ffn_forward(hidden, w_in, w_out, vectors):
    bias_in, bias_out, norm_gain, norm_shift = vectors
    low_hidden = hidden.astype(low_type)
    inner_act = matmul(low_hidden, w_in) + bias_in
    active = gelu_exact(inner_act).astype(low_type)
    summed = hidden + matmul(active, w_out) + bias_out
    return (norm_rows(summed, norm_gain, norm_shift), (low_hidden, inner_act, active, summed))


def ffn_backward(w_in, w_out, vectors, saved_fwd, upstream):
    low_hidden, inner_act, active, summed = saved_fwd
    grad_sum, grad_gain, grad_shift = norm_back(summed, vectors[2], vectors[3], upstream)
    grad_branch = grad_sum.astype(low_type)
    unused, pullback = jax.vjp(gelu_exact, inner_act)
    grad_inner = pullback(matmul_nt(grad_branch, w_out))[0].astype(low_type)
    grad_hidden = grad_sum + matmul_nt(grad_inner, w_in)
    weight_grads = (matmul_tn(low_hidden, grad_inner), matmul_tn(active, grad_branch))
    vector_grads = (column_sum(grad_inner), column_sum(grad_branch), grad_gain, grad_shift)
    return (grad_hidden, weight_grads, vector_grads)


def cross_forward(hidden, memory, src_len, w_query, w_out, vectors):
    bias_q, bias_v, bias_o, norm_gain, norm_shift = vectors
    low_hidden = hidden.astype(low_type)
    queries = (matmul(low_hidden, w_query) + bias_q).astype(low_type)
    allowed = key_mask(hidden.shape[0], memory.shape[1], src_len, False)
    attended, log_total = attend_forward(queries, memory[0], memory[1], allowed)
    attended = (attended + bias_v).astype(low_type)
    summed = hidden + matmul(attended, w_out) + bias_o
    return (
        norm_rows(summed, norm_gain, norm_shift),
        (low_hidden, queries, log_total, attended, summed),
    )


def cross_backward(memory, src_len, w_query, w_out, vectors, saved_fwd, upstream):
    low_hidden, queries, log_total, attended, summed = saved_fwd
    grad_sum, grad_gain, grad_shift = norm_back(summed, vectors[3], vectors[4], upstream)
    grad_branch = grad_sum.astype(low_type)
    grad_attended = matmul_nt(grad_branch, w_out).astype(low_type)
    allowed = key_mask(queries.shape[0], memory.shape[1], src_len, False)
    grad_q, grad_k, grad_v = attend_backward(
        queries, memory[0], memory[1], allowed, log_total, grad_attended
    )
    grad_query = grad_q.astype(low_type)
    grad_memory = jnp.stack([grad_k, grad_v]).astype(low_type)
    grad_hidden = grad_sum + matmul_nt(grad_query, w_query)
    weight_grads = (matmul_tn(low_hidden, grad_query), matmul_tn(attended, grad_branch))
    vector_grads = (
        column_sum(grad_query),
        column_sum(grad_attended),
        column_sum(grad_branch),
        grad_gain,
        grad_shift,
    )
    return (grad_hidden, grad_memory, weight_grads, vector_grads)


def self_vectors(gain_rows, bias_rows, decoder):
    base_row = 10 if decoder else 0
    gain_row = 2 if decoder else 0
    return (
        bias_rows[base_row],
        bias_rows[base_row + 1],
        bias_rows[base_row + 2],
        gain_rows[gain_row],
        bias_rows[base_row + 3],
    )


def ffn_vectors(gain_rows, bias_rows, decoder):
    base_row = 18 if decoder else 4
    gain_row = 4 if decoder else 1
    return (
        bias_rows[base_row : base_row + 4].reshape(-1),
        bias_rows[base_row + 4],
        gain_rows[gain_row],
        bias_rows[base_row + 5],
    )


def cross_vectors(gain_rows, bias_rows):
    return (bias_rows[14], bias_rows[15], bias_rows[16], gain_rows[3], bias_rows[17])


def self_plan(decoder, vector_grads):
    base_row = 10 if decoder else 0
    gain_row = 2 if decoder else 0
    return (
        ("biases", base_row, vector_grads[0]),
        ("biases", base_row + 1, vector_grads[1]),
        ("biases", base_row + 2, vector_grads[2]),
        ("gains", gain_row, vector_grads[3]),
        ("biases", base_row + 3, vector_grads[4]),
    )


def ffn_plan(decoder, vector_grads):
    base_row = 18 if decoder else 4
    gain_row = 4 if decoder else 1
    return (
        ("biases", base_row, vector_grads[0]),
        ("biases", base_row + 4, vector_grads[1]),
        ("gains", gain_row, vector_grads[2]),
        ("biases", base_row + 5, vector_grads[3]),
    )


def cross_plan(vector_grads):
    return (
        ("biases", 14, vector_grads[0]),
        ("biases", 15, vector_grads[1]),
        ("biases", 16, vector_grads[2]),
        ("gains", 3, vector_grads[3]),
        ("biases", 17, vector_grads[4]),
    )


def accumulate(totals, weight_names, weight_grads, vector_plan):
    merged = dict(totals)
    for key_name, tensor in zip(weight_names, weight_grads):
        merged[key_name] = merged[key_name] + tensor
    for table_name, row_at, tensor in vector_plan:
        table_now = merged[table_name]
        row_block = tensor.reshape(-1, table_now.shape[1])
        merged[table_name] = table_now.at[row_at : row_at + row_block.shape[0]].add(row_block)
    return merged


def updated(progress, key_name, position, tensor):
    copied = dict(progress)
    copied[key_name] = [
        tensor if slot_index == position else entry_now
        for slot_index, entry_now in enumerate(progress[key_name])
    ]
    return copied


def with_totals(progress, totals):
    copied = dict(progress)
    copied["totals"] = totals
    return copied


def forward_pass(tensor):
    return jax.tree.map(
        lambda part, own: part.astype(own.dtype), shifted(as_sent(tensor), "stream", 1), tensor
    )


def backward_pass(tensor):
    return jax.tree.map(
        lambda part, own: part.astype(own.dtype), shifted(as_sent(tensor), "stream", -1), tensor
    )


def keep_same(progress):
    return progress


def body(
    inputs,
    lengths,
    cotangent,
    attn_in,
    attn_out,
    cross_first,
    cross_second,
    ffn_in,
    ffn_out,
    gains,
    biases,
):
    own_rows = inputs[0]
    model_width = own_rows.shape[1]
    hidden_width = ffn_in.shape[2]
    head_count = model_width // HDIM
    row_sizes = (SHORT, LONG)
    bucket_spans = ((0, SHORT), (SHORT, SHORT + LONG))
    row_pieces = [own_rows[start_row:stop_row] for start_row, stop_row in bucket_spans]
    grad_pieces = [
        cotangent[start_row:stop_row].astype(wide_type) for start_row, stop_row in bucket_spans
    ]
    src_lens = [lengths[0, 0, bucket_idx] for bucket_idx in range(2)]
    tgt_lens = [lengths[1, 0, bucket_idx] for bucket_idx in range(2)]
    w_proj = attn_in[0]
    w_attn_out = attn_out[0]
    w_first = cross_first[0]
    w_second = cross_second[0]
    w_ffn_in = ffn_in[0]
    w_ffn_out = ffn_out[0]
    gain_rows = gains.astype(wide_type)
    bias_rows = biases.astype(wide_type)
    enc_self = self_vectors(gain_rows, bias_rows, False)
    enc_ffn = ffn_vectors(gain_rows, bias_rows, False)
    dec_self = self_vectors(gain_rows, bias_rows, True)
    dec_ffn = ffn_vectors(gain_rows, bias_rows, True)
    dec_cross = cross_vectors(gain_rows, bias_rows)
    is_decoder = lax.axis_index("stream") == 1

    def blank_self(size_rows):
        return (
            jnp.zeros((3, size_rows, model_width), low_type),
            jnp.zeros((head_count, size_rows, 1), wide_type),
            jnp.zeros((size_rows, model_width), low_type),
            jnp.zeros((size_rows, model_width), wide_type),
        )

    def blank_ffn(size_rows):
        return (
            jnp.zeros((size_rows, model_width), low_type),
            jnp.zeros((size_rows, hidden_width), wide_type),
            jnp.zeros((size_rows, hidden_width), low_type),
            jnp.zeros((size_rows, model_width), wide_type),
        )

    def blank_cross(size_rows):
        return (
            jnp.zeros((size_rows, model_width), low_type),
            jnp.zeros((size_rows, model_width), low_type),
            jnp.zeros((head_count, size_rows, 1), wide_type),
            jnp.zeros((size_rows, model_width), low_type),
            jnp.zeros((size_rows, model_width), wide_type),
        )

    progress = {
        "out": [jnp.zeros((size_rows, model_width), low_type) for size_rows in row_sizes],
        "grad_in": [jnp.zeros((size_rows, model_width), wide_type) for size_rows in row_sizes],
        "send": [jnp.zeros((2, size_rows, model_width), low_type) for size_rows in row_sizes],
        "memory": [jnp.zeros((2, size_rows, model_width), low_type) for size_rows in row_sizes],
        "grad_send": [jnp.zeros((2, size_rows, model_width), low_type) for size_rows in row_sizes],
        "grad_memory": [
            jnp.zeros((2, size_rows, model_width), low_type) for size_rows in row_sizes
        ],
        "mid": [jnp.zeros((size_rows, model_width), wide_type) for size_rows in row_sizes],
        "grad_mid": [jnp.zeros((size_rows, model_width), wide_type) for size_rows in row_sizes],
        "totals": {
            "proj": jnp.zeros(w_proj.shape, wide_type),
            "attn_out": jnp.zeros(w_attn_out.shape, wide_type),
            "first": jnp.zeros(w_first.shape, wide_type),
            "second": jnp.zeros(w_second.shape, wide_type),
            "ffn_in": jnp.zeros(w_ffn_in.shape, wide_type),
            "ffn_out": jnp.zeros(w_ffn_out.shape, wide_type),
            "gains": jnp.zeros(gains.shape, wide_type),
            "biases": jnp.zeros(biases.shape, wide_type),
        },
    }
    progress["self_saved"] = [blank_self(size_rows) for size_rows in row_sizes]
    progress["ffn_saved"] = [blank_ffn(size_rows) for size_rows in row_sizes]
    progress["cross_saved"] = [blank_cross(size_rows) for size_rows in row_sizes]

    def encoder_core(micro_idx):
        h_one, self_saved = self_forward(
            row_pieces[micro_idx], src_lens[micro_idx], False, w_proj, w_attn_out, enc_self
        )
        encoded, ffn_saved = ffn_forward(h_one, w_ffn_in, w_ffn_out, enc_ffn)
        return (encoded.astype(low_type), self_saved, ffn_saved)

    def encoder_forward_step(progress, micro_idx):
        low_memory, self_saved, ffn_saved = encoder_core(micro_idx)
        memory = jnp.stack([matmul(low_memory, w_first), matmul(low_memory, w_second)]).astype(
            low_type
        )
        progress = updated(progress, "out", micro_idx, low_memory)
        progress = updated(progress, "send", micro_idx, memory)
        progress = updated(progress, "self_saved", micro_idx, self_saved)
        progress = updated(progress, "ffn_saved", micro_idx, ffn_saved)
        return progress

    def decoder_head(micro_idx):
        return self_forward(
            row_pieces[micro_idx], tgt_lens[micro_idx], True, w_proj, w_attn_out, dec_self
        )

    def decoder_tail(mid_rows, memory, micro_idx):
        crossed, cross_saved = cross_forward(
            mid_rows, memory, src_lens[micro_idx], w_first, w_second, dec_cross
        )
        decoded, ffn_saved = ffn_forward(crossed, w_ffn_in, w_ffn_out, dec_ffn)
        return (decoded, cross_saved, ffn_saved)

    def decoder_head_step(progress, micro_idx):
        mid_rows, self_saved = decoder_head(micro_idx)
        progress = updated(progress, "mid", micro_idx, mid_rows)
        progress = updated(progress, "self_saved", micro_idx, self_saved)
        return progress

    def decoder_tail_step(progress, micro_idx):
        decoded, cross_saved, ffn_saved = decoder_tail(
            progress["mid"][micro_idx], progress["memory"][micro_idx], micro_idx
        )
        progress = updated(progress, "out", micro_idx, decoded.astype(low_type))
        progress = updated(progress, "cross_saved", micro_idx, cross_saved)
        progress = updated(progress, "ffn_saved", micro_idx, ffn_saved)
        return progress

    def decoder_back_step(progress, micro_idx):
        memory = progress["memory"][micro_idx]
        self_saved = progress["self_saved"][micro_idx]
        cross_saved = progress["cross_saved"][micro_idx]
        ffn_saved = progress["ffn_saved"][micro_idx]
        grad_h_two, ffn_w, ffn_v = ffn_backward(
            w_ffn_in, w_ffn_out, dec_ffn, ffn_saved, grad_pieces[micro_idx]
        )
        grad_h_one, grad_memory, cross_w, cross_v = cross_backward(
            memory, src_lens[micro_idx], w_first, w_second, dec_cross, cross_saved, grad_h_two
        )
        grad_rows, self_w, self_v = self_backward(
            row_pieces[micro_idx],
            tgt_lens[micro_idx],
            True,
            w_proj,
            w_attn_out,
            dec_self,
            self_saved,
            grad_h_one,
        )
        totals = accumulate(
            progress["totals"],
            ("ffn_in", "ffn_out", "first", "second", "proj", "attn_out"),
            ffn_w + cross_w + self_w,
            ffn_plan(True, ffn_v) + cross_plan(cross_v) + self_plan(True, self_v),
        )
        progress = updated(progress, "grad_in", micro_idx, grad_rows)
        progress = updated(progress, "grad_send", micro_idx, grad_memory)
        return with_totals(progress, totals)

    def encoder_top_step(progress, micro_idx):
        low_memory = progress["out"][micro_idx]
        ffn_saved = progress["ffn_saved"][micro_idx]
        grad_memory = progress["grad_memory"][micro_idx]
        grad_encoded = matmul_nt(grad_memory[0], w_first) + matmul_nt(grad_memory[1], w_second)
        grad_h_one, ffn_w, ffn_v = ffn_backward(
            w_ffn_in, w_ffn_out, enc_ffn, ffn_saved, grad_encoded
        )
        projections = (matmul_tn(low_memory, grad_memory[0]), matmul_tn(low_memory, grad_memory[1]))
        totals = accumulate(
            progress["totals"],
            ("first", "second", "ffn_in", "ffn_out"),
            projections + ffn_w,
            ffn_plan(False, ffn_v),
        )
        progress = updated(progress, "grad_mid", micro_idx, grad_h_one)
        return with_totals(progress, totals)

    def encoder_bottom_step(progress, micro_idx):
        self_saved = progress["self_saved"][micro_idx]
        grad_rows, self_w, self_v = self_backward(
            row_pieces[micro_idx],
            src_lens[micro_idx],
            False,
            w_proj,
            w_attn_out,
            enc_self,
            self_saved,
            progress["grad_mid"][micro_idx],
        )
        totals = accumulate(
            progress["totals"], ("proj", "attn_out"), self_w, self_plan(False, self_v)
        )
        progress = updated(progress, "grad_in", micro_idx, grad_rows)
        return with_totals(progress, totals)

    def enc_zero(progress):
        return encoder_forward_step(progress, 0)

    def dec_zero(progress):
        return decoder_head_step(progress, 0)

    def enc_one(progress):
        return encoder_forward_step(progress, 1)

    def dec_one(progress):
        return decoder_tail_step(decoder_head_step(progress, 1), 0)

    def dec_two(progress):
        return decoder_back_step(decoder_tail_step(progress, 1), 1)

    def enc_three(progress):
        return encoder_bottom_step(encoder_top_step(progress, 1), 1)

    def dec_three(progress):
        return decoder_back_step(progress, 0)

    def enc_four(progress):
        return encoder_top_step(progress, 0)

    def enc_five(progress):
        return encoder_bottom_step(progress, 0)

    progress = lax.cond(is_decoder, dec_zero, enc_zero, progress)
    progress = updated(progress, "memory", 0, forward_pass(progress["send"][0]))
    progress = lax.cond(is_decoder, dec_one, enc_one, progress)
    progress = updated(progress, "memory", 1, forward_pass(progress["send"][1]))
    progress = lax.cond(is_decoder, dec_two, keep_same, progress)
    progress = updated(progress, "grad_memory", 1, backward_pass(progress["grad_send"][1]))
    progress = lax.cond(is_decoder, dec_three, enc_three, progress)
    progress = updated(progress, "grad_memory", 0, backward_pass(progress["grad_send"][0]))
    progress = lax.cond(is_decoder, keep_same, enc_four, progress)
    progress = lax.cond(is_decoder, keep_same, enc_five, progress)
    totals = progress["totals"]
    owned = (
        lax.psum_scatter(totals["proj"], "dp", scatter_dimension=1, tiled=True),
        lax.psum_scatter(totals["attn_out"], "dp", scatter_dimension=0, tiled=True),
        lax.psum_scatter(totals["first"], "dp", scatter_dimension=0, tiled=True),
        lax.psum_scatter(totals["second"], "dp", scatter_dimension=0, tiled=True),
        lax.psum_scatter(totals["ffn_in"], "dp", scatter_dimension=0, tiled=True),
        lax.psum_scatter(totals["ffn_out"], "dp", scatter_dimension=0, tiled=True),
        lax.psum_scatter(totals["gains"], "dp", scatter_dimension=1, tiled=True),
        lax.psum_scatter(totals["biases"], "dp", scatter_dimension=1, tiled=True),
    )
    owned_gains, owned_biases = lax.psum((owned[6], owned[7]), "stream")
    layer_out = jnp.concatenate(progress["out"], axis=0)[None]
    grad_inputs = jnp.concatenate(progress["grad_in"], axis=0)[None]
    return (
        layer_out,
        grad_inputs,
        owned[0][None],
        owned[1][None],
        owned[2][None],
        owned[3][None],
        owned[4][None],
        owned[5][None],
        owned_gains,
        owned_biases,
    )


def solution(mesh):
    return jax.shard_map(
        body,
        mesh=mesh,
        in_specs=(
            P("stream", "dp", None),
            P(None, "dp", None),
            P("dp", None),
            P("stream", None, None, None),
            P("stream", None, None),
            P("stream", None, None),
            P("stream", None, None),
            P("stream", None, None),
            P("stream", None, None),
            P(),
            P(),
        ),
        out_specs=(
            P("stream", "dp", None),
            P("stream", "dp", None),
            P("stream", None, "dp", None),
            P("stream", "dp", None),
            P("stream", "dp", None),
            P("stream", "dp", None),
            P("stream", "dp", None),
            P("stream", "dp", None),
            P(None, "dp"),
            P(None, "dp"),
        ),
        check_vma=False,
    )
```

profile of v0, /device:TPU:0, one launch (start us, length us, event | category | flops | bytes accessed | tf_op | source)
XLA Modules:
  0.0 1244.2 jit_solution(9599477456773693169)
XLA Ops:
  14.8 32.1 %conditional.10 = (bf16[128,768]{1,0:T(8,128)(2,1)}, f32[128,3072]{1,0:T(8,128)}, bf16[128,3072]{1,0:T(8,128)(2,1)}, f32[128,768]{1,0:T(8,128)S(1)}, f32[128,768...) conditional(s32[]{:T(128)} %convert_element_type.402, ...), branch_computations={%region_0.7_spmd, %region_7.12_spmd} | conditional | flops 2195328512 | bytes 44831268
  15.6 4.1 fusion.12
  31.0 7.9 fusion.2
  39.6 3.6 fusion.232
  47.1 17.2 %collective-permute-start = (bf16[2,128,768]{1,2,0:T(8,128)(2,1)S(1)}, bf16[2,128,768]{1,2,0:T(8,128)(2,1)S(1)}, u32[]{:S(2)}, u32[]{:S(2)}) collective-permute-start(bf16[2,128,768]{1,2,0:T(8,128)(2,1)S(1)} %copy.242), channel_id=1, source_target_pairs={{0,16},{1,17},{2,18},{3,19},{4,20},{5,21},{6,22},{7,23},{8,24},{9,... | collective-permute-start | bytes 1179656 | tf_op jit(solution)/shard_map/ppermute | solution.py:23
  66.8 44.5 %conditional.11 = (bf16[128,768]{1,0:T(8,128)(2,1)}, bf16[128,768]{1,0:T(8,128)(2,1)}, f32[12,128,1]{1,0,2:T(8,128)}, bf16[128,768]{0,1:T(8,128)(2,1)}, f32[128,...) conditional(s32[]{:T(128)} %convert_element_type.402, ...), branch_computations={%region_12.19_spmd, %region_19.30_spmd} | conditional | flops 4497213440 | bytes 80060048
  67.7 4.4 fusion.43
  81.5 11.0 fusion.29
  93.2 5.2 fusion.238
  117.9 15.2 %collective-permute-done.1 = bf16[2,256,768]{1,2,0:T(8,128)(2,1)} collective-permute-done((bf16[2,256,768]{1,2,0:T(8,128)(2,1)}, bf16[2,256,768]{1,2,0:T(8,128)(2,1)}, u32[]{:S(2)}, u32[]{:S(2)}) %collective-permute-start.1) | collective-permute-done | bytes 786464 | tf_op jit(solution)/shard_map/ppermute | solution.py:23
  133.1 29.4 %conditional.12 = (bf16[256,768]{1,0:T(8,128)(2,1)}, f32[256,3072]{1,0:T(8,128)}, bf16[256,3072]{1,0:T(8,128)(2,1)}, f32[256,768]{1,0:T(8,128)}, f32[256,768]{1,...) conditional(s32[]{:T(128)} %convert_element_type.402, ...), branch_computations={%region_30.31_spmd, %region_31.62_spmd} | conditional | flops 12697853952 | bytes 348670912 | solution.py:563
  133.1 4.9 broadcast_in_dim.230
  138.0 4.2 broadcast_in_dim.231
  142.2 3.5 broadcast_in_dim.241
  167.7 160.4 %collective-permute-done.2 = bf16[2,256,768]{2,1,0:T(8,128)(2,1)S(1)} collective-permute-done((bf16[2,256,768]{2,1,0:T(8,128)(2,1)}, bf16[2,256,768]{2,1,0:T(8,128)(2,1)S(1)}, u32[]{:S(2)}, u32[]{:S(2)}) %collective-permute-start.2) | collective-permute-done | bytes 786464 | tf_op jit(solution)/shard_map/ppermute | solution.py:23
  328.2 153.8 %conditional.13 = (f32[128,768]{1,0:T(8,128)}, f32[256,768]{1,0:T(8,128)}, bf16[2,128,768]{1,2,0:T(8,128)(2,1)}, f32[768,768]{0,1:T(8,128)}, f32[24,768]{1,0:T(8...) conditional(s32[]{:T(128)} %convert_element_type.402, ...), branch_computations={%region_62.81_spmd, %region_81.110_spmd} | conditional | flops 9046919168 | bytes 287514176 | solution.py:565
  341.8 11.3 convert_reduce_fusion.8
  353.7 5.3 multiply_reduce_fusion.20
  378.4 7.4 bitcast_add_fusion.4
  385.8 9.9 copy.249
  395.7 9.4 bitcast_add_fusion.3
  420.2 9.6 copy.250
  429.9 9.3 bitcast_add_fusion.2
  441.3 3.8 bitcast_add_fusion.5
  452.4 3.7 convolution_add_fusion.21
  459.2 3.9 convolution_add_fusion.20
  484.4 25.2 %collective-permute-done.3 = bf16[2,128,768]{2,1,0:T(8,128)(2,1)S(1)} collective-permute-done((bf16[2,128,768]{2,1,0:T(8,128)(2,1)S(1)}, bf16[2,128,768]{2,1,0:T(8,128)(2,1)S(1)}, u32[]{:S(2)}, u32[]{:S(2)}) %collective-permute-start.3) | collective-permute-done | bytes 393248 | tf_op jit(solution)/shard_map/ppermute | solution.py:23
  509.6 50.6 %conditional.14 = (f32[128,768]{1,0:T(8,128)S(1)}, f32[24,768]{1,0:T(8,128)}, f32[768,3072]{0,1:T(8,128)}, f32[3072,768]{0,1:T(8,128)}, f32[768,768]{1,0:T(8,128...) conditional(s32[]{:T(128)} %convert_element_type.402, (bf16[2,128,768]{2,1,0:T(8,128)(2,1)S(1)}, ...), branch_computations={%region_110.119_spmd, %region_119.120_spmd} | conditional | flops 3057452032 | bytes 155490144 | solution.py:567
  513.5 7.0 convert_reduce_fusion.21
  523.4 12.3 bitcast_add_fusion.12
  542.6 4.0 convolution_add_fusion.29
  549.8 3.7 convolution_add_fusion.26
  556.6 3.7 convolution_add_fusion.27
  560.3 35.8 %conditional.15 = ((f32[128,768]{1,0:T(8,128)}, f32[768,768]{0,1:T(8,128)}, f32[24,768]{1,0:T(8,128)}, f32[5,768]{1,0:T(8,128)}, f32[3,768,768]{1,2,0:T(8,128)})) conditional(s32[]{:T(128)} %convert_element_type.402, (f32[1,768]{1,0:T(1,128)S(1)}, f32[128,768]{1,0:T(8,128)S(1)}, f32[128,768]{1,0:T(8,128)}, s32[]{:T(128)}, ...), branch_computations={%region_120.131_spmd, %region_131.132_spmd} | conditional | flops 1342537216 | bytes 63050716 | solution.py:568
  571.7 7.2 bitcast_add_fusion.14
  587.6 4.2 fusion.207
  604.0 8.2 copy.264
  612.3 9.7 copy.266
  622.1 9.7 copy.267
  636.0 17.4 %reduce-scatter.25.cloned.1.call-done = f32[48,5]{1,0:T(8,128)} async-done(((f32[768,5]{1,0:T(8,128)}), f32[48,5]{1,0:T(8,128)}) %reduce-scatter.25.cloned.1.call-update) | async-done | bytes 976
  654.2 57.7 %reduce-scatter.27.cloned.1.call-done = f32[48,24]{1,0:T(8,128)} async-done(((f32[768,24]{1,0:T(8,128)}), f32[48,24]{1,0:T(8,128)}) %reduce-scatter.27.cloned.1.call-update) | async-done | bytes 4624
  712.7 8.6 all-reduce.2
  721.3 56.9 %reduce-scatter.15.cloned.1.call-done = f32[48,768]{1,0:T(8,128)} async-done(((f32[768,768]{1,0:T(8,128)}), f32[48,768]{1,0:T(8,128)}) %reduce-scatter.15.cloned.1.call-update) | async-done | bytes 147472 | tf_op jit(solution)/shard_map/reduce_scatter | solution.py:572
  778.2 66.7 %reduce-scatter.17.cloned.1.call-done = f32[48,768]{1,0:T(8,128)} async-done(((f32[768,768]{1,0:T(8,128)}), f32[48,768]{1,0:T(8,128)}) %reduce-scatter.17.cloned.1.call-update) | async-done | bytes 147472 | tf_op jit(solution)/shard_map/reduce_scatter | solution.py:573
  844.9 66.2 %reduce-scatter.19.cloned.1.call-done = f32[48,768]{1,0:T(8,128)} async-done(((f32[768,768]{1,0:T(8,128)}), f32[48,768]{1,0:T(8,128)}) %reduce-scatter.19.cloned.1.call-update) | async-done | bytes 147472 | tf_op jit(solution)/shard_map/reduce_scatter | solution.py:574
  911.2 94.0 %reduce-scatter.13.cloned.1.call-done = f32[3,48,768]{2,1,0:T(8,128)} async-done(((f32[3,768,768]{2,1,0:T(8,128)}), f32[3,48,768]{2,1,0:T(8,128)}) %reduce-scatter.13.cloned.1.call-update) | async-done | bytes 442384 | tf_op jit(solution)/shard_map/reduce_scatter | solution.py:571
  1005.1 115.6 %reduce-scatter.21.cloned.1.call-done = f32[48,3072]{1,0:T(8,128)} async-done(((f32[768,3072]{1,0:T(8,128)}), f32[48,3072]{1,0:T(8,128)}) %reduce-scatter.21.cloned.1.call-update) | async-done | bytes 589840 | tf_op jit(solution)/shard_map/reduce_scatter | solution.py:575
  1120.8 116.4 %reduce-scatter.23.cloned.1.call-done = f32[192,768]{1,0:T(8,128)} async-done(((f32[3072,768]{1,0:T(8,128)}), f32[192,768]{1,0:T(8,128)}) %reduce-scatter.23.cloned.1.call-update) | async-done | bytes 589840 | tf_op jit(solution)/shard_map/reduce_scatter | solution.py:576
  (358 shorter events, 195.5 us)
Async XLA Ops:
  7.2 646.2 %reduce-scatter.25.cloned.1.call-start = ((), (), s32[]{:S(2)}) async-start(), calls=%async_computation.14 | async-start | bytes 417792
  11.8 54.3 %copy-start.106 = (f32[1,768]{1,0:T(1,128)}, f32[1,768]{1,0:T(1,128)S(1)}, u32[]{:S(2)}) copy-start(f32[1,768]{1,0:T(1,128)S(1)} %get-tuple-element.2361) | copy-start | bytes 9220
  19.8 5.3 copy-start.9
  39.6 4.7 copy-start.6
  47.1 18.9 %collective-permute-start = (bf16[2,128,768]{1,2,0:T(8,128)(2,1)S(1)}, bf16[2,128,768]{1,2,0:T(8,128)(2,1)S(1)}, u32[]{:S(2)}, u32[]{:S(2)}) collective-permute-start(bf16[2,128,768]{1,2,0:T(8,128)(2,1)S(1)} %copy.242), channel_id=1, source_target_pairs={{0,16},{1,17},{2,18},{3,19},{4,20},{5,21},{6,22},{7,23},{8,24},{9,... | collective-permute-start | bytes 1179656 | tf_op jit(solution)/shard_map/ppermute | solution.py:23
  66.8 5.2 copy-start.104
  66.8 5.2 copy-start.108
  93.2 7.3 copy-start.112
  93.2 7.3 copy-start.136
  93.2 9.4 copy-start.7
  98.4 5.7 copy-start.16
  111.3 21.8 %copy-start.5 = (bf16[1,768,768]{2,1,0:T(8,128)(2,1)S(1)}, bf16[1,768,768]{2,1,0:T(8,128)(2,1)}, u32[]{:S(2)}) copy-start(bf16[1,768,768]{2,1,0:T(8,128)(2,1)} %param.120) | copy-start | bytes 3538948
  111.3 21.8 %copy-start.8 = (bf16[1,768,768]{2,1,0:T(8,128)(2,1)S(1)}, bf16[1,768,768]{2,1,0:T(8,128)(2,1)}, u32[]{:S(2)}) copy-start(bf16[1,768,768]{2,1,0:T(8,128)(2,1)} %param.119) | copy-start | bytes 3538948
  111.3 21.8 %copy-start.130 = (f32[1,768]{1,0:T(1,128)S(1)}, f32[1,768]{1,0:T(1,128)}, u32[]{:S(2)}) copy-start(f32[1,768]{1,0:T(1,128)} %get-tuple-element.2344) | copy-start | bytes 9220
  113.8 19.3 %collective-permute-start.1 = (bf16[2,256,768]{1,2,0:T(8,128)(2,1)}, bf16[2,256,768]{1,2,0:T(8,128)(2,1)}, u32[]{:S(2)}, u32[]{:S(2)}) collective-permute-start(bf16[2,256,768]{1,2,0:T(8,128)(2,1)} %copy.245), channel_id=1, source_target_pairs={{0,16},{1,17},{2,18},{3,19},{4,20},{5,21},{6,22},{7,23},{8,24},{9,... | collective-permute-start | bytes 2359304 | tf_op jit(solution)/shard_map/ppermute | solution.py:23
  164.7 163.4 %collective-permute-start.2 = (bf16[2,256,768]{2,1,0:T(8,128)(2,1)}, bf16[2,256,768]{2,1,0:T(8,128)(2,1)S(1)}, u32[]{:S(2)}, u32[]{:S(2)}) collective-permute-start(bf16[2,256,768]{2,1,0:T(8,128)(2,1)} %copy.247), channel_id=1, source_target_pairs={{16,0},{17,1},{18,2},{19,3},{20,4},{21,5},{22,6},{23,7},{24,8},{25... | collective-permute-start | bytes 2359304 | tf_op jit(solution)/shard_map/ppermute | solution.py:23
  329.2 6.2 copy-start.113
  335.4 6.4 copy-start.24
  340.2 12.9 %copy-start.168 = (f32[256]{0:T(256)}, f32[256]{0:T(256)S(1)}, u32[]{:S(2)}) copy-start(f32[256]{0:T(256)S(1)} %negate_multiply_fusion.9) | copy-start | bytes 3076 | tf_op jit(solution)/shard_map/cond
  341.8 11.3 copy-start.63
  341.8 11.3 copy-start.154
  341.8 11.8 copy-start.110
  353.7 5.4 copy-start.161
  395.7 13.6 %copy-start.144 = (f32[768]{0:T(1024)S(1)}, f32[768]{0:T(1024)}, u32[]{:S(2)}) copy-start(f32[768]{0:T(1024)} %get-tuple-element.2162) | copy-start | bytes 9220 | tf_op jit(solution)/shard_map/cond
  395.7 15.7 %copy-start.40 = (bf16[12,256,64]{1,2,0:T(8,128)(2,1)S(1)}, bf16[12,256,64]{1,2,0:T(8,128)(2,1)}, u32[]{:S(2)}) copy-start(bf16[12,256,64]{1,2,0:T(8,128)(2,1)} %fusion.135) | copy-start | bytes 1179652 | tf_op jit(solution)/shard_map/cond
  420.2 9.6 copy-start.64
  429.8 9.3 copy-start.59
  429.8 9.3 copy-start.91
  429.8 9.3 copy-start.92
  429.8 9.3 copy-start.93
  429.9 9.3 copy-start.167
  429.9 9.3 copy-start.178
  441.3 5.9 copy-start.163
  483.1 26.5 %collective-permute-start.3 = (bf16[2,128,768]{2,1,0:T(8,128)(2,1)S(1)}, bf16[2,128,768]{2,1,0:T(8,128)(2,1)S(1)}, u32[]{:S(2)}, u32[]{:S(2)}) collective-permute-start(bf16[2,128,768]{2,1,0:T(8,128)(2,1)S(1)} %copy.258), channel_id=1, source_target_pairs={{16,0},{17,1},{18,2},{19,3},{20,4},{21,5},{22,6},{23,7},{24,8},{25... | collective-permute-start | bytes 1179656 | tf_op jit(solution)/shard_map/ppermute | solution.py:23
  509.6 50.6 %copy-start.107 = (f32[1,768]{1,0:T(1,128)S(1)}, f32[1,768]{1,0:T(1,128)}, u32[]{:S(2)}) copy-start(f32[1,768]{1,0:T(1,128)} %copy-done.106) | copy-start | bytes 9220
  513.5 7.0 slice-start
  513.5 7.0 slice-start.1
  513.5 7.0 slice-start.2
  523.4 12.3 copy-start
  571.7 15.9 %copy-start.84 = (f32[128,768]{1,0:T(8,128)S(1)}, f32[128,768]{1,0:T(8,128)}, u32[]{:S(2)}) copy-start(f32[128,768]{1,0:T(8,128)} %copy-done.83) | copy-start | bytes 1179652 | tf_op jit(solution)/shard_map/cond
  587.6 5.6 copy-start.22
  597.8 114.1 %reduce-scatter.27.cloned.1.call-start = ((), (), s32[]{:S(2)}) async-start(), calls=%async_computation.15 | async-start | bytes 417792
  599.7 178.6 %reduce-scatter.15.cloned.1.call-start = ((), (), s32[]{:S(2)}) async-start(), calls=%async_computation.9 | async-start | bytes 2506752 | tf_op jit(solution)/shard_map/reduce_scatter | solution.py:572
  602.8 242.1 %reduce-scatter.17.cloned.1.call-start = ((), (), s32[]{:S(2)}) async-start(), calls=%async_computation.10 | async-start | bytes 2506752 | tf_op jit(solution)/shard_map/reduce_scatter | solution.py:573
  603.4 307.8 %reduce-scatter.19.cloned.1.call-start = ((), (), s32[]{:S(2)}) async-start(), calls=%async_computation.11 | async-start | bytes 2506752 | tf_op jit(solution)/shard_map/reduce_scatter | solution.py:574
  604.0 401.2 %reduce-scatter.13.cloned.1.call-start = ((), (), s32[]{:S(2)}) async-start(), calls=%async_computation.8 | async-start | bytes 7520256 | tf_op jit(solution)/shard_map/reduce_scatter | solution.py:571
  612.2 508.6 %reduce-scatter.21.cloned.1.call-start = ((), (), s32[]{:S(2)}) async-start(), calls=%async_computation.12 | async-start | bytes 10027008 | tf_op jit(solution)/shard_map/reduce_scatter | solution.py:575
  622.0 615.1 %reduce-scatter.23.cloned.1.call-start = ((), (), s32[]{:S(2)}) async-start(), calls=%async_computation.13 | async-start | bytes 10027008 | tf_op jit(solution)/shard_map/reduce_scatter | solution.py:576
  (32 other events, 73.6 us)
Sparse Core Ops, SparseCore 0:
  597.9 55.4 reduce-scatter.24
  657.3 54.5 reduce-scatter.26
  716.2 61.9 reduce-scatter.14
  782.9 61.9 reduce-scatter.16
  849.1 61.9 reduce-scatter.18
  916.1 88.9 reduce-scatter.12
  1009.8 110.9 reduce-scatter.20
  1126.0 111.1 reduce-scatter.22
where the time goes:
time: 1260 us; the launch traced here: 1240 us
  waiting for transfers between devices  793 us (63%)
  matrix products  172 us (14%)
  local copies, waits for them, and re-layouts  154 us (12%)
  other arithmetic  55.8 us (4%)
  loops' own time  24.7 us (2%)
  starting transfers between devices  22.2 us (2%)
  between operations  14.4 us (1%)
    ppermute x4, waiting for transfers between devices, shifted(): return lax.ppermute(shard, axis, pairs)  201 us
    reduce_scatter x1, waiting for transfers between devices, body(): lax.psum_scatter(totals['ffn_out'], 'dp', scatter_dimension=0, tiled=True)  116 us
    reduce_scatter x1, waiting for transfers between devices, body(): lax.psum_scatter(totals['ffn_in'], 'dp', scatter_dimension=0, tiled=True)  116 us
    reduce_scatter x1, waiting for transfers between devices, body(): lax.psum_scatter(totals['proj'], 'dp', scatter_dimension=1, tiled=True)  94 us
    unnamed x10, waiting for transfers between devices  76.3 us
    reduce_scatter x1, waiting for transfers between devices, body(): lax.psum_scatter(totals['first'], 'dp', scatter_dimension=0, tiled=True)  66.7 us
    reduce_scatter x1, waiting for transfers between devices, body(): lax.psum_scatter(totals['second'], 'dp', scatter_dimension=0, tiled=True)  66.2 us
    reduce_scatter x1, waiting for transfers between devices, body(): lax.psum_scatter(totals['attn_out'], 'dp', scatter_dimension=0, tiled=True)  56.9 us
  transfers between devices with their start and end apart: 12, of which 11 were waited for; matrix products, arithmetic and copies ran while one was open for 4% of the time, Pallas kernels for 0%

commit v1 on v0

--- a/solution.py
+++ b/solution.py
@@ -1,11 +1,152 @@
+import functools
+
 import jax
 import jax.numpy as jnp
 from jax import lax
+from jax.experimental import pallas as pl
+from jax.experimental.pallas import tpu as pltpu
 from jax.sharding import PartitionSpec as P
 
 HDIM = 64
 SHORT = 128
 LONG = 256
+MESH = pl.DeviceIdType.MESH
+bf16, f32 = jnp.bfloat16, jnp.float32
+PIECE = 48
+
+
+def rs_kernel(nz, chunks, g_ref, vec_ref, *refs):
+    out_refs = refs[:7]
+    (keep, crecv, yrecv, zrecv, vbuf, vzbuf,
+     keep_sem, csend, crecv_sem, ysend, yrecv_sem, zsend, zrecv_sem,
+     vsend, vrecv_sem, vzsend, vzrecv_sem) = refs[7:]
+    me = lax.axis_index("dp")
+    st = lax.axis_index("stream")
+    z, y, c = me // 4, (me // 2) % 2, me % 2
+    core_id = {"dp": z * 4 + y * 2 + (1 - c)}
+    y_id = {"dp": z * 4 + (1 - y) * 2 + c}
+    x_id = {"stream": 1 - st}
+
+    def z_id(dz):
+        return {"dp": lax.rem(z + dz, nz) * 4 + y * 2 + c}
+
+    barrier = pltpu.get_barrier_semaphore()
+    peers = [core_id, y_id, x_id] + [z_id(d) for d in range(1, nz)]
+    for p in peers:
+        pl.semaphore_signal(barrier, inc=1, device_id=p, device_id_type=MESH)
+    pl.semaphore_wait(barrier, len(peers))
+
+    def rcopy(src, dst, ss, rs, dev):
+        return pltpu.make_async_remote_copy(src_ref=src, dst_ref=dst, send_sem=ss, recv_sem=rs,
+                                            device_id=dev, device_id_type=MESH)
+    n = len(chunks)
+    starts = [sum(chunks[:i]) for i in range(n)]
+    rows = [pl.ds(starts[i] * PIECE, chunks[i] * PIECE) for i in range(n)]
+    ccopy = [rcopy(g_ref.at[:, :, 1 - c, rows[i]], crecv.at[:, :, rows[i]], csend.at[i], crecv_sem.at[i], core_id) for i in range(n)]
+    kcopy = [pltpu.make_async_copy(g_ref.at[:, :, c, rows[i]], keep.at[:, :, rows[i]], keep_sem.at[i]) for i in range(n)]
+    ycopy = [rcopy(crecv.at[:, 1 - y, rows[i]], yrecv.at[:, rows[i]], ysend.at[i], yrecv_sem.at[i], y_id) for i in range(n)]
+    zcopy = [[rcopy(yrecv.at[lax.rem(z + d, nz), rows[i]], zrecv.at[d - 1, rows[i]], zsend.at[i, d - 1], zrecv_sem.at[i, d - 1], z_id(d))
+              for d in range(1, nz)] for i in range(n)]
+    vcopy = [rcopy(vbuf.at[0], vbuf.at[1], vsend.at[0], vrecv_sem.at[0], core_id),
+             rcopy(vbuf.at[2], vbuf.at[3], vsend.at[1], vrecv_sem.at[1], y_id)]
+    vz = [rcopy(vbuf.at[4], vzbuf.at[d - 1], vzsend.at[d - 1], vzrecv_sem.at[d - 1], z_id(d)) for d in range(1, nz)]
+    vx = rcopy(vbuf.at[5], vbuf.at[6], vsend.at[2], vrecv_sem.at[2], x_id)
+    vbuf[0] = vec_ref[...]
+    vcopy[0].start()
+    for i in range(n):
+        ccopy[i].start()
+        kcopy[i].start()
+
+    def c_add(i):
+        ccopy[i].wait()
+        kcopy[i].wait()
+        for p in range(starts[i], starts[i] + chunks[i]):
+            def bodyf(j, carry):
+                zz, yy = j // 2, j % 2
+                sl = pl.ds(p * PIECE, PIECE)
+                crecv[zz, yy, sl] = (crecv[zz, yy, sl].astype(f32) + keep[zz, yy, sl].astype(f32)).astype(bf16)
+                return carry
+            lax.fori_loop(0, nz * 2, bodyf, 0)
+        ycopy[i].start()
+
+    def y_add(i):
+        ycopy[i].wait()
+        for p in range(starts[i], starts[i] + chunks[i]):
+            def bodyf(zz, carry):
+                sl = pl.ds(p * PIECE, PIECE)
+                yrecv[zz, sl] = (yrecv[zz, sl].astype(f32) + crecv[zz, y, sl].astype(f32)).astype(bf16)
+                return carry
+            lax.fori_loop(0, nz, bodyf, 0)
+        for d in range(1, nz):
+            zcopy[i][d - 1].start()
+
+    def z_add(i):
+        for d in range(1, nz):
+            zcopy[i][d - 1].wait()
+        for p in range(starts[i], starts[i] + chunks[i]):
+            sl = pl.ds(p * PIECE, PIECE)
+            tot = yrecv[z, sl].astype(f32)
+            for d in range(1, nz):
+                tot = tot + zrecv[d - 1, sl].astype(f32)
+            if p < 4:
+                out_refs[0][pl.ds(p * PIECE, PIECE)] = tot
+            elif p < 8:
+                out_refs[1][:, pl.ds((p - 4) * 768, 768)] = tot
+            elif p < 11:
+                out_refs[p - 6][...] = tot
+            else:
+                out_refs[5][p - 11] = tot
+
+    for t in range(n + 2):
+        if t < n:
+            c_add(t)
+        if 1 <= t <= n:
+            y_add(t - 1)
+        if t == 0:
+            vcopy[0].wait()
+            vbuf[2] = vbuf[0] + vbuf[1]
+            vcopy[1].start()
+        if t == 1:
+            vcopy[1].wait()
+            vbuf[4] = vbuf[2] + vbuf[3]
+            for cp in vz:
+                cp.start()
+        if t == 2:
+            for cp in vz:
+                cp.wait()
+            tot = vbuf[4]
+            for d in range(1, nz):
+                tot = tot + vzbuf[d - 1]
+            vbuf[5] = tot
+            vx.start()
+        if t >= 2:
+            z_add(t - 2)
+    vx.wait()
+    out_refs[6][...] = vbuf[5] + vbuf[6]
+
+
+def reduce_scatter(nz, g, vec, chunks=(2,) * 7):
+    n = len(chunks)
+    r = g.shape[3]
+    w = g.shape[4]
+    shapes = [(192, w), (48, 4 * w), (48, w), (48, w), (48, w), (3, 48, w), vec.shape]
+    return pl.pallas_call(
+        functools.partial(rs_kernel, nz, chunks),
+        out_shape=[jax.ShapeDtypeStruct(s, f32) for s in shapes],
+        in_specs=[pl.BlockSpec(memory_space=pl.ANY), pl.BlockSpec(memory_space=pltpu.VMEM)],
+        out_specs=[pl.BlockSpec(memory_space=pltpu.VMEM)] * 7,
+        scratch_shapes=[
+            pltpu.VMEM((nz, 2, r, w), bf16), pltpu.VMEM((nz, 2, r, w), bf16),
+            pltpu.VMEM((nz, r, w), bf16), pltpu.VMEM((nz - 1, r, w), bf16),
+            pltpu.VMEM((7,) + vec.shape, f32), pltpu.VMEM((nz - 1,) + vec.shape, f32),
+            pltpu.SemaphoreType.DMA((n,)), pltpu.SemaphoreType.DMA((n,)), pltpu.SemaphoreType.DMA((n,)),
+            pltpu.SemaphoreType.DMA((n,)), pltpu.SemaphoreType.DMA((n,)),
+            pltpu.SemaphoreType.DMA((n, nz - 1)), pltpu.SemaphoreType.DMA((n, nz - 1)),
+            pltpu.SemaphoreType.DMA((3,)), pltpu.SemaphoreType.DMA((3,)),
+            pltpu.SemaphoreType.DMA((nz - 1,)), pltpu.SemaphoreType.DMA((nz - 1,)),
+        ],
+        compiler_params=pltpu.CompilerParams(collective_id=0, has_side_effects=True, vmem_limit_bytes=56 << 20),
+    )(g, vec)
 
 
 eps_norm = 1e-05
@@ -567,17 +708,35 @@
     progress = lax.cond(is_decoder, keep_same, enc_four, progress)
     progress = lax.cond(is_decoder, keep_same, enc_five, progress)
     totals = progress["totals"]
-    owned = (
-        lax.psum_scatter(totals["proj"], "dp", scatter_dimension=1, tiled=True),
-        lax.psum_scatter(totals["attn_out"], "dp", scatter_dimension=0, tiled=True),
-        lax.psum_scatter(totals["first"], "dp", scatter_dimension=0, tiled=True),
-        lax.psum_scatter(totals["second"], "dp", scatter_dimension=0, tiled=True),
-        lax.psum_scatter(totals["ffn_in"], "dp", scatter_dimension=0, tiled=True),
-        lax.psum_scatter(totals["ffn_out"], "dp", scatter_dimension=0, tiled=True),
-        lax.psum_scatter(totals["gains"], "dp", scatter_dimension=1, tiled=True),
-        lax.psum_scatter(totals["biases"], "dp", scatter_dimension=1, tiled=True),
-    )
-    owned_gains, owned_biases = lax.psum((owned[6], owned[7]), "stream")
+    dp_size = lax.axis_size("dp")
+    if dp_size % 4 == 0 and model_width // dp_size == PIECE:
+        nz = dp_size // 4
+        split = lambda t: t.astype(low_type).reshape(nz, 2, 2, -1, t.shape[-1])
+        parts = [
+            split(totals["ffn_out"]),
+            split(totals["ffn_in"]).reshape(nz, 2, 2, PIECE, 4, model_width).swapaxes(3, 4).reshape(nz, 2, 2, 4 * PIECE, model_width),
+            split(totals["second"]),
+            split(totals["first"]),
+            split(totals["attn_out"]),
+        ] + [split(totals["proj"][j]) for j in range(3)]
+        packed = jnp.concatenate(parts, axis=3)
+        rows = jnp.concatenate([totals["gains"], totals["biases"], jnp.zeros((3, model_width), f32)])
+        s_out, s_in, s_second, s_first, s_attn, s_proj, rows = reduce_scatter(nz, packed, rows, (1,) * 14)
+        owned = (s_proj, s_attn, s_first, s_second, s_in, s_out)
+        own_cols = lax.dynamic_slice_in_dim(rows, lax.axis_index("dp") * PIECE, PIECE, 1)
+        owned_gains, owned_biases = own_cols[:5], own_cols[5:29]
+    else:
+        owned = (
+            lax.psum_scatter(totals["proj"], "dp", scatter_dimension=1, tiled=True),
+            lax.psum_scatter(totals["attn_out"], "dp", scatter_dimension=0, tiled=True),
+            lax.psum_scatter(totals["first"], "dp", scatter_dimension=0, tiled=True),
+            lax.psum_scatter(totals["second"], "dp", scatter_dimension=0, tiled=True),
+            lax.psum_scatter(totals["ffn_in"], "dp", scatter_dimension=0, tiled=True),
+            lax.psum_scatter(totals["ffn_out"], "dp", scatter_dimension=0, tiled=True),
+            lax.psum_scatter(totals["gains"], "dp", scatter_dimension=1, tiled=True),
+            lax.psum_scatter(totals["biases"], "dp", scatter_dimension=1, tiled=True),
+        )
+        owned_gains, owned_biases = lax.psum((owned[6], owned[7]), "stream")
     layer_out = jnp.concatenate(progress["out"], axis=0)[None]
     grad_inputs = jnp.concatenate(progress["grad_in"], axis=0)[None]
     return (

time: 1260 us -> 802 us (0.64)
  waiting for transfers between devices: 793 us -> 210 us
  Pallas kernels: 0 us -> 115 us
  local copies, waits for them, and re-layouts: 154 us -> 181 us
  other arithmetic: 55.8 us -> 73.4 us
  starting transfers between devices: 22.2 us -> 6.06 us
  between operations: 14.4 us -> 1.23 us
    reduce_scatter x6 -> x0, waiting for transfers between devices: 516 us -> none  [the longest x1 116 us: body(): lax.psum_scatter(totals['ffn_out'], 'dp', scatter_dimension=0, tiled=True)]
    pallas_call x0 -> x1, Pallas kernels: none -> 115 us  [reduce_scatter(): pl.pallas_call(functools.partial(rs_kernel, nz, chunks), out_shape=[jax.S...]
    unnamed x10 -> x0, waiting for transfers between devices: 76.3 us -> none
    cond x98 -> x80, local copies, waits for them, and re-layouts: 37.8 us -> 4.63 us  [the longest x2 19.4 us: body(): progress = lax.cond(is_decoder, keep_same, enc_four, progress)]
    another operation x54 -> x58, local copies, waits for them, and re-layouts: 50.5 us -> 70.9 us
    unnamed x16 -> x58, local copies, waits for them, and re-layouts: 5.87 us -> 23.2 us
    ppermute x4, starting transfers between devices: 21.9 us -> 6.06 us  [shifted(): return lax.ppermute(shard, axis, pairs)]
    convert_element_type x0 -> x2, local copies, waits for them, and re-layouts: none -> 13.4 us  [body(): split = lambda t: t.astype(low_type).reshape(nz, 2, 2, -1, t.shape[-1])]
  transfers between devices with their start and end apart: 12 -> 4, of which waited for: 11 -> 4; matrix products, arithmetic and copies ran while one was open for 4% -> 1% of each run, Pallas kernels for 0% -> 0%
where the time goes in v1:
time: 802 us; the launch traced here: 788 us
  waiting for transfers between devices  210 us (26%)
  local copies, waits for them, and re-layouts  181 us (23%)
  matrix products  169 us (21%)
  Pallas kernels  115 us (14%)
  other arithmetic  73.4 us (9%)
  loops' own time  32.8 us (4%)
    ppermute x4, waiting for transfers between devices, shifted(): return lax.ppermute(shard, axis, pairs)  210 us
    pallas_call x1, Pallas kernels, reduce_scatter(): pl.pallas_call(functools.partial(rs_kernel, nz, chunks), out_shape=[jax.S...  115 us
    another operation x57, local copies, waits for them, and re-layouts  61.1 us
    dot_general x10, matrix products, matmul_tn(): lax.dot_general(left_mat, right_mat, (((0,), (0,)), ((), ())), preferred_...  51.9 us
    dot_general x10, matrix products, matmul_nt(): lax.dot_general(left_mat, right_mat, (((1,), (1,)), ((), ())), preferred_...  39.1 us
    dot_general x10, matrix products, matmul(): return jnp.dot(left_mat, right_mat, preferred_element_type=wide_type)  37.4 us
    unnamed x58, local copies, waits for them, and re-layouts  23.2 us
    scatter-add x16, local copies, waits for them, and re-layouts, accumulate(): table_now.at[row_at:row_at + row_block.shape[0]].add(row_block)  21.8 us
  transfers between devices with their start and end apart: 4, of which 4 were waited for; matrix products, arithmetic and copies ran while one was open for 1% of the time, Pallas kernels for 0%

profile of v1, /device:TPU:0, one launch (start us, length us, event | category | flops | bytes accessed | tf_op | source)
XLA Modules:
  0.0 787.9 jit_solution(15502033487596236770)
XLA Ops:
  8.4 36.2 %conditional.12 = (bf16[128,768]{1,0:T(8,128)(2,1)}, f32[128,3072]{1,0:T(8,128)}, bf16[128,3072]{1,0:T(8,128)(2,1)}, f32[128,768]{1,0:T(8,128)}, f32[128,768]{1,...) conditional(s32[]{:T(128)} %convert_element_type.479, ...), branch_computations={%region_0.7_spmd, %region_7.12_spmd} | conditional | flops 2195328512 | bytes 47559176
  8.5 3.3 fusion.12
  24.4 7.9 fusion.2
  33.0 4.3 fusion.235
  47.1 8.2 %collective-permute-done = bf16[2,128,768]{1,2,0:T(8,128)(2,1)S(1)} collective-permute-done((bf16[2,128,768]{1,2,0:T(8,128)(2,1)S(1)}, bf16[2,128,768]{1,2,0:T(8,128)(2,1)S(1)}, u32[]{:S(2)}, u32[]{:S(2)}) %collective-permute-start) | collective-permute-done | bytes 393248 | tf_op jit(solution)/shard_map/ppermute | solution.py:164
  56.1 53.5 %conditional.13 = (bf16[128,768]{1,0:T(8,128)(2,1)}, bf16[128,768]{1,0:T(8,128)(2,1)}, f32[12,128,1]{1,0,2:T(8,128)}, bf16[128,768]{0,1:T(8,128)(2,1)}, f32[128,...) conditional(s32[]{:T(128)} %convert_element_type.479, ...), branch_computations={%region_12.19_spmd, %region_19.30_spmd} | conditional | flops 4497213440 | bytes 76914272
  56.2 4.3 fusion.43
  71.2 11.0 %fusion.29 = (bf16[256,3072]{1,0:T(8,128)(2,1)}, f32[256,3072]{1,0:T(8,128)}) fusion(f32[3072]{0:T(1024)S(1)} %add.857, bf16[256,768]{1,0:T(8,128)(2,1)} %fusion.49, bf16[768,3072]{1,0:T(8,128)(2,1)} %get-tuple-element.1165), kind=kOutput, calls=%fused_computation.79 | convolution fusion | flops 1259864064 | bytes 9842688 | tf_op jit(solution)/shard_map/cond/branch_0_fun/dot_general | solution.py:168
  82.9 5.2 fusion.241
  116.2 14.6 %collective-permute-done.1 = bf16[2,256,768]{1,2,0:T(8,128)(2,1)} collective-permute-done((bf16[2,256,768]{1,2,0:T(8,128)(2,1)}, bf16[2,256,768]{1,2,0:T(8,128)(2,1)}, u32[]{:S(2)}, u32[]{:S(2)}) %collective-permute-start.1) | collective-permute-done | bytes 786464 | tf_op jit(solution)/shard_map/ppermute | solution.py:164
  130.8 29.6 %conditional.14 = (bf16[256,768]{1,0:T(8,128)(2,1)}, f32[256,3072]{1,0:T(8,128)}, bf16[256,3072]{1,0:T(8,128)(2,1)}, f32[256,768]{1,0:T(8,128)}, f32[256,768]{1,...) conditional(s32[]{:T(128)} %convert_element_type.479, ...), branch_computations={%region_30.31_spmd, %region_31.62_spmd} | conditional | flops 12697853952 | bytes 348670912 | solution.py:704
  130.8 4.9 broadcast_in_dim.244
  135.7 4.2 broadcast_in_dim.245
  139.9 3.5 broadcast_in_dim.247
  165.6 159.5 %collective-permute-done.2 = bf16[2,256,768]{2,1,0:T(8,128)(2,1)S(1)} collective-permute-done((bf16[2,256,768]{2,1,0:T(8,128)(2,1)}, bf16[2,256,768]{2,1,0:T(8,128)(2,1)S(1)}, u32[]{:S(2)}, u32[]{:S(2)}) %collective-permute-start.2) | collective-permute-done | bytes 786464 | tf_op jit(solution)/shard_map/ppermute | solution.py:164
  325.1 152.9 %conditional.15 = (f32[128,768]{1,0:T(8,128)}, f32[256,768]{1,0:T(8,128)}, bf16[2,128,768]{1,2,0:T(8,128)(2,1)}, f32[768,768]{0,1:T(8,128)}, f32[24,768]{1,0:T(8...) conditional(s32[]{:T(128)} %convert_element_type.479, ...), branch_computations={%region_62.81_spmd, %region_81.110_spmd} | conditional | flops 9046919168 | bytes 287571552 | solution.py:706
  332.4 3.3 multiply_reduce_fusion.21
  338.8 11.3 %convert_reduce_fusion.8 = (f32[3072]{0:T(1024)}, bf16[256,3072]{1,0:T(8,128)(2,1)}) fusion(f32[256,3072]{1,0:T(8,128)} %get-tuple-element.1235, bf16[256,768]{1,0:T(8,128)(2,1)S(1)} %get-tuple-element.2060, bf16[3072,768]{1,0:T(8,128)(2,1)S(1)} %copy-done.23), kind=kOutput, calls=%fused_computation.331 | convolution fusion | flops 1266152448 | bytes 9842688 | tf_op jit(solution)/shard_map/cond/branch_0_fun/dot_general | solution.py:178
  350.8 5.3 multiply_reduce_fusion.20
  375.5 7.4 bitcast_add_fusion.4
  382.9 9.7 %copy.177 = f32[768,3072]{0,1:T(8,128)} copy(f32[768,3072]{1,0:T(8,128)} %get-tuple-element.1924) | data formatting | bytes 18874368 | tf_op jit(solution)/shard_map
  392.7 9.4 %bitcast_add_fusion.3 = f32[768,3072]{0,1:T(8,128)} fusion(f32[768,3072]{0,1:T(8,128)} %copy.177, bf16[256,3072]{1,0:T(8,128)(2,1)} %get-tuple-element.2062, bf16[256,768]{1,0:T(8,128)(2,1)} %get-tuple-element.1249), kind=kOutput, calls=%fused_computation.323 | convolution fusion | flops 1210318848 | bytes 20840448 | tf_op jit(solution)/shard_map/cond/branch_0_fun/dot_general | solution.py:172
  416.5 9.7 %copy.178 = f32[3072,768]{0,1:T(8,128)} copy(f32[3072,768]{1,0:T(8,128)} %get-tuple-element.1926) | data formatting | bytes 18874368 | tf_op jit(solution)/shard_map
  426.2 9.3 %bitcast_add_fusion.2 = f32[3072,768]{0,1:T(8,128)} fusion(f32[3072,768]{0,1:T(8,128)} %copy.178, bf16[256,768]{1,0:T(8,128)(2,1)S(1)} %copy-done.68, bf16[256,3072]{1,0:T(8,128)(2,1)} %get-tuple-element.1251), kind=kOutput, calls=%fused_computation.322 | convolution fusion | flops 1210318848 | bytes 20840448 | tf_op jit(solution)/shard_map/cond/branch_0_fun/dot_general | solution.py:172
  437.6 3.8 bitcast_add_fusion.5
  445.6 3.1 copy.179
  448.7 3.7 convolution_add_fusion.21
  452.4 3.1 copy.143
  455.5 3.9 convolution_add_fusion.20
  483.0 27.4 %collective-permute-done.3 = bf16[2,128,768]{2,1,0:T(8,128)(2,1)} collective-permute-done((bf16[2,128,768]{2,1,0:T(8,128)(2,1)S(1)}, bf16[2,128,768]{2,1,0:T(8,128)(2,1)}, u32[]{:S(2)}, u32[]{:S(2)}) %collective-permute-start.3) | collective-permute-done | bytes 393248 | tf_op jit(solution)/shard_map/ppermute | solution.py:164
  510.4 59.0 %conditional.16 = (f32[128,768]{1,0:T(8,128)}, f32[24,768]{1,0:T(8,128)}, f32[768,3072]{0,1:T(8,128)}, f32[5,768]{1,0:T(8,128)}, bf16[4,2,2,192,768]{4,3,2,1,0:T...) conditional(s32[]{:T(128)} %convert_element_type.479, ...), branch_computations={%region_110.119_spmd, %region_119.120_spmd} | conditional | flops 3060990976 | bytes 121660168 | solution.py:708
  519.1 6.9 convert_reduce_fusion.21
  526.0 8.9 %bitcast_add_fusion.13 = f32[768,3072]{0,1:T(8,128)} fusion(f32[768,3072]{0,1:T(8,128)} %get-tuple-element.1303, bf16[128,3072]{1,0:T(8,128)(2,1)S(1)} %get-tuple-element.2084, bf16[128,768]{1,0:T(8,128)(2,1)} %get-tuple-element.1304), kind=kOutput, calls=%fused_computation.532 | convolution fusion | flops 606339072 | bytes 19857408 | tf_op jit(solution)/shard_map/cond/branch_0_fun/dot_general | solution.py:172
  535.0 4.8 fusion.182
  539.8 6.7 copy.157
  553.5 4.8 convolution_add_fusion.27
  563.7 3.1 copy.189
  569.4 6.8 convert_element_type.484
  576.2 6.7 copy.198
  582.9 9.8 %reshape_reshape.3 = bf16[4,2,2,48,4,768]{5,4,3,2,1,0:T(4,128)(2,1)} reshape(bf16[768,3072]{1,0:T(8,128)(2,1)} %copy.198) | data formatting | bytes 9437184 | tf_op jit(solution)/shard_map/reshape;reshape | solution.py:717
  592.7 5.5 copy.199
  602.5 5.7 copy-done.20
  608.2 44.8 %conditional.17 = (f32[128,768]{1,0:T(8,128)}, f32[24,768]{1,0:T(8,128)}, f32[5,768]{1,0:T(8,128)}, bf16[4,2,2,48,768]{4,3,2,1,0:T(8,128)(2,1)}, bf16[4,2,2,48,7...) conditional(s32[]{:T(128)} %convert_element_type.479, ...), branch_computations={%region_120.131_spmd, %region_131.132_spmd} | conditional | flops 1346076160 | bytes 76420120
  618.9 8.1 %copy.195 = f32[3,768,768]{2,1,0:T(8,128)} copy(f32[3,768,768]{1,2,0:T(8,128)} %get-tuple-element.2005) | data formatting | bytes 14155776 | tf_op jit(solution)/shard_map
  627.1 4.2 bitcast_add_fusion.14
  641.7 4.5 fusion.209
  649.5 3.3 fusion.205
  663.0 114.9 %shard_map.186 = (f32[192,768]{1,0:T(8,128)}, f32[48,3072]{1,0:T(8,128)}, f32[48,768]{1,0:T(8,128)}, f32[48,768]{1,0:T(8,128)}, f32[48,768]{1,0:T(8,128)}, /*index=5*/f32[3,48,768]{2,1,0:T(8,128)}, f32[32,768]{1,0:T(8,128)}) custom-call(bf16[4,2,2,672,768]{4,3,2,1,0:T(8,128)(2,1)} %constant_dynamic-update-slice_fusion.g_ref, ...), custom_call_target="tpu_custom_call" | custom-call | tf_op jit(solution)/shard_map/pallas_call | solution.py:133
  (374 shorter events, 207.9 us)
Async XLA Ops:
  2.3 6.0 copy-start.124
  2.3 6.0 copy-start.126
  2.3 6.0 copy-start.134
  2.4 6.0 copy-start.136
  33.0 8.8 %copy-start.5 = (bf16[768,768]{1,0:T(8,128)(2,1)S(1)}, bf16[768,768]{1,0:T(8,128)(2,1)}, u32[]{:S(2)}) copy-start(bf16[768,768]{1,0:T(8,128)(2,1)} %get-tuple-element.1141) | copy-start | bytes 3538948 | tf_op jit(solution)/shard_map/conditional.3
  37.3 5.8 copy-start.12
  44.8 10.5 %collective-permute-start = (bf16[2,128,768]{1,2,0:T(8,128)(2,1)S(1)}, bf16[2,128,768]{1,2,0:T(8,128)(2,1)S(1)}, u32[]{:S(2)}, u32[]{:S(2)}) collective-permute-start(bf16[2,128,768]{1,2,0:T(8,128)(2,1)S(1)} %copy.170), channel_id=1, source_target_pairs={{0,16},{1,17},{2,18},{3,19},{4,20},{5,21},{6,22},{7,23},{8,24},{9,... | collective-permute-start | bytes 1179656 | tf_op jit(solution)/shard_map/ppermute | solution.py:164
  82.9 10.2 %copy-start.6 = (bf16[768,768]{1,0:T(8,128)(2,1)S(1)}, bf16[768,768]{1,0:T(8,128)(2,1)}, u32[]{:S(2)}) copy-start(bf16[768,768]{1,0:T(8,128)(2,1)} %get-tuple-element.1172) | copy-start | bytes 3538948 | tf_op jit(solution)/shard_map/conditional.4
  88.1 6.4 copy-start.13
  109.6 21.2 %copy-start.4 = (bf16[1,768,768]{2,1,0:T(8,128)(2,1)S(1)}, bf16[1,768,768]{2,1,0:T(8,128)(2,1)}, u32[]{:S(2)}) copy-start(bf16[1,768,768]{2,1,0:T(8,128)(2,1)} %param.120) | copy-start | bytes 3538948
  109.6 21.2 %copy-start.7 = (bf16[1,768,768]{2,1,0:T(8,128)(2,1)S(1)}, bf16[1,768,768]{2,1,0:T(8,128)(2,1)}, u32[]{:S(2)}) copy-start(bf16[1,768,768]{2,1,0:T(8,128)(2,1)} %param.119) | copy-start | bytes 3538948
  109.6 21.2 %copy-start.133 = (f32[1,768]{1,0:T(1,128)S(1)}, f32[1,768]{1,0:T(1,128)}, u32[]{:S(2)}) copy-start(f32[1,768]{1,0:T(1,128)} %get-tuple-element.2211) | copy-start | bytes 9220
  112.0 18.7 %collective-permute-start.1 = (bf16[2,256,768]{1,2,0:T(8,128)(2,1)}, bf16[2,256,768]{1,2,0:T(8,128)(2,1)}, u32[]{:S(2)}, u32[]{:S(2)}) collective-permute-start(bf16[2,256,768]{1,2,0:T(8,128)(2,1)} %copy.173), channel_id=1, source_target_pairs={{0,16},{1,17},{2,18},{3,19},{4,20},{5,21},{6,22},{7,23},{8,24},{9,... | collective-permute-start | bytes 2359304 | tf_op jit(solution)/shard_map/ppermute | solution.py:164
  162.6 162.5 %collective-permute-start.2 = (bf16[2,256,768]{2,1,0:T(8,128)(2,1)}, bf16[2,256,768]{2,1,0:T(8,128)(2,1)S(1)}, u32[]{:S(2)}, u32[]{:S(2)}) collective-permute-start(bf16[2,256,768]{2,1,0:T(8,128)(2,1)} %copy.175), channel_id=1, source_target_pairs={{16,0},{17,1},{18,2},{19,3},{20,4},{21,5},{22,6},{23,7},{24,8},{25... | collective-permute-start | bytes 2359304 | tf_op jit(solution)/shard_map/ppermute | solution.py:164
  332.4 6.4 copy-start.23
  338.8 11.3 %copy-start.67 = (bf16[256,768]{1,0:T(8,128)(2,1)}, bf16[256,768]{1,0:T(8,128)(2,1)S(1)}, u32[]{:S(2)}) copy-start(bf16[256,768]{1,0:T(8,128)(2,1)S(1)} %get-tuple-element.2060) | copy-start | bytes 1179652 | tf_op jit(solution)/shard_map/cond
  338.8 11.3 %copy-start.158 = (f32[256]{0:T(256)S(1)}, f32[256]{0:T(256)}, u32[]{:S(2)}) copy-start(f32[256]{0:T(256)} %get-tuple-element.2171) | copy-start | bytes 3076 | tf_op jit(solution)/shard_map/cond
  392.7 9.4 %copy-start.153 = (f32[3072]{0:T(1024)S(1)}, f32[3072]{0:T(1024)}, u32[]{:S(2)}) copy-start(f32[3072]{0:T(1024)} %get-tuple-element.2061) | copy-start | bytes 36868 | tf_op jit(solution)/shard_map/cond
  392.7 10.8 %copy-start.146 = (f32[768]{0:T(1024)S(1)}, f32[768]{0:T(1024)}, u32[]{:S(2)}) copy-start(f32[768]{0:T(1024)} %get-tuple-element.2059) | copy-start | bytes 9220 | tf_op jit(solution)/shard_map/cond
  392.7 12.9 %copy-start.145 = (f32[768]{0:T(1024)S(1)}, f32[768]{0:T(1024)}, u32[]{:S(2)}) copy-start(f32[768]{0:T(1024)} %get-tuple-element.2025) | copy-start | bytes 9220 | tf_op jit(solution)/shard_map/cond
  392.7 15.0 %copy-start.44 = (bf16[12,256,64]{1,2,0:T(8,128)(2,1)S(1)}, bf16[12,256,64]{1,2,0:T(8,128)(2,1)}, u32[]{:S(2)}) copy-start(bf16[12,256,64]{1,2,0:T(8,128)(2,1)} %fusion.135) | copy-start | bytes 1179652 | tf_op jit(solution)/shard_map/cond
  392.7 19.6 %copy-start.147 = (f32[768]{0:T(1024)S(1)}, f32[768]{0:T(1024)}, u32[]{:S(2)}) copy-start(f32[768]{0:T(1024)} %get-tuple-element.2057) | copy-start | bytes 9220 | tf_op jit(solution)/shard_map/cond
  392.7 21.7 %copy-start.167 = (f32[768]{0:T(1024)S(1)}, f32[768]{0:T(1024)}, u32[]{:S(2)}) copy-start(f32[768]{0:T(1024)} %get-tuple-element.2024) | copy-start | bytes 9220 | tf_op jit(solution)/shard_map/cond
  416.5 9.7 %copy-start.68 = (bf16[256,768]{1,0:T(8,128)(2,1)S(1)}, bf16[256,768]{1,0:T(8,128)(2,1)}, u32[]{:S(2)}) copy-start(bf16[256,768]{1,0:T(8,128)(2,1)} %copy-done.67) | copy-start | bytes 1179652 | tf_op jit(solution)/shard_map/cond
  426.1 9.4 %copy-start.63 = (f32[256,768]{1,0:T(8,128)S(1)}, f32[256,768]{1,0:T(8,128)}, u32[]{:S(2)}) copy-start(f32[256,768]{1,0:T(8,128)} %copy-done.62) | copy-start | bytes 2359300 | tf_op jit(solution)/shard_map/cond
  426.1 9.4 %copy-start.94 = (bf16[1,256,768]{2,1,0:T(8,128)(2,1)S(1)}, bf16[1,256,768]{2,1,0:T(8,128)(2,1)}, u32[]{:S(2)}) copy-start(bf16[1,256,768]{2,1,0:T(8,128)(2,1)} %copy.139) | copy-start | bytes 1179652 | tf_op jit(solution)/shard_map/cond
  426.1 9.4 %copy-start.95 = (bf16[1,256,768]{2,1,0:T(8,128)(2,1)S(1)}, bf16[1,256,768]{2,1,0:T(8,128)(2,1)}, u32[]{:S(2)}) copy-start(bf16[1,256,768]{2,1,0:T(8,128)(2,1)} %copy.140) | copy-start | bytes 1179652 | tf_op jit(solution)/shard_map/cond
  426.1 9.4 %copy-start.96 = (bf16[1,256,768]{2,1,0:T(8,128)(2,1)S(1)}, bf16[1,256,768]{2,1,0:T(8,128)(2,1)}, u32[]{:S(2)}) copy-start(bf16[1,256,768]{2,1,0:T(8,128)(2,1)} %copy.141) | copy-start | bytes 1179652 | tf_op jit(solution)/shard_map/cond
  426.2 9.4 %copy-start.171 = (f32[256]{0:T(256)S(1)}, f32[256]{0:T(256)}, u32[]{:S(2)}) copy-start(f32[256]{0:T(256)} %copy-done.170) | copy-start | bytes 3076 | tf_op jit(solution)/shard_map/cond
  426.2 9.4 %copy-start.187 = (bf16[3,768,768]{2,1,0:T(8,128)(2,1)S(1)}, bf16[3,768,768]{2,1,0:T(8,128)(2,1)}, u32[]{:S(2)}) copy-start(bf16[3,768,768]{2,1,0:T(8,128)(2,1)} %get-tuple-element.1244) | copy-start | bytes 10616836 | tf_op jit(solution)/shard_map/cond
  437.6 5.9 copy-start.166
  479.2 31.2 %collective-permute-start.3 = (bf16[2,128,768]{2,1,0:T(8,128)(2,1)S(1)}, bf16[2,128,768]{2,1,0:T(8,128)(2,1)}, u32[]{:S(2)}, u32[]{:S(2)}) collective-permute-start(bf16[2,128,768]{2,1,0:T(8,128)(2,1)S(1)} %copy.187), channel_id=1, source_target_pairs={{16,0},{17,1},{18,2},{19,3},{20,4},{21,5},{22,6},{23,7},{24,8},{25... | collective-permute-start | bytes 1179656 | tf_op jit(solution)/shard_map/ppermute | solution.py:164
  526.0 9.0 %slice-start = ((s8[9437184]{0:T(1024)(128)(4,1)}), s8[4194304]{0:T(1024)(128)(4,1)S(1)}, s32[]{:S(2)}) async-start(s8[9437184]{0:T(1024)(128)(4,1)} %bitcast.492), calls=%async_computation | async-start | bytes 8388608 | tf_op jit(solution)/shard_map/cond
  526.0 9.0 %slice-start.1 = ((s8[9437184]{0:T(1024)(128)(4,1)}), s8[4194304]{0:T(1024)(128)(4,1)S(1)}, s32[]{:S(2)}) async-start(s8[9437184]{0:T(1024)(128)(4,1)} %bitcast.492), calls=%async_computation.1 | async-start | bytes 8388608 | tf_op jit(solution)/shard_map/cond
  526.0 9.0 %slice-start.2 = ((s8[9437184]{0:T(1024)(128)(4,1)}), s8[1048576]{0:T(1024)(128)(4,1)S(1)}, s32[]{:S(2)}) async-start(s8[9437184]{0:T(1024)(128)(4,1)} %bitcast.492), calls=%async_computation.2 | async-start | bytes 2097152 | tf_op jit(solution)/shard_map/cond
  569.4 6.8 copy-start.37
  582.9 15.3 %slice-start.5 = ((s8[4718592]{0:T(1024)(128)(4,1)}), s8[524288]{0:T(1024)(128)(4,1)S(1)}, s32[]{:S(2)}) async-start(s8[4718592]{0:T(1024)(128)(4,1)} %bitcast.534), calls=%async_computation.5 | async-start | bytes 1048576
  592.7 5.5 slice-start.6
  602.5 5.7 copy-start.20
  617.8 9.2 %copy-start.102 = (bf16[1,128,768]{2,1,0:T(8,128)(2,1)}, bf16[1,128,768]{2,1,0:T(8,128)(2,1)S(1)}, u32[]{:S(2)}) copy-start(bf16[1,128,768]{2,1,0:T(8,128)(2,1)S(1)} %copy.162) | copy-start | bytes 589828 | tf_op jit(solution)/shard_map/conditional.5
  618.4 8.7 %copy-start.103 = (bf16[1,128,768]{2,1,0:T(8,128)(2,1)}, bf16[1,128,768]{2,1,0:T(8,128)(2,1)S(1)}, u32[]{:S(2)}) copy-start(bf16[1,128,768]{2,1,0:T(8,128)(2,1)S(1)} %copy.163) | copy-start | bytes 589828 | tf_op jit(solution)/shard_map/conditional.5
  618.9 8.2 %copy-start.104 = (bf16[1,128,768]{2,1,0:T(8,128)(2,1)}, bf16[1,128,768]{2,1,0:T(8,128)(2,1)S(1)}, u32[]{:S(2)}) copy-start(bf16[1,128,768]{2,1,0:T(8,128)(2,1)S(1)} %copy.164) | copy-start | bytes 589828 | tf_op jit(solution)/shard_map/conditional.5
  641.7 5.8 copy-start.21
  777.9 6.1 copy-start.114
  777.9 6.8 copy-start.113
  777.9 7.4 copy-start.112
  777.9 8.1 %copy-start.106 = (f32[48,3072]{1,0:T(8,128)S(1)}, f32[48,3072]{1,0:T(8,128)}, u32[]{:S(2)}) copy-start(f32[48,3072]{1,0:T(8,128)} %get-tuple-element.1501) | copy-start | bytes 1769476
  780.8 6.0 copy-start.105
  (33 other events, 82.4 us)

commit v2 on v0

--- a/solution.py
+++ b/solution.py
@@ -1,11 +1,632 @@
+import functools
+
 import jax
 import jax.numpy as jnp
 from jax import lax
+from jax.experimental import pallas as pl
+from jax.experimental.pallas import tpu as pltpu
 from jax.sharding import PartitionSpec as P
 
 HDIM = 64
 SHORT = 128
 LONG = 256
+ROWS = SHORT + LONG
+PIECE = 48
+PIECES = 14
+MESH = pl.DeviceIdType.MESH
+bf16, f32 = jnp.bfloat16, jnp.float32
+VMEM_LIMIT = 64 << 20
+
+
+def dot_nn(a, b):
+    return jnp.dot(a, b, preferred_element_type=f32)
+
+
+def dot_nt(a, b):
+    return lax.dot_general(a, b, (((1,), (1,)), ((), ())), preferred_element_type=f32)
+
+
+def dot_tn(a, b):
+    return lax.dot_general(a, b, (((0,), (0,)), ((), ())), preferred_element_type=f32)
+
+
+def cols(j, width):
+    return pl.ds(pl.multiple_of(j * width, width), width)
+
+
+def step_kernel(
+    nz, width, hidden,
+    lens, vec, bias_in, x_hbm, cot_hbm, wproj_hbm, wo_hbm, wfirst_hbm, wsecond_hbm, win_hbm, wout_hbm,
+    out_rows, out_grad, out_own, out_z, out_vec,
+    wproj, wo, wfirst, wsecond, win, wout, wx,
+    xb, up, mem, obuf, hlow, dg, kv, acc, grad, u_self, u_cross, u_ffn, gr, grp, lt, ltp, ysend, yrecv, gmem, vg, vbuf, vzbuf,
+    load_sem, wx_send, wx_recv, mem_send, mem_recv, gm_send, gm_recv, gk_send, gk_recv, lt_send, lt_recv, gr_send, gr_recv,
+    y_send, y_recv, z_send, z_recv, own_sem, io_sem, v_send, v_recv, vz_send, vz_recv,
+):
+    st = lax.axis_index("stream")
+    me = lax.axis_index("dp")
+    z, y, c = me // 4, (me // 2) % 2, me % 2
+    is_dec = st == 1
+    is_enc = st == 0
+    core_id = {"dp": z * 4 + y * 2 + (1 - c)}
+    y_id = {"dp": z * 4 + (1 - y) * 2 + c}
+    x_id = {"stream": 1 - st}
+    tiles = width // 256
+    slots = hidden // width
+
+    def z_id(d):
+        return {"dp": lax.rem(z + d, nz) * 4 + y * 2 + c}
+
+    def remote(src, dst, ss, rs, dev):
+        return pltpu.make_async_remote_copy(
+            src_ref=src, dst_ref=dst, send_sem=ss, recv_sem=rs, device_id=dev, device_id_type=MESH)
+
+    loads = [
+        pltpu.make_async_copy(src, dst, load_sem.at[i])
+        for i, (src, dst) in enumerate((
+            (x_hbm, xb), (wproj_hbm, wproj), (wo_hbm, wo), (wfirst_hbm, wfirst), (wsecond_hbm, wsecond),
+            (win_hbm, win), (wout_hbm, wout)))
+    ]
+    for cp in loads:
+        cp.start()
+    cot_load = pltpu.make_async_copy(cot_hbm, up, load_sem.at[7])
+
+    @pl.when(is_dec)
+    def _():
+        cot_load.start()
+
+    barrier = pltpu.get_barrier_semaphore()
+    peers = [core_id, y_id, x_id] + [z_id(d) for d in range(1, nz)]
+    for p in peers:
+        pl.semaphore_signal(barrier, inc=1, device_id=p, device_id_type=MESH)
+    pl.semaphore_wait(barrier, len(peers))
+
+    half = width // 2
+    quarter = y * 2 + c
+    wx_first = remote(wfirst_hbm.at[pl.ds(c * half, half)], wx.at[quarter], wx_send.at[0], wx_recv.at[0], x_id)
+    wx_second = remote(wsecond_hbm.at[pl.ds(c * half, half)], wx.at[quarter], wx_send.at[0], wx_recv.at[0], x_id)
+    wx_y = remote(wx.at[quarter], wx.at[quarter], wx_send.at[1], wx_recv.at[1], y_id)
+    wx_c0 = remote(wx.at[quarter], wx.at[quarter], wx_send.at[2], wx_recv.at[2], core_id)
+    far = (1 - y) * 2 + c
+    wx_c1 = remote(wx.at[far], wx.at[far], wx_send.at[3], wx_recv.at[3], core_id)
+
+    @pl.when(is_enc & (y == 0))
+    def _():
+        wx_first.start()
+
+    @pl.when(is_enc & (y == 1))
+    def _():
+        wx_second.start()
+
+    lt_copy = [remote(lt.at[i, :, :, 1 - c], ltp.at[i], lt_send.at[i], lt_recv.at[i], core_id) for i in range(9)]
+    gr_copy = [remote(gr.at[i], grp.at[i], gr_send.at[i], gr_recv.at[i], core_id) for i in range(11)]
+    mem_copy = remote(xb, mem, mem_send, mem_recv, x_id)
+    gm_copy = remote(gmem, up, gm_send, gm_recv, x_id)
+    gk_copy = [remote(kv.at[0], gr.at[6], gk_send.at[0], gk_recv.at[0], x_id),
+               remote(kv.at[1], gr.at[5], gk_send.at[1], gk_recv.at[1], x_id)]
+    vg[...] = jnp.zeros_like(vg)
+
+    def row_loop(block, body):
+        def step(i, carry):
+            body(pl.ds(pl.multiple_of(i * block, block), block))
+            return carry
+        lax.fori_loop(0, ROWS // block, step, 0)
+
+    def vrow(r):
+        return vec[pl.ds(r, 1), :]
+
+    def transposed(i, value):
+        lt[i] = value.T.reshape(nz, 2, 2, PIECE, ROWS)
+
+    def col_sum(slot, row):
+        def step(i, carry):
+            block = slot[pl.ds(pl.multiple_of(i * 64, 64), 64), :].astype(f32)
+            return carry + jnp.sum(block.reshape(8, 8, width), axis=0)
+        total = lax.fori_loop(0, ROWS // 64, step, jnp.zeros((8, width), f32))
+        vg[pl.ds(row, 1), :] = jnp.sum(total, axis=0, keepdims=True)
+
+    def norm_forward(sum_ref, add_bias, gain, shift, out_low, keep_wide):
+        def body(rows):
+            u = grad[rows, :] + acc[rows, :] + vrow(add_bias)
+            sum_ref[rows, :] = u
+            centre = u - jnp.mean(u, axis=-1, keepdims=True)
+            spread = jnp.mean(centre * centre, axis=-1, keepdims=True)
+            h = centre * lax.rsqrt(spread + 1e-05) * vrow(gain) + vrow(shift)
+            if keep_wide:
+                grad[rows, :] = h
+            out_low[rows, :] = h.astype(bf16)
+        row_loop(32, body)
+
+    def norm_backward(sum_ref, source, gain, shift, slot):
+        def step(i, carry):
+            rows = pl.ds(pl.multiple_of(i * 32, 32), 32)
+            r = source[rows, :].astype(f32)
+            u = sum_ref[rows, :]
+            centre = u - jnp.mean(u, axis=-1, keepdims=True)
+            spread = jnp.mean(centre * centre, axis=-1, keepdims=True)
+            inv = lax.rsqrt(spread + 1e-05)
+            uhat = centre * inv
+            t = r * vrow(gain)
+            gu = (t - jnp.mean(t, axis=-1, keepdims=True) - uhat * jnp.mean(t * uhat, axis=-1, keepdims=True)) * inv
+            grad[rows, :] = gu
+            slot[rows, :] = gu.astype(bf16)
+            return (carry[0] + jnp.sum((r * uhat).reshape(4, 8, width), axis=0),
+                    carry[1] + jnp.sum(r.reshape(4, 8, width), axis=0))
+        zero = jnp.zeros((8, width), f32)
+        total = lax.fori_loop(0, ROWS // 32, step, (zero, zero))
+        vg[pl.ds(gain, 1), :] = jnp.sum(total[0], axis=0, keepdims=True)
+        vg[pl.ds(shift, 1), :] = jnp.sum(total[1], axis=0, keepdims=True)
+
+    def masked_scores(q_half, k2, n, length, diagonal):
+        s = dot_nt(q_half, k2) * (HDIM ** -0.5)
+        column = lax.broadcasted_iota(jnp.int32, (n, n), 1)
+        row = lax.broadcasted_iota(jnp.int32, (n, n), 0)
+        return jnp.where((column < length) & (column <= row + diagonal), s, -1e30)
+
+    def softmax(s):
+        e = jnp.exp(s - jnp.max(s, axis=-1, keepdims=True))
+        return e * (1.0 / jnp.sum(e, axis=-1, keepdims=True))
+
+    buckets = ((0, SHORT), (SHORT, LONG))
+
+    def halves(n):
+        lane = lax.broadcasted_iota(jnp.int32, (n, 2 * HDIM), 1)
+        return lane < HDIM
+
+    def attend_forward(q_ref, k_ref, v_ref, len_at, diagonal, bias_row, out_ref):
+        for b, (r0, n) in enumerate(buckets):
+            rows = pl.ds(r0, n)
+            length = lens[len_at + b]
+            first = halves(n)
+
+            def step(p, carry, rows=rows, n=n, length=length, first=first):
+                at = cols(p, 2 * HDIM)
+                q2, k2, v2 = q_ref[rows, at], k_ref[rows, at], v_ref[rows, at]
+                zero = jnp.zeros_like(q2)
+                parts = []
+                for lanes in (first, ~first):
+                    prob = softmax(masked_scores(jnp.where(lanes, q2, zero), k2, n, length, diagonal))
+                    parts.append(dot_nn(prob.astype(bf16), v2))
+                att = jnp.where(first, parts[0], parts[1])
+                if bias_row is not None:
+                    att = att + vec[pl.ds(bias_row, 1), at]
+                out_ref[rows, at] = att.astype(bf16)
+                return carry
+            lax.fori_loop(0, width // (2 * HDIM), step, 0)
+
+    def attend_backward(b, q_ref, k_ref, v_ref, len_at, diagonal):
+        r0, n = buckets[b]
+        rows = pl.ds(r0, n)
+        length = lens[len_at + b]
+        first = halves(n)
+        scale = HDIM ** -0.5
+
+        def step(p, carry):
+            at = cols(p, 2 * HDIM)
+            q2, k2, v2, go2 = q_ref[rows, at], k_ref[rows, at], v_ref[rows, at], obuf[rows, at]
+            zero = jnp.zeros_like(q2)
+            got = []
+            for lanes in (first, ~first):
+                prob = softmax(masked_scores(jnp.where(lanes, q2, zero), k2, n, length, diagonal))
+                gv = dot_tn(prob.astype(bf16), go2)
+                gp = dot_nt(jnp.where(lanes, go2, zero), v2)
+                gs = (prob * (gp - jnp.sum(prob * gp, axis=-1, keepdims=True))).astype(bf16)
+                got.append((dot_nn(gs, k2), dot_tn(gs, q2), gv))
+            q_ref[rows, at] = (jnp.where(first, got[0][0], got[1][0]) * scale).astype(bf16)
+            k_ref[rows, at] = (jnp.where(first, got[0][1], got[1][1]) * scale).astype(bf16)
+            v_ref[rows, at] = jnp.where(first, got[0][2], got[1][2]).astype(bf16)
+            return carry
+        lax.fori_loop(0, width // (2 * HDIM), step, 0)
+
+    q_ref, k_ref, v_ref = gr.at[8], gr.at[9], gr.at[10]
+    diagonal = (1 - st) * 4096
+
+    loads[0].wait()
+    loads[1].wait()
+    bias_at = 5 + 10 * st
+
+    def project(i, carry):
+        which, t = i // tiles, i % tiles
+        at = cols(t, 256)
+        value = dot_nn(xb[...], wproj[which, :, at])
+        bias = vec[pl.ds(bias_at + which // 2, 1), at] * jnp.where(which == 1, 0.0, 1.0)
+        gr[8 + which, :, at] = (value + bias).astype(bf16)
+        return carry
+    lax.fori_loop(0, 3 * tiles, project, 0)
+    transposed(4, xb[...])
+    lt_copy[4].start()
+
+    def load_residual(rows):
+        grad[rows, :] = xb[rows, :].astype(f32)
+    row_loop(64, load_residual)
+
+    attend_forward(q_ref, k_ref, v_ref, 2 * st, diagonal, None, obuf)
+    loads[2].wait()
+
+    def by_tiles(fn):
+        def step(t, carry):
+            fn(t)
+            return carry
+        lax.fori_loop(0, tiles, step, 0)
+
+    def self_out(t):
+        acc[:, cols(t, 256)] = dot_nn(obuf[...], wo[:, cols(t, 256)])
+    by_tiles(self_out)
+    norm_forward(u_self, bias_at + 2, 2 * st, bias_at + 3, hlow, True)
+    transposed(5, obuf[...])
+    lt_copy[5].start()
+
+    loads[3].wait()
+    loads[4].wait()
+
+    @pl.when(is_dec)
+    def _():
+        wx_first.wait_recv()
+        wx_y.start()
+        wx_c0.start()
+
+        def cross_query(t):
+            at = cols(t, 256)
+            gr[6, :, at] = (dot_nn(hlow[...], wfirst[:, at]) + vec[pl.ds(19, 1), at]).astype(bf16)
+        by_tiles(cross_query)
+        transposed(8, hlow[...])
+        lt_copy[8].start()
+        wx_y.wait()
+        wx_c1.start()
+        wx_c0.wait()
+        wx_c1.wait()
+        mem_copy.wait_recv()
+
+        def memory_kv(i, carry):
+            which, t = i // tiles, i % tiles
+            at = cols(t, 256)
+            value = dot_nn(mem[:, pl.ds(0, half)], wx[2 * which, :, at]) + dot_nn(mem[:, pl.ds(half, half)], wx[2 * which + 1, :, at])
+            kv[which, :, at] = value.astype(bf16)
+            return carry
+        lax.fori_loop(0, 2 * tiles, memory_kv, 0)
+        attend_forward(gr.at[6], kv.at[0], kv.at[1], 0, 4096, 20, obuf)
+
+        def cross_out(t):
+            acc[:, cols(t, 256)] = dot_nn(obuf[...], wsecond[:, cols(t, 256)])
+        by_tiles(cross_out)
+        norm_forward(u_cross, 21, 3, 22, hlow, True)
+        transposed(7, obuf[...])
+        lt_copy[7].start()
+
+    loads[5].wait()
+    loads[6].wait()
+
+    def ffn_slot(j, carry):
+        def tile(t, carry2):
+            at = cols(t, 256)
+            wide = pl.ds(pl.multiple_of(j * width + t * 256, 256), 256)
+            acc[:, at] = dot_nn(hlow[...], win[:, wide])
+
+            def activate(rows):
+                zv = acc[rows, at] + bias_in[pl.ds(st, 1), wide]
+                cdf = 0.5 * (1.0 + lax.erf(zv * (0.5 ** 0.5)))
+                pdf = jnp.exp(-0.5 * zv * zv) * 0.3989422804014327
+                gr[1 + j, rows, at] = (zv * cdf).astype(bf16)
+                dg[j, rows, at] = (cdf + zv * pdf).astype(bf16)
+            row_loop(64, activate)
+            return carry2
+        lax.fori_loop(0, tiles, tile, 0)
+        turned = gr[1 + j].T.reshape(2, 2, 4, PIECE, ROWS)
+        for k in range(4):
+            lt[k, j] = turned[:, :, k]
+        return carry
+    lax.fori_loop(0, slots, ffn_slot, 0)
+    for k in range(4):
+        lt_copy[k].start()
+
+    def ffn_out(t):
+        at = cols(t, 256)
+        total = dot_nn(gr[1], wout[pl.ds(0, width), at])
+        for j in range(1, slots):
+            total = total + dot_nn(gr[1 + j], wout[pl.ds(j * width, width), at])
+        acc[:, at] = total
+    by_tiles(ffn_out)
+    ffn_at = 5 + 8 + 14 * st
+    norm_forward(u_ffn, ffn_at, 1 + 3 * st, ffn_at + 1, xb, False)
+
+    @pl.when(is_enc)
+    def _():
+        mem_copy.start()
+    rows_copy = pltpu.make_async_copy(xb, out_rows, io_sem.at[0])
+    rows_copy.start()
+    transposed(6, hlow[...])
+    lt_copy[6].start()
+
+    @pl.when(is_enc)
+    def _():
+        transposed(7, xb[...])
+        lt_copy[7].start()
+        gm_copy.wait_recv()
+
+    @pl.when(is_dec)
+    def _():
+        cot_load.wait()
+
+    norm_backward(u_ffn, up, 1 + 3 * st, ffn_at + 1, gr.at[0])
+    gr_copy[0].start()
+
+    def ffn_inner(j, carry):
+        def tile(t, carry2):
+            at = cols(t, 256)
+            wide = pl.ds(pl.multiple_of(j * width + t * 256, 256), 256)
+            acc[:, at] = dot_nt(gr[0], wout[wide, :])
+
+            def scale(rows):
+                gr[1 + j, rows, at] = (acc[rows, at] * dg[j, rows, at].astype(f32)).astype(bf16)
+            row_loop(64, scale)
+            return carry2
+        lax.fori_loop(0, tiles, tile, 0)
+        remote(gr.at[1 + j], grp.at[1 + j], gr_send.at[1 + j], gr_recv.at[1 + j], core_id).start()
+        return carry
+    lax.fori_loop(0, slots, ffn_inner, 0)
+
+    def ffn_input(t):
+        at = cols(t, 256)
+        total = grad[:, at]
+        for j in range(slots):
+            total = total + dot_nt(gr[1 + j], win[at, pl.ds(j * width, width)])
+        grad[:, at] = total
+    by_tiles(ffn_input)
+
+    @pl.when(is_dec)
+    def _():
+        norm_backward(u_cross, grad, 3, 22, gr.at[5])
+        gr_copy[5].start()
+
+        def cross_up(t):
+            at = cols(t, 256)
+            obuf[:, at] = dot_nt(gr[5], wsecond[at, :]).astype(bf16)
+        by_tiles(cross_up)
+        col_sum(obuf, 20)
+        for b in range(2):
+            attend_backward(b, gr.at[6], kv.at[0], kv.at[1], 0, 4096)
+
+        def memory_half(h, carry):
+            at = cols(h, half)
+            gmem[:, at] = (dot_nt(kv[0], wx[h]) + dot_nt(kv[1], wx[2 + h])).astype(bf16)
+            return carry
+        lax.fori_loop(0, 2, memory_half, 0)
+        gm_copy.start()
+        gk_copy[0].start()
+        gk_copy[1].start()
+        gr_copy[6].start()
+        col_sum(gr.at[6], 19)
+        col_sum(gr.at[5], 21)
+
+        def cross_input(t):
+            at = cols(t, 256)
+            grad[:, at] = grad[:, at] + dot_nt(gr[6], wfirst[at, :])
+        by_tiles(cross_input)
+
+
+    def y_copy(i):
+        return remote(ysend.at[i], yrecv.at[i], y_send.at[i], y_recv.at[i], y_id)
+
+    def z_copy(i, d):
+        return remote(yrecv.at[i, lax.rem(z + d, nz)], out_z.at[d - 1, i], z_send.at[i, d - 1], z_recv.at[i, d - 1], z_id(d))
+
+    def product(left, slot, yy, at):
+        mine = lt[left, :, yy, c].reshape(nz * PIECE, ROWS)
+        theirs = ltp[left, :, yy].reshape(nz * PIECE, ROWS)
+        return dot_nn(mine, gr[slot, :, at]) + dot_nn(theirs, grp[slot, :, at])
+
+    def send_piece(i, left, slot):
+        def tile(t):
+            at = cols(t, 256)
+            ysend[i, :, :, at] = product(left, slot, 1 - y, at).astype(bf16).reshape(nz, PIECE, 256)
+        by_tiles(tile)
+        y_copy(i).start()
+
+    def keep_piece(i, left, slot):
+        y_copy(i).wait()
+
+        def tile(t):
+            at = cols(t, 256)
+            total = yrecv[i, :, :, at].reshape(nz * PIECE, 256).astype(f32) + product(left, slot, y, at)
+            yrecv[i, :, :, at] = total.astype(bf16).reshape(nz, PIECE, 256)
+        by_tiles(tile)
+        for d in range(1, nz):
+            z_copy(i, d).start()
+        pltpu.make_async_copy(yrecv.at[i, z], out_own.at[i], own_sem.at[i]).start()
+
+    def loop(lo, hi, fn):
+        def step(i, carry):
+            fn(i)
+            return carry
+        lax.fori_loop(lo, hi, step, 0)
+
+    for i in (0, 1, 2, 3, 6):
+        lt_copy[i].wait()
+    gr_copy[0].wait()
+    loop(0, 4, lambda i: send_piece(i, i, 0))
+    for j in range(slots):
+        gr_copy[1 + j].wait()
+    loop(4, 8, lambda i: send_piece(i, 6, i - 3))
+
+    norm_backward(u_self, grad, 2 * st, bias_at + 3, gr.at[7])
+    gr_copy[7].start()
+
+    def self_up(t):
+        at = cols(t, 256)
+        obuf[:, at] = dot_nt(gr[7], wo[at, :]).astype(bf16)
+    by_tiles(self_up)
+    loop(0, 1, lambda i: keep_piece(i, i, 0))
+    attend_backward(0, q_ref, k_ref, v_ref, 2 * st, diagonal)
+    loop(1, 2, lambda i: keep_piece(i, i, 0))
+    attend_backward(1, q_ref, k_ref, v_ref, 2 * st, diagonal)
+    for j in range(3):
+        gr_copy[8 + j].start()
+
+    @pl.when(is_enc)
+    def _():
+        gk_copy[0].wait_recv()
+        gk_copy[1].wait_recv()
+        gr_copy[5].start()
+        gr_copy[6].start()
+
+    def self_input(t):
+        at = cols(t, 256)
+        total = grad[:, at]
+        for j in range(3):
+            total = total + dot_nt(gr[8 + j], wproj[j, at, :])
+        grad[:, at] = total
+    by_tiles(self_input)
+    grad_copy = pltpu.make_async_copy(grad, out_grad, io_sem.at[1])
+    grad_copy.start()
+    loop(2, 4, lambda i: keep_piece(i, i, 0))
+    for i in (4, 5, 7):
+        lt_copy[i].wait()
+
+    @pl.when(is_dec)
+    def _():
+        lt_copy[8].wait()
+    for i in range(5, 11):
+        gr_copy[i].wait()
+    first_left = 7 + st
+    rest = ((8, 7, 5), (9, first_left, 6), (10, 5, 7), (11, 4, 8), (12, 4, 9), (13, 4, 10))
+    for i, left, slot in rest:
+        send_piece(i, left, slot)
+
+    col_sum(gr.at[0], ffn_at)
+    loop(0, slots, lambda j: col_sum(gr.at[1 + j], ffn_at - 4 + j))
+    col_sum(gr.at[7], bias_at + 2)
+    col_sum(gr.at[8], bias_at)
+    col_sum(gr.at[10], bias_at + 1)
+    v_copy = [remote(vbuf.at[0], vbuf.at[1], v_send.at[0], v_recv.at[0], core_id),
+              remote(vbuf.at[2], vbuf.at[3], v_send.at[1], v_recv.at[1], y_id),
+              remote(vbuf.at[5], vbuf.at[6], v_send.at[2], v_recv.at[2], x_id)]
+    vz_copy = [remote(vbuf.at[4], vzbuf.at[d - 1], vz_send.at[d - 1], vz_recv.at[d - 1], z_id(d)) for d in range(1, nz)]
+    vbuf[0] = vg[...]
+    v_copy[0].start()
+    loop(4, 5, lambda i: keep_piece(i, 6, i - 3))
+    v_copy[0].wait()
+    vbuf[2] = vbuf[0] + vbuf[1]
+    v_copy[1].start()
+    loop(5, 6, lambda i: keep_piece(i, 6, i - 3))
+    v_copy[1].wait()
+    vbuf[4] = vbuf[2] + vbuf[3]
+    for cp in vz_copy:
+        cp.start()
+    loop(6, 8, lambda i: keep_piece(i, 6, i - 3))
+    for cp in vz_copy:
+        cp.wait()
+    total = vbuf[4]
+    for d in range(1, nz):
+        total = total + vzbuf[d - 1]
+    vbuf[5] = total
+    v_copy[2].start()
+    for i, left, slot in rest:
+        keep_piece(i, left, slot)
+    v_copy[2].wait()
+    out_vec[...] = vbuf[5] + vbuf[6]
+
+    def finish(i):
+        for d in range(1, nz):
+            z_copy(i, d).wait()
+        pltpu.make_async_copy(yrecv.at[i, z], out_own.at[i], own_sem.at[i]).wait()
+    loop(0, PIECES, finish)
+    rows_copy.wait()
+    grad_copy.wait()
+
+    @pl.when(is_enc)
+    def _():
+        wx_first.wait_send()
+        mem_copy.wait_send()
+
+    @pl.when(is_dec)
+    def _():
+        gm_copy.wait_send()
+        gk_copy[0].wait_send()
+        gk_copy[1].wait_send()
+
+
+def last_kernel(nz, width, rows_in, grad_in, own, parts, rows_out, grad_out, *outs):
+    rows_out[...] = rows_in[...]
+    grad_out[...] = grad_in[...]
+    for i in range(PIECES):
+        total = own[i].astype(f32)
+        for d in range(nz - 1):
+            total = total + parts[d, i].astype(f32)
+        if i < 4:
+            outs[0][pl.ds(i * PIECE, PIECE), :] = total
+        elif i < 8:
+            outs[1][:, pl.ds((i - 4) * width, width)] = total
+        elif i < 11:
+            outs[i - 6][...] = total
+        else:
+            outs[5][i - 11] = total
+
+
+def whole_step(nz, lens, vec, bias_in, x, cot, wproj, wo, wfirst, wsecond, win, wout):
+    width = x.shape[1]
+    hidden = win.shape[1]
+    half = width // 2
+    any_space = pl.BlockSpec(memory_space=pl.ANY)
+    vmem = pl.BlockSpec(memory_space=pltpu.VMEM)
+    dma = pltpu.SemaphoreType.DMA
+    slots = hidden // width
+    results = pl.pallas_call(
+        functools.partial(step_kernel, nz, width, hidden),
+        out_shape=[
+            jax.ShapeDtypeStruct((ROWS, width), bf16),
+            jax.ShapeDtypeStruct((ROWS, width), f32),
+            jax.ShapeDtypeStruct((PIECES, PIECE, width), bf16),
+            jax.ShapeDtypeStruct((nz - 1, PIECES, PIECE, width), bf16),
+            jax.ShapeDtypeStruct(vec.shape, f32),
+        ],
+        in_specs=[pl.BlockSpec(memory_space=pltpu.SMEM), vmem, vmem] + [any_space] * 8,
+        out_specs=[any_space] * 4 + [vmem],
+        scratch_shapes=[
+            pltpu.VMEM(wproj.shape, bf16), pltpu.VMEM(wo.shape, bf16), pltpu.VMEM(wfirst.shape, bf16),
+            pltpu.VMEM(wsecond.shape, bf16), pltpu.VMEM(win.shape, bf16), pltpu.VMEM(wout.shape, bf16),
+            pltpu.VMEM((4, half, width), bf16),
+            pltpu.VMEM((ROWS, width), bf16),
+            pltpu.VMEM((ROWS, width), bf16),
+            pltpu.VMEM((ROWS, width), bf16),
+            pltpu.VMEM((ROWS, width), bf16),
+            pltpu.VMEM((ROWS, width), bf16),
+            pltpu.VMEM((slots, ROWS, width), bf16),
+            pltpu.VMEM((2, ROWS, width), bf16),
+            pltpu.VMEM((ROWS, width), f32),
+            pltpu.VMEM((ROWS, width), f32),
+            pltpu.VMEM((ROWS, width), f32),
+            pltpu.VMEM((ROWS, width), f32),
+            pltpu.VMEM((ROWS, width), f32),
+            pltpu.VMEM((11, ROWS, width), bf16),
+            pltpu.VMEM((11, ROWS, width), bf16),
+            pltpu.VMEM((9, nz, 2, 2, PIECE, ROWS), bf16),
+            pltpu.VMEM((9, nz, 2, PIECE, ROWS), bf16),
+            pltpu.VMEM((PIECES, nz, PIECE, width), bf16),
+            pltpu.VMEM((PIECES, nz, PIECE, width), bf16),
+            pltpu.VMEM((ROWS, width), bf16),
+            pltpu.VMEM(vec.shape, f32),
+            pltpu.VMEM((7,) + vec.shape, f32),
+            pltpu.VMEM((nz - 1,) + vec.shape, f32),
+            dma((8,)), dma((4,)), dma((4,)), dma, dma, dma, dma, dma((2,)), dma((2,)),
+            dma((9,)), dma((9,)), dma((11,)), dma((11,)),
+            dma((PIECES,)), dma((PIECES,)), dma((PIECES, nz - 1)), dma((PIECES, nz - 1)), dma((PIECES,)), dma((2,)),
+            dma((3,)), dma((3,)), dma((nz - 1,)), dma((nz - 1,)),
+        ],
+        compiler_params=pltpu.CompilerParams(collective_id=0, has_side_effects=True, vmem_limit_bytes=VMEM_LIMIT),
+        name="step",
+    )(lens, vec, bias_in, x, cot, wproj, wo, wfirst, wsecond, win, wout)
+    rows, grad, own, parts, vec_sum = results
+    shapes = [(4 * PIECE, width), (PIECE, hidden), (PIECE, width), (PIECE, width), (PIECE, width), (3, PIECE, width)]
+    outs = pl.pallas_call(
+        functools.partial(last_kernel, nz, width),
+        out_shape=[jax.ShapeDtypeStruct(rows.shape, bf16), jax.ShapeDtypeStruct(grad.shape, f32)]
+        + [jax.ShapeDtypeStruct(s, f32) for s in shapes],
+        in_specs=[vmem] * 4,
+        out_specs=[vmem] * 8,
+        compiler_params=pltpu.CompilerParams(vmem_limit_bytes=32 << 20),
+        name="last",
+    )(rows, grad, own, parts)
+    return list(outs) + [vec_sum]
 
 
 eps_norm = 1e-05
@@ -326,7 +947,7 @@
     return progress
 
 
-def body(
+def plain_body(
     inputs,
     lengths,
     cotangent,
@@ -594,7 +1215,23 @@
     )
 
 
+def fused_body(inputs, lengths, cotangent, attn_in, attn_out, cross_first, cross_second, ffn_in, ffn_out, gains, biases):
+    nz = lax.axis_size("dp") // 4
+    vec = jnp.concatenate([gains, biases, jnp.zeros((3, gains.shape[1]), gains.dtype)]).astype(f32)
+    bias_in = jnp.stack([biases[4:8].reshape(-1), biases[18:22].reshape(-1)]).astype(f32)
+    rows, grad, s_out, s_in, s_second, s_first, s_attn, s_proj, vec_sum = whole_step(
+        nz, lengths.reshape(-1), vec, bias_in, inputs[0], cotangent, attn_in[0], attn_out[0],
+        cross_first[0], cross_second[0], ffn_in[0], ffn_out[0])
+    own_cols = lax.dynamic_slice_in_dim(vec_sum, lax.axis_index("dp") * PIECE, PIECE, 1)
+    return (rows[None], grad[None], s_proj[None], s_attn[None], s_first[None], s_second[None],
+            s_in[None], s_out[None], own_cols[:5], own_cols[5:29])
+
+
 def solution(mesh):
+    def body(*args):
+        width = args[0].shape[2]
+        fits = mesh.shape["dp"] * PIECE == width and args[0].shape[1] == ROWS and args[7].shape[2] == 4 * width
+        return (fused_body if fits else plain_body)(*args)
     return jax.shard_map(
         body,
         mesh=mesh,

time: 1260 us -> 306 us (0.24); the launches traced: 1240 us -> 305 us
  waiting for transfers between devices: 793 us -> 0 us
  Pallas kernels: 0 us -> 291 us
  matrix products: 172 us -> 0 us
  local copies, waits for them, and re-layouts: 154 us -> 10.2 us
  other arithmetic: 55.8 us -> 3.47 us
  loops' own time: 24.7 us -> 0 us
  starting transfers between devices: 22.2 us -> 0 us
  between operations: 14.4 us -> 0.69 us
    reduce_scatter x6 -> x0, waiting for transfers between devices: 516 us -> none  [the longest x1 116 us: body(): lax.psum_scatter(totals['ffn_out'], 'dp', scatter_dimension=0, tiled=True)]
    pallas_call x0 -> x2, Pallas kernels: none -> 291 us  [the longest x1 289 us: whole_step(): pl.pallas_call(functools.partial(step_kernel, nz, width, hidden), out_sha...]
    ppermute x4 -> x0, waiting for transfers between devices: 201 us -> none  [shifted(): return lax.ppermute(shard, axis, pairs)]
    dot_general x50 -> x0, matrix products: 172 us -> none  [the longest x10 54 us: matmul_tn(): lax.dot_general(left_mat, right_mat, (((0,), (0,)), ((), ())), preferred_...]
    unnamed x10 -> x0, waiting for transfers between devices: 76.3 us -> none
    another operation x56 -> x0, local copies, waits for them, and re-layouts: 50.7 us -> none
    cond x100 -> x0, local copies, waits for them, and re-layouts: 41.3 us -> none  [the longest x2 19.4 us: body(): progress = lax.cond(is_decoder, keep_same, enc_four, progress)]
    another operation x4 -> x0, loops' own time: 23.9 us -> none  [the longest x1 14.6 us: body(): progress = lax.cond(is_decoder, dec_three, enc_three, progress)]
  transfers between devices with their start and end apart: 12 -> 0, of which waited for: 11 -> 0; matrix products, arithmetic and copies ran while one was open for 4% -> 0% of each run, Pallas kernels for 0% -> 0%
where the time goes in v2:
time: 306 us; the launch traced here: 305 us
  Pallas kernels  291 us (95%)
  local copies, waits for them, and re-layouts  10.2 us (3%)
  other arithmetic  3.47 us (1%)
    pallas_call x1, Pallas kernels, whole_step(): pl.pallas_call(functools.partial(step_kernel, nz, width, hidden), out_sha...  289 us
    unnamed x12, local copies, waits for them, and re-layouts  6.69 us

profile of v2, /device:TPU:0, one launch (start us, length us, event | category | flops | bytes accessed | tf_op | source)
XLA Modules:
  0.0 305.2 jit_solution(9619372111991076930)
XLA Ops:
  0.6 0.7 slice_bitcast_fusion.1
  1.4 0.6 maximum_convert_fusion.1.bias_in
  2.1 0.1 pad.4.clone
  2.1 1.5 maximum_convert_fusion.vec
  3.6 0.5 broadcast.5
  4.1 1.3 reduce.3
  5.5 0.6 reshape.23.lens
  6.1 288.5 %step.1 = (bf16[384,768]{1,0:T(8,128)(2,1)}, f32[384,768]{1,0:T(8,128)}, bf16[14,48,768]{2,1,0:T(8,128)(2,1)}, bf16[3,14,48,768]{3,2,1,0:T(8,128)(2,1)}, f32[32,768]{1,0:T(8,128)}) custom-call(s32[4]{0:T(128)} %reshape.23.lens, f32[32,768]{1,0:T(8,128)} %maximum_convert_fusion.vec, f32[2,3072]{1,0:T(2,128)} %maximum_convert_fusion.1.bias_in, ...), custom_call_target="tpu_custom_call" | custom-call | tf_op jit(solution)/shard_map/step/pallas_call | solution.py:573
  294.6 0.0 copy-start
  294.6 1.9 copy-done
  296.5 0.0 copy-start.1
  296.5 1.3 copy-done.1
  297.8 0.0 copy-start.2
  297.8 1.2 copy-done.2
  299.0 0.0 copy-start.3
  299.0 1.1 copy-done.3
  300.1 2.4 last.1
  302.4 1.4 dynamic-slice.1
  303.9 1.4 constant_dynamic-slice_fusion
  (3 shorter events, 0.0 us)
Async XLA Ops:
  294.6 1.9 copy-start
  296.5 1.3 copy-start.1
  297.8 1.2 copy-start.2
  299.0 1.1 copy-start.3

commit v3 on v0

--- a/solution.py
+++ b/solution.py
@@ -1,11 +1,801 @@
+import functools
+
 import jax
 import jax.numpy as jnp
 from jax import lax
+from jax.experimental import pallas as pl
+from jax.experimental.pallas import tpu as pltpu
 from jax.sharding import PartitionSpec as P
 
 HDIM = 64
 SHORT = 128
 LONG = 256
+ROWS = SHORT + LONG
+PIECE = 48
+PIECES = 14
+SEND_SLOTS = 8
+WX_CHUNKS = 4
+MESH = pl.DeviceIdType.MESH
+bf16, f32 = jnp.bfloat16, jnp.float32
+VMEM_LIMIT = 64 << 20
+
+
+def dot_nn(a, b):
+    return jnp.dot(a, b, preferred_element_type=f32)
+
+
+def dot_nt(a, b):
+    return lax.dot_general(a, b, (((1,), (1,)), ((), ())), preferred_element_type=f32)
+
+
+def dot_tn(a, b):
+    return lax.dot_general(a, b, (((0,), (0,)), ((), ())), preferred_element_type=f32)
+
+
+def cols(j, width):
+    return pl.ds(pl.multiple_of(j * width, width), width)
+
+
+def step_kernel(
+    width, hidden,
+    lengths, gains, biases, x_hbm, cot_hbm, wproj_hbm, wo_hbm, wfirst_hbm, wsecond_hbm, win_hbm, wout_hbm,
+    out_rows, out_grad, out_own, out_part, out_vec,
+    vec, bias_in, wproj, wo, wfirst, wsecond, win, wout, wx,
+    xb, up, mem, obuf, hlow, dg, kv, acc, grad, hw, u_self, u_cross, u_ffn, gr, grp, lt, ltp, one_send, one_recv, two_recv, gmem, vg, vbuf,
+    load_sem, wx_send, wx_recv, mem_send, mem_recv, gm_send, gm_recv, gk_send, gk_recv, lt_send, lt_recv, gr_send, gr_recv,
+    sem_send, sem_recv, own_sem, io_sem, v_send, v_recv,
+):
+    st = lax.axis_index("stream")
+    me = lax.axis_index("dp")
+    z, y, c = me // 4, (me // 2) % 2, me % 2
+    is_dec = st == 1
+    is_enc = st == 0
+    core_id = {"dp": z * 4 + y * 2 + (1 - c)}
+    y_id = {"dp": z * 4 + (1 - y) * 2 + c}
+    x_id = {"stream": 1 - st}
+    tiles = width // 256
+    slots = hidden // width
+
+    zh, zl = z // 2, z % 2
+
+    def z_id(other):
+        return {"dp": other * 4 + y * 2 + c}
+    near_id = z_id(zh * 2 + 1 - zl)
+    far_id = z_id((1 - zh) * 2 + zl)
+
+    def remote(src, dst, ss, rs, dev):
+        return pltpu.make_async_remote_copy(
+            src_ref=src, dst_ref=dst, send_sem=ss, recv_sem=rs, device_id=dev, device_id_type=MESH)
+
+    loads = [
+        pltpu.make_async_copy(src, dst, load_sem.at[i])
+        for i, (src, dst) in enumerate((
+            (x_hbm, xb), (wproj_hbm, wproj), (wo_hbm, wo), (win_hbm, win), (wout_hbm, wout),
+            (wfirst_hbm, wfirst), (wsecond_hbm, wsecond)))
+    ]
+    cot_load = pltpu.make_async_copy(cot_hbm, up, load_sem.at[7])
+    loads[0].start()
+    loads[1].start()
+
+    barrier = pltpu.get_barrier_semaphore()
+    peers = [core_id, y_id, x_id, near_id, far_id]
+    for p in peers:
+        pl.semaphore_signal(barrier, inc=1, device_id=p, device_id_type=MESH)
+
+    lens = [lengths[i // 2, 0, i % 2] for i in range(4)]
+    own_lens = [jnp.where(is_dec, lens[2 + i], lens[i]) for i in range(2)]
+    vec[pl.ds(0, 5), :] = gains[...].astype(f32)
+    vec[pl.ds(5, 24), :] = biases[...].astype(f32)
+    for i in range(slots):
+        for s in range(2):
+            bias_in[pl.ds(s, 1), pl.ds(i * width, width)] = vec[pl.ds(9 + 14 * s + i, 1), :]
+    vg[...] = jnp.zeros_like(vg)
+    pl.semaphore_wait(barrier, len(peers))
+
+    half = width // 2
+    chunk = half // WX_CHUNKS
+    quarter = y * 2 + c
+    far = (1 - y) * 2 + c
+
+    def wx_from(source, h):
+        return remote(source.at[pl.ds(c * half + h * chunk, chunk)], wx.at[quarter, pl.ds(h * chunk, chunk)],
+                      wx_send.at[h], wx_recv.at[h], x_id)
+
+    def wx_pass(at, h, sem, dev):
+        ref = wx.at[at, pl.ds(h * chunk, chunk)]
+        return remote(ref, ref, wx_send.at[sem * WX_CHUNKS + h], wx_recv.at[sem * WX_CHUNKS + h], dev)
+    wx_first = [wx_from(wfirst_hbm, h) for h in range(WX_CHUNKS)]
+    wx_y = [wx_pass(quarter, h, 1, y_id) for h in range(WX_CHUNKS)]
+    wx_near = [wx_pass(quarter, h, 2, core_id) for h in range(WX_CHUNKS)]
+    wx_far = [wx_pass(far, h, 3, core_id) for h in range(WX_CHUNKS)]
+
+    @pl.when(is_enc & (y == 0))
+    def _():
+        for h in range(WX_CHUNKS):
+            wx_first[h].start()
+
+    @pl.when(is_enc & (y == 1))
+    def _():
+        for h in range(WX_CHUNKS):
+            wx_from(wsecond_hbm, h).start()
+    loads[0].wait()
+    loads[1].wait()
+    for cp in loads[2:]:
+        cp.start()
+
+    @pl.when(is_dec)
+    def _():
+        cot_load.start()
+
+    lt_copy = [remote(lt.at[i, :, :, :, 1 - c], ltp.at[i], lt_send.at[i], lt_recv.at[i], core_id) for i in range(9)]
+    gr_copy = [remote(gr.at[i], grp.at[i], gr_send.at[i], gr_recv.at[i], core_id) for i in range(11)]
+    buckets = ((0, SHORT), (SHORT, LONG))
+    short, long, both = (0,), (1,), (0, 1)
+
+    def span(bs):
+        return buckets[bs[0]][0], sum(buckets[b][1] for b in bs)
+
+    def at_rows(bs):
+        return pl.ds(*span(bs))
+    mem_copy = [remote(xb.at[at_rows((b,))], mem.at[at_rows((b,))], mem_send.at[b], mem_recv.at[b], x_id) for b in range(2)]
+    gm_copy = [remote(gmem.at[at_rows((b,))], up.at[at_rows((b,))], gm_send.at[b], gm_recv.at[b], x_id) for b in range(2)]
+    gk_copy = [remote(kv.at[0], gr.at[6], gk_send.at[0], gk_recv.at[0], x_id),
+               remote(kv.at[1], gr.at[5], gk_send.at[1], gk_recv.at[1], x_id)]
+
+    def row_loop(bs, block, body, unroll=1):
+        r0, n = span(bs)
+
+        def step(i, carry):
+            body(pl.ds(pl.multiple_of(r0 + i * block, block), block))
+            return carry
+        lax.fori_loop(0, n // block, step, 0, unroll=unroll)
+
+    def vrow(r):
+        return vec[pl.ds(r, 1), :]
+
+    def transposed(i, bs, ref):
+        r0, n = span(bs)
+        lt[i, :, :, :, :, :, pl.ds(r0, n)] = ref[pl.ds(r0, n), :].T.reshape(2, 2, 2, 2, PIECE, n)
+
+    def transposed_active(bs):
+        r0, n = span(bs)
+
+        def step(j, carry):
+            turned = gr[1 + j, pl.ds(r0, n), :].T.reshape(2, 2, 4, PIECE, n)
+            for k in range(4):
+                lt[k, j // 2, j % 2, :, :, :, pl.ds(r0, n)] = turned[:, :, k]
+            return carry
+        lax.fori_loop(0, slots, step, 0)
+
+    def col_sum(slot, row):
+        def step(i, carry):
+            block = slot[pl.ds(pl.multiple_of(i * 64, 64), 64), :].astype(f32)
+            return carry + jnp.sum(block.reshape(8, 8, width), axis=0)
+        total = lax.fori_loop(0, ROWS // 64, step, jnp.zeros((8, width), f32))
+        vg[pl.ds(row, 1), :] = jnp.sum(total, axis=0, keepdims=True)
+
+    def norm_forward(bs, residual, sum_ref, add_bias, gain, shift, out_low, out_wide):
+        def body(rows):
+            u = residual[rows, :].astype(f32) + acc[rows, :] + vrow(add_bias)
+            sum_ref[rows, :] = u
+            centre = u - jnp.mean(u, axis=-1, keepdims=True)
+            spread = jnp.mean(centre * centre, axis=-1, keepdims=True)
+            h = centre * lax.rsqrt(spread + 1e-05) * vrow(gain) + vrow(shift)
+            if out_wide is not None:
+                out_wide[rows, :] = h
+            out_low[rows, :] = h.astype(bf16)
+        row_loop(bs, 32, body, 4)
+
+    def norm_backward(bs, sum_ref, source, gain, shift, out_wide, slot):
+        r0, n = span(bs)
+
+        def step(i, carry):
+            rows = pl.ds(pl.multiple_of(r0 + i * 32, 32), 32)
+            r = source[rows, :].astype(f32)
+            u = sum_ref[rows, :]
+            centre = u - jnp.mean(u, axis=-1, keepdims=True)
+            spread = jnp.mean(centre * centre, axis=-1, keepdims=True)
+            inv = lax.rsqrt(spread + 1e-05)
+            uhat = centre * inv
+            t = r * vrow(gain)
+            gu = (t - jnp.mean(t, axis=-1, keepdims=True) - uhat * jnp.mean(t * uhat, axis=-1, keepdims=True)) * inv
+            out_wide[rows, :] = gu
+            slot[rows, :] = gu.astype(bf16)
+            return (carry[0] + jnp.sum((r * uhat).reshape(4, 8, width), axis=0),
+                    carry[1] + jnp.sum(r.reshape(4, 8, width), axis=0))
+        zero = jnp.zeros((8, width), f32)
+        total = lax.fori_loop(0, n // 32, step, (zero, zero), unroll=4)
+        for row, part in ((gain, total[0]), (shift, total[1])):
+            vg[pl.ds(row, 1), :] = vg[pl.ds(row, 1), :] + jnp.sum(part, axis=0, keepdims=True)
+
+    def masked_scores(q_half, k2, n, length, diagonal):
+        s = dot_nt(q_half, k2) * (HDIM ** -0.5)
+        column = lax.broadcasted_iota(jnp.int32, (n, n), 1)
+        row = lax.broadcasted_iota(jnp.int32, (n, n), 0)
+        return jnp.where((column < length) & (column <= row + diagonal), s, -1e30)
+
+    def softmax(s):
+        e = jnp.exp(s - jnp.max(s, axis=-1, keepdims=True))
+        return e * (1.0 / jnp.sum(e, axis=-1, keepdims=True))
+
+    def halves(n):
+        lane = lax.broadcasted_iota(jnp.int32, (n, 2 * HDIM), 1)
+        return lane < HDIM
+
+    def head_loop(bs, body):
+        pairs = {short: 3, long: 2, both: 1}[bs]
+
+        def step(p, carry):
+            body([(b, pl.ds(pl.multiple_of((p * pairs + i) * 2 * HDIM, 2 * HDIM), 2 * HDIM)) for b in bs for i in range(pairs)])
+            return carry
+        lax.fori_loop(0, width // (2 * HDIM * pairs), step, 0)
+
+    def attend_forward(bs, q_ref, k_ref, v_ref, lengths_at, diagonal, bias_row, out_ref):
+        def body(units):
+            work = []
+            for b, at in units:
+                r0, n = buckets[b]
+                rows = pl.ds(r0, n)
+                q2, k2 = q_ref[rows, at], k_ref[rows, at]
+                first = halves(n)
+                for lanes in (first, ~first):
+                    work.append(masked_scores(jnp.where(lanes, q2, jnp.zeros_like(q2)), k2, n, lengths_at[b], diagonal))
+            work = [softmax(s).astype(bf16) for s in work]
+            work = [dot_nn(prob, v_ref[pl.ds(*buckets[units[i // 2][0]]), units[i // 2][1]]) for i, prob in enumerate(work)]
+            for i, (b, at) in enumerate(units):
+                r0, n = buckets[b]
+                att = jnp.where(halves(n), work[2 * i], work[2 * i + 1])
+                if bias_row is not None:
+                    att = att + vec[pl.ds(bias_row, 1), at]
+                out_ref[pl.ds(r0, n), at] = att.astype(bf16)
+        head_loop(bs, body)
+
+    def attend_backward(bs, q_ref, k_ref, v_ref, lengths_at, diagonal):
+        scale = HDIM ** -0.5
+
+        def body(units):
+            scores, ups = [], []
+            for b, at in units:
+                r0, n = buckets[b]
+                rows = pl.ds(r0, n)
+                q2, k2, v2, go2 = q_ref[rows, at], k_ref[rows, at], v_ref[rows, at], obuf[rows, at]
+                first = halves(n)
+                zero = jnp.zeros_like(q2)
+                for lanes in (first, ~first):
+                    scores.append(masked_scores(jnp.where(lanes, q2, zero), k2, n, lengths_at[b], diagonal))
+                    ups.append(dot_nt(jnp.where(lanes, go2, zero), v2))
+            probs = [softmax(s) for s in scores]
+            gs = [(p * (gp - jnp.sum(p * gp, axis=-1, keepdims=True))).astype(bf16) for p, gp in zip(probs, ups)]
+            for i, (b, at) in enumerate(units):
+                r0, n = buckets[b]
+                rows = pl.ds(r0, n)
+                q2, k2, go2 = q_ref[rows, at], k_ref[rows, at], obuf[rows, at]
+                first = halves(n)
+                two = (2 * i, 2 * i + 1)
+                gv = [dot_tn(probs[u].astype(bf16), go2) for u in two]
+                gq = [dot_nn(gs[u], k2) for u in two]
+                gk = [dot_tn(gs[u], q2) for u in two]
+                q_ref[rows, at] = (jnp.where(first, gq[0], gq[1]) * scale).astype(bf16)
+                k_ref[rows, at] = (jnp.where(first, gk[0], gk[1]) * scale).astype(bf16)
+                v_ref[rows, at] = jnp.where(first, gv[0], gv[1]).astype(bf16)
+        head_loop(bs, body)
+
+    q_ref, k_ref, v_ref = gr.at[8], gr.at[9], gr.at[10]
+    diagonal = (1 - st) * 4096
+    bias_at = 5 + 10 * st
+    ffn_at = 13 + 14 * st
+    ffn_gain = 1 + 3 * st
+
+    def by_tiles(fn):
+        def step(t, carry):
+            fn(cols(t, 256))
+            return carry
+        lax.fori_loop(0, tiles, step, 0)
+
+    def self_project(bs):
+        rows = at_rows(bs)
+
+        def project(i, carry):
+            which, t = i // tiles, i % tiles
+            at = cols(t, 256)
+            value = dot_nn(xb[rows, :], wproj[which, :, at])
+            bias = vec[pl.ds(bias_at + which // 2, 1), at] * jnp.where(which == 1, 0.0, 1.0)
+            gr[8 + which, rows, at] = (value + bias).astype(bf16)
+            return carry
+        lax.fori_loop(0, 3 * tiles, project, 0)
+
+    def self_output(bs):
+        rows = at_rows(bs)
+
+        def tile(at):
+            acc[rows, at] = dot_nn(obuf[rows, :], wo[:, at])
+        by_tiles(tile)
+        norm_forward(bs, xb, u_self, bias_at + 2, 2 * st, bias_at + 3, hlow, grad)
+
+    def ffn_forward(bs, residual):
+        r0, n = span(bs)
+        rows = pl.ds(r0, n)
+
+        def ffn_slot(j, carry):
+            def tile(t, carry2):
+                at = cols(t, 256)
+                wide = pl.ds(pl.multiple_of(j * width + t * 256, 256), 256)
+                acc[rows, at] = dot_nn(hlow[rows, :], win[:, wide])
+
+                def activate(block):
+                    zv = acc[block, at] + bias_in[pl.ds(st, 1), wide]
+                    cdf = 0.5 * (1.0 + lax.erf(zv * (0.5 ** 0.5)))
+                    pdf = jnp.exp(-0.5 * zv * zv) * 0.3989422804014327
+                    gr[1 + j, block, at] = (zv * cdf).astype(bf16)
+                    dg[j, block, at] = (cdf + zv * pdf).astype(bf16)
+                row_loop(bs, 64, activate)
+                return carry2
+            lax.fori_loop(0, tiles, tile, 0)
+            return carry
+        lax.fori_loop(0, slots, ffn_slot, 0)
+
+        def ffn_out(at):
+            total = dot_nn(gr[1, rows, :], wout[pl.ds(0, width), at])
+            for j in range(1, slots):
+                total = total + dot_nn(gr[1 + j, rows, :], wout[pl.ds(j * width, width), at])
+            acc[rows, at] = total
+        by_tiles(ffn_out)
+        norm_forward(bs, residual, u_ffn, ffn_at, ffn_gain, ffn_at + 1, xb, None)
+
+    def ffn_inner(bs, lo, hi):
+        r0, n = span(bs)
+        rows = pl.ds(r0, n)
+
+        def ffn_inner_slot(j, carry):
+            def tile(t, carry2):
+                at = cols(t, 256)
+                wide = pl.ds(pl.multiple_of(j * width + t * 256, 256), 256)
+                acc[rows, at] = dot_nt(gr[0, rows, :], wout[wide, :])
+
+                def scale(block):
+                    gr[1 + j, block, at] = (acc[block, at] * dg[j, block, at].astype(f32)).astype(bf16)
+                row_loop(bs, 64, scale)
+                return carry2
+            lax.fori_loop(0, tiles, tile, 0)
+            if bs == long:
+                remote(gr.at[1 + j], grp.at[1 + j], gr_send.at[1 + j], gr_recv.at[1 + j], core_id).start()
+            return carry
+        lax.fori_loop(lo, hi, ffn_inner_slot, 0)
+
+    def ffn_input(bs):
+        rows = at_rows(bs)
+
+        def tile(at):
+            total = grad[rows, at]
+            for j in range(slots):
+                total = total + dot_nt(gr[1 + j, rows, :], win[at, pl.ds(j * width, width)])
+            grad[rows, at] = total
+        by_tiles(tile)
+
+    def cross_forward(bs):
+        rows = at_rows(bs)
+
+        def memory_kv(i, carry):
+            which, t = i // tiles, i % tiles
+            at = cols(t, 256)
+            value = dot_nn(mem[rows, pl.ds(0, half)], wx[2 * which, :, at]) + dot_nn(mem[rows, pl.ds(half, half)], wx[2 * which + 1, :, at])
+            kv[which, rows, at] = value.astype(bf16)
+            return carry
+        lax.fori_loop(0, 2 * tiles, memory_kv, 0)
+        attend_forward(bs, gr.at[6], kv.at[0], kv.at[1], lens[:2], 4096, 20, obuf)
+
+        def cross_out(at):
+            acc[rows, at] = dot_nn(obuf[rows, :], wsecond[:, at])
+        by_tiles(cross_out)
+        norm_forward(bs, grad, u_cross, 21, 3, 22, hlow, hw)
+        transposed(7, bs, obuf)
+
+    def cross_backward(bs):
+        rows = at_rows(bs)
+        norm_backward(bs, u_cross, grad, 3, 22, hw, gr.at[5])
+
+        def cross_up(at):
+            obuf[rows, at] = dot_nt(gr[5, rows, :], wsecond[at, :]).astype(bf16)
+        by_tiles(cross_up)
+        attend_backward(bs, gr.at[6], kv.at[0], kv.at[1], lens[:2], 4096)
+
+        def memory_half(h, carry):
+            at = cols(h, half)
+            gmem[rows, at] = (dot_nt(kv[0, rows, :], wx[h]) + dot_nt(kv[1, rows, :], wx[2 + h])).astype(bf16)
+            return carry
+        lax.fori_loop(0, 2, memory_half, 0)
+        gm_copy[bs[0]].start()
+
+    def cross_input(at):
+        grad[:, at] = hw[:, at] + dot_nt(gr[6], wfirst[at, :])
+
+    def first_copy(i, z_first):
+        return remote(one_send.at[i % SEND_SLOTS], one_recv.at[i], sem_send.at[i, 0], sem_recv.at[i, 0], near_id if z_first else y_id)
+
+    def second_copy(i, z_first):
+        source = one_recv.at[i, 1 - zh] if z_first else one_recv.at[i, :, 1 - zl]
+        return remote(source, two_recv.at[i], sem_send.at[i, 1], sem_recv.at[i, 1], far_id if z_first else near_id)
+
+    def third_copy(i, z_first):
+        source = two_recv.at[i, 1 - y if z_first else 1 - zh]
+        return remote(source, out_part.at[i], sem_send.at[i, 2], sem_recv.at[i, 2], y_id if z_first else far_id)
+
+    def own_copy(i, z_first):
+        return pltpu.make_async_copy(two_recv.at[i, y if z_first else zh], out_own.at[i], own_sem.at[i])
+
+    def product(left, slot, z_first, other, at):
+        if z_first:
+            zz = 1 - zl if other else zl
+            mine, theirs = lt[left, :, zz, :, c], ltp[left, :, zz]
+        else:
+            yy = 1 - y if other else y
+            mine, theirs = lt[left, :, :, yy, c], ltp[left, :, :, yy]
+        shape = (4 * PIECE, ROWS)
+        return dot_nn(mine.reshape(shape), gr[slot, :, at]) + dot_nn(theirs.reshape(shape), grp[slot, :, at])
+
+    def send_piece(i, left, slot, z_first=False):
+        def tile(at):
+            one_send[i % SEND_SLOTS, :, :, :, at] = product(left, slot, z_first, True, at).astype(bf16).reshape(2, 2, PIECE, 256)
+        by_tiles(tile)
+        first_copy(i, z_first).start()
+
+    def keep_piece(i, left, slot, z_first=False):
+        first_copy(i, z_first).wait()
+
+        def tile(at):
+            total = one_recv[i, :, :, :, at].reshape(4 * PIECE, 256).astype(f32) + product(left, slot, z_first, False, at)
+            one_recv[i, :, :, :, at] = total.astype(bf16).reshape(2, 2, PIECE, 256)
+        by_tiles(tile)
+        second_copy(i, z_first).start()
+
+    def pass_piece(i, z_first=False):
+        second_copy(i, z_first).wait()
+        for k in range(2):
+            mine = one_recv[i, zh, k] if z_first else one_recv[i, k, zl]
+            two_recv[i, k] = (two_recv[i, k].astype(f32) + mine.astype(f32)).astype(bf16)
+        third_copy(i, z_first).start()
+        own_copy(i, z_first).start()
+
+    def loop(lo, hi, fn):
+        def step(i, carry):
+            fn(i)
+            return carry
+        lax.fori_loop(lo, hi, step, 0)
+
+    def wait_active():
+        for i in range(4):
+            lt_copy[i].wait()
+        gr_copy[0].wait()
+
+    def first_sends():
+        loop(2, 3, lambda i: send_piece(i, i, 0))
+        loop(0, 1, lambda i: send_piece(i, i, 0, True))
+        loop(3, 4, lambda i: send_piece(i, i, 0))
+        loop(1, 2, lambda i: send_piece(i, i, 0, True))
+
+    @pl.when(is_enc)
+    def _():
+        again = pltpu.make_async_copy(x_hbm, mem, load_sem.at[8])
+        again.start()
+        for bs in (short, long):
+            self_project(bs)
+            attend_forward(bs, q_ref, k_ref, v_ref, own_lens, diagonal, None, obuf)
+            if bs == short:
+                loads[2].wait()
+            self_output(bs)
+            if bs == short:
+                loads[3].wait()
+                loads[4].wait()
+            ffn_forward(bs, grad)
+            mem_copy[bs[0]].start()
+        transposed_active(both)
+        for k in range(4):
+            lt_copy[k].start()
+        again.wait()
+        for i, ref in ((4, mem), (5, obuf), (6, hlow), (7, xb)):
+            transposed(i, both, ref)
+            lt_copy[i].start()
+        loads[5].wait()
+        loads[6].wait()
+        for bs in (short, long):
+            gm_copy[bs[0]].wait_recv()
+            norm_backward(bs, u_ffn, up, ffn_gain, ffn_at + 1, grad, gr.at[0])
+            if bs == short:
+                ffn_inner(bs, 0, slots)
+                ffn_input(bs)
+        gr_copy[0].start()
+        ffn_inner(long, 0, 2)
+        wait_active()
+        first_sends()
+        ffn_inner(long, 2, slots)
+        ffn_input(long)
+
+    @pl.when(is_dec)
+    def _():
+        self_project(both)
+        transposed(4, both, xb)
+        lt_copy[4].start()
+
+        def wx_forward(h):
+            wx_first[h].wait_recv()
+            wx_y[h].start()
+            wx_near[h].start()
+        wx_forward(0)
+        attend_forward(both, q_ref, k_ref, v_ref, own_lens, diagonal, None, obuf)
+        wx_forward(1)
+        loads[2].wait()
+        self_output(both)
+        wx_forward(2)
+        for cp in loads[3:]:
+            cp.wait()
+
+        def cross_query(at):
+            gr[6, :, at] = (dot_nn(hlow[...], wfirst[:, at]) + vec[pl.ds(19, 1), at]).astype(bf16)
+        by_tiles(cross_query)
+        wx_forward(3)
+        transposed(5, both, obuf)
+        lt_copy[5].start()
+        transposed(8, both, hlow)
+        lt_copy[8].start()
+        cot_load.wait()
+        for h in range(WX_CHUNKS):
+            wx_y[h].wait()
+            wx_far[h].start()
+        for h in range(WX_CHUNKS):
+            wx_near[h].wait()
+            wx_far[h].wait()
+        for bs in (short, long):
+            mem_copy[bs[0]].wait_recv()
+            cross_forward(bs)
+            ffn_forward(bs, hw)
+            transposed_active(bs)
+            norm_backward(bs, u_ffn, up, ffn_gain, ffn_at + 1, grad, gr.at[0])
+            ffn_inner(bs, 0, slots)
+            ffn_input(bs)
+            cross_backward(bs)
+        gr_copy[0].start()
+        for k in range(4):
+            lt_copy[k].start()
+        transposed(6, both, hlow)
+        lt_copy[6].start()
+        lt_copy[7].start()
+        wait_active()
+        first_sends()
+        gr_copy[5].start()
+        gr_copy[6].start()
+        by_tiles(cross_input)
+        col_sum(obuf, 20)
+        col_sum(gr.at[6], 19)
+        col_sum(gr.at[5], 21)
+
+    rows_copy = pltpu.make_async_copy(xb, out_rows, io_sem.at[0])
+    rows_copy.start()
+    lt_copy[6].wait()
+    for j in range(slots):
+        gr_copy[1 + j].wait()
+    loop(4, 8, lambda i: send_piece(i, 6, i - 3))
+
+    norm_backward(both, u_self, grad, 2 * st, bias_at + 3, hw, gr.at[7])
+    gr_copy[7].start()
+
+    def self_up(at):
+        obuf[:, at] = dot_nt(gr[7], wo[at, :]).astype(bf16)
+    by_tiles(self_up)
+    loop(2, 3, lambda i: keep_piece(i, i, 0))
+    loop(0, 1, lambda i: keep_piece(i, i, 0, True))
+    attend_backward(both, q_ref, k_ref, v_ref, own_lens, diagonal)
+    for j in range(3):
+        gr_copy[8 + j].start()
+
+    @pl.when(is_dec)
+    def _():
+        gk_copy[0].start()
+        gk_copy[1].start()
+    loop(3, 4, lambda i: keep_piece(i, i, 0))
+    loop(1, 2, lambda i: keep_piece(i, i, 0, True))
+    loop(2, 3, lambda i: pass_piece(i))
+    loop(0, 1, lambda i: pass_piece(i, True))
+
+    def self_input(at):
+        total = hw[:, at]
+        for j in range(3):
+            total = total + dot_nt(gr[8 + j], wproj[j, at, :])
+        hw[:, at] = total
+    by_tiles(self_input)
+    grad_copy = pltpu.make_async_copy(hw, out_grad, io_sem.at[1])
+    grad_copy.start()
+    loop(4, 5, lambda i: keep_piece(i, 6, i - 3))
+    for i in (4, 5, 7):
+        lt_copy[i].wait()
+
+    @pl.when(is_dec)
+    def _():
+        lt_copy[8].wait()
+    for i in range(7, 11):
+        gr_copy[i].wait()
+    first_left = 7 + st
+    rest = ((8, 5, 7), (9, 4, 8), (10, 4, 9), (11, 4, 10), (12, 7, 5), (13, first_left, 6))
+
+    col_sum(gr.at[0], ffn_at)
+    loop(0, slots, lambda j: col_sum(gr.at[1 + j], ffn_at - 4 + j))
+    col_sum(gr.at[7], bias_at + 2)
+    col_sum(gr.at[8], bias_at)
+    col_sum(gr.at[10], bias_at + 1)
+    v_copy = [remote(vbuf.at[2 * k], vbuf.at[2 * k + 1], v_send.at[k], v_recv.at[k], dev)
+              for k, dev in enumerate((core_id, y_id, near_id, far_id, x_id))]
+    vbuf[0] = vg[...]
+
+    def v_next(k):
+        v_copy[k].wait()
+        vbuf[2 * k + 2] = vbuf[2 * k] + vbuf[2 * k + 1]
+        v_copy[k + 1].start()
+    v_copy[0].start()
+    for i, left, slot in rest[:2]:
+        send_piece(i, left, slot)
+    v_next(0)
+    for i, left, slot in rest[2:4]:
+        send_piece(i, left, slot)
+    loop(3, 4, lambda i: pass_piece(i))
+    loop(1, 2, lambda i: pass_piece(i, True))
+    loop(5, 6, lambda i: keep_piece(i, 6, i - 3))
+    loop(4, 5, lambda i: pass_piece(i))
+
+    @pl.when(is_enc)
+    def _():
+        gk_copy[0].wait_recv()
+        gk_copy[1].wait_recv()
+        gr_copy[5].start()
+        gr_copy[6].start()
+    loop(6, 7, lambda i: keep_piece(i, 6, i - 3))
+    for i in range(5, 7):
+        gr_copy[i].wait()
+    for i, left, slot in rest[4:]:
+        send_piece(i, left, slot)
+    loop(5, 6, lambda i: pass_piece(i))
+    loop(7, 8, lambda i: keep_piece(i, 6, i - 3))
+    loop(6, 7, lambda i: pass_piece(i))
+    for k, (i, left, slot) in enumerate(rest):
+        keep_piece(i, left, slot)
+        pass_piece(i - 1)
+        if 2 <= k <= 4:
+            v_next(k - 1)
+    pass_piece(13)
+    v_copy[4].wait()
+    out_vec[...] = vbuf[8] + vbuf[9]
+
+    def finish(i, z_first=False):
+        third_copy(i, z_first).wait()
+        own_copy(i, z_first).wait()
+    loop(0, 2, lambda i: finish(i, True))
+    loop(2, PIECES, finish)
+    rows_copy.wait()
+    grad_copy.wait()
+
+    @pl.when(is_enc)
+    def _():
+        for h in range(WX_CHUNKS):
+            wx_first[h].wait_send()
+        for h in range(2):
+            mem_copy[h].wait_send()
+
+    @pl.when(is_dec)
+    def _():
+        for h in range(2):
+            gm_copy[h].wait_send()
+            gk_copy[h].wait_send()
+
+
+def last_kernel(width, rows_in, grad_in, own, parts, vec_sum, rows_out, grad_out, *refs):
+    outs, (rows_buf, grad_buf, own_buf, part_buf, sums, in_sem, through_sem, out_sem) = refs[:8], refs[8:]
+    into = [pltpu.make_async_copy(rows_in, rows_buf, through_sem.at[0]), pltpu.make_async_copy(grad_in, grad_buf, through_sem.at[1])]
+    through = [pltpu.make_async_copy(rows_buf, rows_out, out_sem.at[PIECES]),
+               pltpu.make_async_copy(grad_buf, grad_out, out_sem.at[PIECES + 1])]
+    for cp in into:
+        cp.start()
+    loads = [(pltpu.make_async_copy(own.at[i], own_buf.at[i], in_sem.at[i, 0]),
+              pltpu.make_async_copy(parts.at[i], part_buf.at[i], in_sem.at[i, 1])) for i in range(PIECES)]
+    for pair in loads:
+        for cp in pair:
+            cp.start()
+    shift = lax.rem(width - lax.axis_index("dp") * PIECE, width)
+    turned = pltpu.roll(vec_sum[...], shift, 1)
+    outs[6][...] = turned[:5, :PIECE]
+    outs[7][...] = turned[5:29, :PIECE]
+    for cp, out in zip(into, through):
+        cp.wait()
+        out.start()
+    stores = []
+    for i in range(PIECES):
+        for cp in loads[i]:
+            cp.wait()
+        sums[i] = own_buf[i].astype(f32) + part_buf[i].astype(f32)
+        if i < 4:
+            target = outs[0].at[pl.ds(i * PIECE, PIECE), :]
+        elif i < 8:
+            target = outs[1].at[:, pl.ds((i - 4) * width, width)]
+        elif i == 8:
+            target = outs[4]
+        elif i < 12:
+            target = outs[5].at[i - 9]
+        else:
+            target = outs[i - 10]
+        stores.append(pltpu.make_async_copy(sums.at[i], target, out_sem.at[i]))
+        stores[-1].start()
+    for cp in stores + through:
+        cp.wait()
+
+
+def whole_step(lengths, gains, biases, x, cot, wproj, wo, wfirst, wsecond, win, wout):
+    width = x.shape[1]
+    hidden = win.shape[1]
+    half = width // 2
+    any_space = pl.BlockSpec(memory_space=pl.ANY)
+    vmem = pl.BlockSpec(memory_space=pltpu.VMEM)
+    dma = pltpu.SemaphoreType.DMA
+    slots = hidden // width
+    small = (32, width)
+    results = pl.pallas_call(
+        functools.partial(step_kernel, width, hidden),
+        out_shape=[
+            jax.ShapeDtypeStruct((ROWS, width), bf16),
+            jax.ShapeDtypeStruct((ROWS, width), f32),
+            jax.ShapeDtypeStruct((PIECES, PIECE, width), bf16),
+            jax.ShapeDtypeStruct((PIECES, PIECE, width), bf16),
+            jax.ShapeDtypeStruct(small, f32),
+        ],
+        in_specs=[pl.BlockSpec(memory_space=pltpu.SMEM), vmem, vmem] + [any_space] * 8,
+        out_specs=[any_space] * 4 + [vmem],
+        scratch_shapes=[
+            pltpu.VMEM(small, f32), pltpu.VMEM((2, hidden), f32),
+            pltpu.VMEM(wproj.shape, bf16), pltpu.VMEM(wo.shape, bf16), pltpu.VMEM(wfirst.shape, bf16),
+            pltpu.VMEM(wsecond.shape, bf16), pltpu.VMEM(win.shape, bf16), pltpu.VMEM(wout.shape, bf16),
+            pltpu.VMEM((4, half, width), bf16),
+            pltpu.VMEM((ROWS, width), bf16),
+            pltpu.VMEM((ROWS, width), bf16),
+            pltpu.VMEM((ROWS, width), bf16),
+            pltpu.VMEM((ROWS, width), bf16),
+            pltpu.VMEM((ROWS, width), bf16),
+            pltpu.VMEM((slots, ROWS, width), bf16),
+            pltpu.VMEM((2, ROWS, width), bf16),
+            pltpu.VMEM((ROWS, width), f32),
+            pltpu.VMEM((ROWS, width), f32),
+            pltpu.VMEM((ROWS, width), f32),
+            pltpu.VMEM((ROWS, width), f32),
+            pltpu.VMEM((ROWS, width), f32),
+            pltpu.VMEM((ROWS, width), f32),
+            pltpu.VMEM((11, ROWS, width), bf16),
+            pltpu.VMEM((11, ROWS, width), bf16),
+            pltpu.VMEM((9, 2, 2, 2, 2, PIECE, ROWS), bf16),
+            pltpu.VMEM((9, 2, 2, 2, PIECE, ROWS), bf16),
+            pltpu.VMEM((SEND_SLOTS, 2, 2, PIECE, width), bf16),
+            pltpu.VMEM((PIECES, 2, 2, PIECE, width), bf16),
+            pltpu.VMEM((PIECES, 2, PIECE, width), bf16),
+            pltpu.VMEM((ROWS, width), bf16),
+            pltpu.VMEM(small, f32),
+            pltpu.VMEM((10,) + small, f32),
+            dma((9,)), dma((4 * WX_CHUNKS,)), dma((4 * WX_CHUNKS,)), dma((2,)), dma((2,)), dma((2,)), dma((2,)), dma((2,)), dma((2,)),
+            dma((9,)), dma((9,)), dma((11,)), dma((11,)),
+            dma((PIECES, 3)), dma((PIECES, 3)), dma((PIECES,)), dma((2,)), dma((5,)), dma((5,)),
+        ],
+        compiler_params=pltpu.CompilerParams(collective_id=0, has_side_effects=True, vmem_limit_bytes=VMEM_LIMIT),
+        name="step",
+    )(lengths, gains, biases, x, cot, wproj, wo, wfirst, wsecond, win, wout)
+    shapes = [(4 * PIECE, width), (PIECE, hidden), (PIECE, width), (PIECE, width), (PIECE, width), (3, PIECE, width),
+              (5, PIECE), (24, PIECE)]
+    return pl.pallas_call(
+        functools.partial(last_kernel, width),
+        out_shape=[jax.ShapeDtypeStruct((ROWS, width), bf16), jax.ShapeDtypeStruct((ROWS, width), f32)]
+        + [jax.ShapeDtypeStruct(shape, f32) for shape in shapes],
+        in_specs=[any_space] * 4 + [vmem],
+        out_specs=[any_space] * 8 + [vmem] * 2,
+        scratch_shapes=[
+            pltpu.VMEM((ROWS, width), bf16), pltpu.VMEM((ROWS, width), f32),
+            pltpu.VMEM((PIECES, PIECE, width), bf16), pltpu.VMEM((PIECES, PIECE, width), bf16),
+            pltpu.VMEM((PIECES, PIECE, width), f32), dma((PIECES, 2)), dma((2,)), dma((PIECES + 2,)),
+        ],
+        compiler_params=pltpu.CompilerParams(vmem_limit_bytes=VMEM_LIMIT),
+        name="last",
+    )(*results)
 
 
 eps_norm = 1e-05
@@ -326,7 +1116,7 @@
     return progress
 
 
-def body(
+def plain_body(
     inputs,
     lengths,
     cotangent,
@@ -594,7 +1384,19 @@
     )
 
 
+def fused_body(inputs, lengths, cotangent, attn_in, attn_out, cross_first, cross_second, ffn_in, ffn_out, gains, biases):
+    rows, grad, s_out, s_in, s_second, s_first, s_attn, s_proj, own_gains, own_biases = whole_step(
+        lengths, gains, biases, inputs[0], cotangent, attn_in[0], attn_out[0],
+        cross_first[0], cross_second[0], ffn_in[0], ffn_out[0])
+    return (rows[None], grad[None], s_proj[None], s_attn[None], s_first[None], s_second[None],
+            s_in[None], s_out[None], own_gains, own_biases)
+
+
 def solution(mesh):
+    def body(*args):
+        width = args[0].shape[2]
+        fits = mesh.shape["dp"] * PIECE == width and args[0].shape[1] == ROWS and args[7].shape[2] == 4 * width
+        return (fused_body if fits else plain_body)(*args)
     return jax.shard_map(
         body,
         mesh=mesh,

time: 1260 us -> 191 us (0.15); the launches traced: 1240 us -> 191 us
  waiting for transfers between devices: 793 us -> 0 us
  Pallas kernels: 0 us -> 190 us
  matrix products: 172 us -> 0 us
  local copies, waits for them, and re-layouts: 154 us -> 0 us
  other arithmetic: 55.8 us -> 0 us
  loops' own time: 24.7 us -> 0 us
  starting transfers between devices: 22.2 us -> 0 us
  between operations: 14.4 us -> 0.84 us
    reduce_scatter x6 -> x0, waiting for transfers between devices: 516 us -> none  [the longest x1 116 us: body(): lax.psum_scatter(totals['ffn_out'], 'dp', scatter_dimension=0, tiled=True)]
    ppermute x4 -> x0, waiting for transfers between devices: 201 us -> none  [shifted(): return lax.ppermute(shard, axis, pairs)]
    pallas_call x0 -> x2, Pallas kernels: none -> 190 us  [the longest x1 184 us: whole_step(): pl.pallas_call(functools.partial(step_kernel, width, hidden), out_shape=[...]
    dot_general x50 -> x0, matrix products: 172 us -> none  [the longest x10 54 us: matmul_tn(): lax.dot_general(left_mat, right_mat, (((0,), (0,)), ((), ())), preferred_...]
    unnamed x10 -> x0, waiting for transfers between devices: 76.3 us -> none
    another operation x56 -> x0, local copies, waits for them, and re-layouts: 50.7 us -> none
    cond x100 -> x0, local copies, waits for them, and re-layouts: 41.3 us -> none  [the longest x2 19.4 us: body(): progress = lax.cond(is_decoder, keep_same, enc_four, progress)]
    another operation x4 -> x0, loops' own time: 23.9 us -> none  [the longest x1 14.6 us: body(): progress = lax.cond(is_decoder, dec_three, enc_three, progress)]
  transfers between devices with their start and end apart: 12 -> 0, of which waited for: 11 -> 0; matrix products, arithmetic and copies ran while one was open for 4% -> 0% of each run, Pallas kernels for 0% -> 0%
where the time goes in v3:
time: 191 us
  Pallas kernels  190 us (99%)
    pallas_call x1, Pallas kernels, whole_step(): pl.pallas_call(functools.partial(step_kernel, width, hidden), out_shape=[...  184 us
    pallas_call x1, Pallas kernels, whole_step(): pl.pallas_call(functools.partial(last_kernel, width), out_shape=[jax.Shap...  5.77 us

profile of v3, /device:TPU:0, one launch (start us, length us, event | category | flops | bytes accessed | tf_op | source)
XLA Modules:
  0.0 190.6 jit_solution(4992037174363305517)
XLA Ops:
  0.6 184.0 %step.1 = (bf16[384,768]{1,0:T(8,128)(2,1)}, f32[384,768]{1,0:T(8,128)}, bf16[14,48,768]{2,1,0:T(8,128)(2,1)}, bf16[14,48,768]{2,1,0:T(8,128)(2,1)}, f32[32,768]{1,0:T(8,128)}) custom-call(s32[2,1,2]{2,1,0:T(1,128)} %lengths.1, bf16[5,768]{1,0:T(8,128)(2,1)} %gains.1, bf16[24,768]{1,0:T(8,128)(2,1)} %biases.1, bf16[384,768]{1,0:T(8,128)(2,1)} %bitcast.21, ...), custom_call_target="tpu_custom_call" | custom-call | tf_op jit(solution)/shard_map/step/pallas_call | solution.py:737
  184.6 5.8 %last.1 = (bf16[384,768]{1,0:T(8,128)(2,1)}, f32[384,768]{1,0:T(8,128)}, f32[192,768]{1,0:T(8,128)}, f32[48,3072]{1,0:T(8,128)}, f32[48,768]{1,0:T(8,128)}, /*in...) custom-call(bf16[384,768]{1,0:T(8,128)(2,1)} %get-tuple-element.25.rows_in, ...), custom_call_target="tpu_custom_call" | custom-call | tf_op jit(solution)/shard_map/last/pallas_call | solution.py:785

commit v4 on v3

--- a/solution.py
+++ b/solution.py
@@ -13,6 +13,7 @@
 ROWS = SHORT + LONG
 PIECE = 48
 PIECES = 14
+VEC_ROWS = 24
 SEND_SLOTS = 8
 WX_CHUNKS = 4
 MESH = pl.DeviceIdType.MESH
@@ -41,7 +42,7 @@
     lengths, gains, biases, x_hbm, cot_hbm, wproj_hbm, wo_hbm, wfirst_hbm, wsecond_hbm, win_hbm, wout_hbm,
     out_rows, out_grad, out_own, out_part, out_vec,
     vec, bias_in, wproj, wo, wfirst, wsecond, win, wout, wx,
-    xb, up, mem, obuf, hlow, dg, kv, acc, grad, hw, u_self, u_cross, u_ffn, gr, grp, lt, ltp, one_send, one_recv, two_recv, gmem, vg, vbuf,
+    xb, up, mem, obuf, hlow, dg, kv, acc, grad, hw, u_self, u_cross, u_ffn, gr, grp, lt, ltp, one_send, one_recv, two_recv, gmem, vg, vbuf, vboth,
     load_sem, wx_send, wx_recv, mem_send, mem_recv, gm_send, gm_recv, gk_send, gk_recv, lt_send, lt_recv, gr_send, gr_recv,
     sem_send, sem_recv, own_sem, io_sem, v_send, v_recv,
 ):
@@ -127,8 +128,10 @@
     def _():
         cot_load.start()
 
+    gain_row = lambda r: pl.ds(r - 2 * st, 1)
+    bias_row_of = lambda r: pl.ds(r - 2 - 10 * st, 1)
     lt_copy = [remote(lt.at[i, :, :, :, 1 - c], ltp.at[i], lt_send.at[i], lt_recv.at[i], core_id) for i in range(9)]
-    gr_copy = [remote(gr.at[i], grp.at[i], gr_send.at[i], gr_recv.at[i], core_id) for i in range(11)]
+    gr_copy = {i: remote(gr.at[i], grp.at[i], gr_send.at[i], gr_recv.at[i], core_id) for i in range(5, 11)}
     buckets = ((0, SHORT), (SHORT, LONG))
     short, long, both = (0,), (1,), (0, 1)
 
@@ -142,6 +145,9 @@
     gk_copy = [remote(kv.at[0], gr.at[6], gk_send.at[0], gk_recv.at[0], x_id),
                remote(kv.at[1], gr.at[5], gk_send.at[1], gk_recv.at[1], x_id)]
 
+    gr_first = [remote(gr.at[0, at_rows((b,))], grp.at[0, at_rows((b,))], gr_send.at[11 * b], gr_recv.at[11 * b], core_id)
+                for b in range(2)]
+
     def row_loop(bs, block, body, unroll=1):
         r0, n = span(bs)
 
@@ -172,7 +178,7 @@
             block = slot[pl.ds(pl.multiple_of(i * 64, 64), 64), :].astype(f32)
             return carry + jnp.sum(block.reshape(8, 8, width), axis=0)
         total = lax.fori_loop(0, ROWS // 64, step, jnp.zeros((8, width), f32))
-        vg[pl.ds(row, 1), :] = jnp.sum(total, axis=0, keepdims=True)
+        vg[bias_row_of(row), :] = jnp.sum(total, axis=0, keepdims=True)
 
     def norm_forward(bs, residual, sum_ref, add_bias, gain, shift, out_low, out_wide):
         def body(rows):
@@ -205,11 +211,11 @@
                     carry[1] + jnp.sum(r.reshape(4, 8, width), axis=0))
         zero = jnp.zeros((8, width), f32)
         total = lax.fori_loop(0, n // 32, step, (zero, zero), unroll=4)
-        for row, part in ((gain, total[0]), (shift, total[1])):
-            vg[pl.ds(row, 1), :] = vg[pl.ds(row, 1), :] + jnp.sum(part, axis=0, keepdims=True)
+        for row, part in ((gain_row(gain), total[0]), (bias_row_of(shift), total[1])):
+            vg[row, :] = vg[row, :] + jnp.sum(part, axis=0, keepdims=True)
 
     def masked_scores(q_half, k2, n, length, diagonal):
-        s = dot_nt(q_half, k2) * (HDIM ** -0.5)
+        s = dot_nt(q_half, k2)
         column = lax.broadcasted_iota(jnp.int32, (n, n), 1)
         row = lax.broadcasted_iota(jnp.int32, (n, n), 0)
         return jnp.where((column < length) & (column <= row + diagonal), s, -1e30)
@@ -222,13 +228,13 @@
         lane = lax.broadcasted_iota(jnp.int32, (n, 2 * HDIM), 1)
         return lane < HDIM
 
-    def head_loop(bs, body):
+    def head_loop(bs, body, lo=0, hi=None):
         pairs = {short: 3, long: 2, both: 1}[bs]
 
         def step(p, carry):
             body([(b, pl.ds(pl.multiple_of((p * pairs + i) * 2 * HDIM, 2 * HDIM), 2 * HDIM)) for b in bs for i in range(pairs)])
             return carry
-        lax.fori_loop(0, width // (2 * HDIM * pairs), step, 0)
+        lax.fori_loop(lo, width // (2 * HDIM * pairs) if hi is None else hi, step, 0)
 
     def attend_forward(bs, q_ref, k_ref, v_ref, lengths_at, diagonal, bias_row, out_ref):
         def body(units):
@@ -239,7 +245,7 @@
                 q2, k2 = q_ref[rows, at], k_ref[rows, at]
                 first = halves(n)
                 for lanes in (first, ~first):
-                    work.append(masked_scores(jnp.where(lanes, q2, jnp.zeros_like(q2)), k2, n, lengths_at[b], diagonal))
+                    work.append(masked_scores(jnp.where(lanes, q2 * 0.125, jnp.zeros_like(q2)), k2, n, lengths_at[b], diagonal))
             work = [softmax(s).astype(bf16) for s in work]
             work = [dot_nn(prob, v_ref[pl.ds(*buckets[units[i // 2][0]]), units[i // 2][1]]) for i, prob in enumerate(work)]
             for i, (b, at) in enumerate(units):
@@ -250,7 +256,7 @@
                 out_ref[pl.ds(r0, n), at] = att.astype(bf16)
         head_loop(bs, body)
 
-    def attend_backward(bs, q_ref, k_ref, v_ref, lengths_at, diagonal):
+    def attend_backward(bs, q_ref, k_ref, v_ref, lengths_at, diagonal, lo=0, hi=None):
         scale = HDIM ** -0.5
 
         def body(units):
@@ -262,7 +268,7 @@
                 first = halves(n)
                 zero = jnp.zeros_like(q2)
                 for lanes in (first, ~first):
-                    scores.append(masked_scores(jnp.where(lanes, q2, zero), k2, n, lengths_at[b], diagonal))
+                    scores.append(masked_scores(jnp.where(lanes, q2 * 0.125, zero), k2, n, lengths_at[b], diagonal))
                     ups.append(dot_nt(jnp.where(lanes, go2, zero), v2))
             probs = [softmax(s) for s in scores]
             gs = [(p * (gp - jnp.sum(p * gp, axis=-1, keepdims=True))).astype(bf16) for p, gp in zip(probs, ups)]
@@ -278,7 +284,7 @@
                 q_ref[rows, at] = (jnp.where(first, gq[0], gq[1]) * scale).astype(bf16)
                 k_ref[rows, at] = (jnp.where(first, gk[0], gk[1]) * scale).astype(bf16)
                 v_ref[rows, at] = jnp.where(first, gv[0], gv[1]).astype(bf16)
-        head_loop(bs, body)
+        head_loop(bs, body, lo, hi)
 
     q_ref, k_ref, v_ref = gr.at[8], gr.at[9], gr.at[10]
     diagonal = (1 - st) * 4096
@@ -287,22 +293,20 @@
     ffn_gain = 1 + 3 * st
 
     def by_tiles(fn):
-        def step(t, carry):
-            fn(cols(t, 256))
-            return carry
-        lax.fori_loop(0, tiles, step, 0)
+        for t in range(tiles):
+            fn(pl.ds(t * 256, 256))
 
     def self_project(bs):
         rows = at_rows(bs)
 
-        def project(i, carry):
-            which, t = i // tiles, i % tiles
-            at = cols(t, 256)
-            value = dot_nn(xb[rows, :], wproj[which, :, at])
-            bias = vec[pl.ds(bias_at + which // 2, 1), at] * jnp.where(which == 1, 0.0, 1.0)
-            gr[8 + which, rows, at] = (value + bias).astype(bf16)
+        def project(which, carry):
+            for t in range(tiles):
+                at = pl.ds(t * 256, 256)
+                value = dot_nn(xb[rows, :], wproj[which, :, at])
+                bias = vec[pl.ds(bias_at + which // 2, 1), at] * jnp.where(which == 1, 0.0, 1.0)
+                gr[8 + which, rows, at] = (value + bias).astype(bf16)
             return carry
-        lax.fori_loop(0, 3 * tiles, project, 0)
+        lax.fori_loop(0, 3, project, 0)
 
     def self_output(bs):
         rows = at_rows(bs)
@@ -312,26 +316,22 @@
         by_tiles(tile)
         norm_forward(bs, xb, u_self, bias_at + 2, 2 * st, bias_at + 3, hlow, grad)
 
-    def ffn_forward(bs, residual):
+    def ffn_forward(bs, residual, wait_in, wait_out):
         r0, n = span(bs)
         rows = pl.ds(r0, n)
 
         def ffn_slot(j, carry):
-            def tile(t, carry2):
-                at = cols(t, 256)
+            for t in range(tiles):
+                at = pl.ds(t * 256, 256)
                 wide = pl.ds(pl.multiple_of(j * width + t * 256, 256), 256)
-                acc[rows, at] = dot_nn(hlow[rows, :], win[:, wide])
-
-                def activate(block):
-                    zv = acc[block, at] + bias_in[pl.ds(st, 1), wide]
-                    cdf = 0.5 * (1.0 + lax.erf(zv * (0.5 ** 0.5)))
-                    pdf = jnp.exp(-0.5 * zv * zv) * 0.3989422804014327
-                    gr[1 + j, block, at] = (zv * cdf).astype(bf16)
-                    dg[j, block, at] = (cdf + zv * pdf).astype(bf16)
-                row_loop(bs, 64, activate)
-                return carry2
-            lax.fori_loop(0, tiles, tile, 0)
+                zv = dot_nn(hlow[rows, :], win[:, wide]) + bias_in[pl.ds(st, 1), wide]
+                cdf = 0.5 * (1.0 + lax.erf(zv * (0.5 ** 0.5)))
+                pdf = jnp.exp(-0.5 * zv * zv) * 0.3989422804014327
+                gr[1 + j, rows, at] = (zv * cdf).astype(bf16)
+                dg[j, rows, at] = (cdf + zv * pdf).astype(bf16)
             return carry
+        if wait_in:
+            loads[3].wait()
         lax.fori_loop(0, slots, ffn_slot, 0)
 
         def ffn_out(at):
@@ -339,25 +339,22 @@
             for j in range(1, slots):
                 total = total + dot_nn(gr[1 + j, rows, :], wout[pl.ds(j * width, width), at])
             acc[rows, at] = total
+        if wait_out:
+            loads[4].wait()
         by_tiles(ffn_out)
         norm_forward(bs, residual, u_ffn, ffn_at, ffn_gain, ffn_at + 1, xb, None)
 
-    def ffn_inner(bs, lo, hi):
+    def ffn_inner(bs, lo, hi, last):
         r0, n = span(bs)
         rows = pl.ds(r0, n)
 
         def ffn_inner_slot(j, carry):
-            def tile(t, carry2):
-                at = cols(t, 256)
+            for t in range(tiles):
+                at = pl.ds(t * 256, 256)
                 wide = pl.ds(pl.multiple_of(j * width + t * 256, 256), 256)
-                acc[rows, at] = dot_nt(gr[0, rows, :], wout[wide, :])
-
-                def scale(block):
-                    gr[1 + j, block, at] = (acc[block, at] * dg[j, block, at].astype(f32)).astype(bf16)
-                row_loop(bs, 64, scale)
-                return carry2
-            lax.fori_loop(0, tiles, tile, 0)
-            if bs == long:
+                value = dot_nt(gr[0, rows, :], wout[wide, :])
+                gr[1 + j, rows, at] = (value * dg[j, rows, at].astype(f32)).astype(bf16)
+            if last:
                 remote(gr.at[1 + j], grp.at[1 + j], gr_send.at[1 + j], gr_recv.at[1 + j], core_id).start()
             return carry
         lax.fori_loop(lo, hi, ffn_inner_slot, 0)
@@ -375,13 +372,13 @@
     def cross_forward(bs):
         rows = at_rows(bs)
 
-        def memory_kv(i, carry):
-            which, t = i // tiles, i % tiles
-            at = cols(t, 256)
-            value = dot_nn(mem[rows, pl.ds(0, half)], wx[2 * which, :, at]) + dot_nn(mem[rows, pl.ds(half, half)], wx[2 * which + 1, :, at])
-            kv[which, rows, at] = value.astype(bf16)
+        def memory_kv(which, carry):
+            for t in range(tiles):
+                at = pl.ds(t * 256, 256)
+                value = dot_nn(mem[rows, pl.ds(0, half)], wx[2 * which, :, at]) + dot_nn(mem[rows, pl.ds(half, half)], wx[2 * which + 1, :, at])
+                kv[which, rows, at] = value.astype(bf16)
             return carry
-        lax.fori_loop(0, 2 * tiles, memory_kv, 0)
+        lax.fori_loop(0, 2, memory_kv, 0)
         attend_forward(bs, gr.at[6], kv.at[0], kv.at[1], lens[:2], 4096, 20, obuf)
 
         def cross_out(at):
@@ -409,19 +406,31 @@
     def cross_input(at):
         grad[:, at] = hw[:, at] + dot_nt(gr[6], wfirst[at, :])
 
-    def first_copy(i, z_first):
-        return remote(one_send.at[i % SEND_SLOTS], one_recv.at[i], sem_send.at[i, 0], sem_recv.at[i, 0], near_id if z_first else y_id)
-
-    def second_copy(i, z_first):
-        source = one_recv.at[i, 1 - zh] if z_first else one_recv.at[i, :, 1 - zl]
-        return remote(source, two_recv.at[i], sem_send.at[i, 1], sem_recv.at[i, 1], far_id if z_first else near_id)
-
-    def third_copy(i, z_first):
-        source = two_recv.at[i, 1 - y if z_first else 1 - zh]
-        return remote(source, out_part.at[i], sem_send.at[i, 2], sem_recv.at[i, 2], y_id if z_first else far_id)
-
-    def own_copy(i, z_first):
-        return pltpu.make_async_copy(two_recv.at[i, y if z_first else zh], out_own.at[i], own_sem.at[i])
+    def lanes_of(h):
+        return pl.ds(0, width) if h is None else cols(h, half)
+
+    def sems(i, stage, h):
+        k = 2 * stage + (0 if h is None else h)
+        return sem_send.at[i, k], sem_recv.at[i, k]
+
+    def first_copy(i, z_first, h):
+        at = lanes_of(h)
+        return remote(one_send.at[i % SEND_SLOTS, :, :, :, at], one_recv.at[i, :, :, :, at], *sems(i, 0, h),
+                      near_id if z_first else y_id)
+
+    def second_copy(i, z_first, h):
+        at = lanes_of(h)
+        source = one_recv.at[i, 1 - zh, :, :, at] if z_first else one_recv.at[i, :, 1 - zl, :, at]
+        return remote(source, two_recv.at[i, :, :, at], *sems(i, 1, h), far_id if z_first else near_id)
+
+    def third_copy(i, z_first, h):
+        at = lanes_of(h)
+        source = two_recv.at[i, 1 - y if z_first else 1 - zh, :, at]
+        return remote(source, out_part.at[i, :, at], *sems(i, 2, h), y_id if z_first else far_id)
+
+    def own_copy(i, z_first, h):
+        at = lanes_of(h)
+        return pltpu.make_async_copy(two_recv.at[i, y if z_first else zh, :, at], out_own.at[i, :, at], own_sem.at[i, 0 if h is None else h])
 
     def product(left, slot, z_first, other, at):
         if z_first:
@@ -433,28 +442,35 @@
         shape = (4 * PIECE, ROWS)
         return dot_nn(mine.reshape(shape), gr[slot, :, at]) + dot_nn(theirs.reshape(shape), grp[slot, :, at])
 
-    def send_piece(i, left, slot, z_first=False):
-        def tile(at):
-            one_send[i % SEND_SLOTS, :, :, :, at] = product(left, slot, z_first, True, at).astype(bf16).reshape(2, 2, PIECE, 256)
-        by_tiles(tile)
-        first_copy(i, z_first).start()
-
-    def keep_piece(i, left, slot, z_first=False):
-        first_copy(i, z_first).wait()
-
-        def tile(at):
-            total = one_recv[i, :, :, :, at].reshape(4 * PIECE, 256).astype(f32) + product(left, slot, z_first, False, at)
-            one_recv[i, :, :, :, at] = total.astype(bf16).reshape(2, 2, PIECE, 256)
-        by_tiles(tile)
-        second_copy(i, z_first).start()
-
-    def pass_piece(i, z_first=False):
-        second_copy(i, z_first).wait()
+    def piece_tiles(h, fn):
+        if h is None:
+            loop(0, tiles, lambda t: fn(cols(t, 256), 256))
+        else:
+            fn(cols(h, half), half)
+
+    def send_piece(i, left, slot, z_first=False, h=None):
+        def tile(at, n):
+            one_send[i % SEND_SLOTS, :, :, :, at] = product(left, slot, z_first, True, at).astype(bf16).reshape(2, 2, PIECE, n)
+        piece_tiles(h, tile)
+        first_copy(i, z_first, h).start()
+
+    def keep_piece(i, left, slot, z_first=False, h=None):
+        first_copy(i, z_first, h).wait()
+
+        def tile(at, n):
+            total = one_recv[i, :, :, :, at].reshape(4 * PIECE, n).astype(f32) + product(left, slot, z_first, False, at)
+            one_recv[i, :, :, :, at] = total.astype(bf16).reshape(2, 2, PIECE, n)
+        piece_tiles(h, tile)
+        second_copy(i, z_first, h).start()
+
+    def pass_piece(i, z_first=False, h=None):
+        second_copy(i, z_first, h).wait()
+        at = lanes_of(h)
         for k in range(2):
-            mine = one_recv[i, zh, k] if z_first else one_recv[i, k, zl]
-            two_recv[i, k] = (two_recv[i, k].astype(f32) + mine.astype(f32)).astype(bf16)
-        third_copy(i, z_first).start()
-        own_copy(i, z_first).start()
+            mine = one_recv[i, zh, k, :, at] if z_first else one_recv[i, k, zl, :, at]
+            two_recv[i, k, :, at] = (two_recv[i, k, :, at].astype(f32) + mine.astype(f32)).astype(bf16)
+        third_copy(i, z_first, h).start()
+        own_copy(i, z_first, h).start()
 
     def loop(lo, hi, fn):
         def step(i, carry):
@@ -465,28 +481,20 @@
     def wait_active():
         for i in range(4):
             lt_copy[i].wait()
-        gr_copy[0].wait()
-
-    def first_sends():
-        loop(2, 3, lambda i: send_piece(i, i, 0))
-        loop(0, 1, lambda i: send_piece(i, i, 0, True))
-        loop(3, 4, lambda i: send_piece(i, i, 0))
-        loop(1, 2, lambda i: send_piece(i, i, 0, True))
+        gr_first[0].wait()
+        gr_first[1].wait()
 
     @pl.when(is_enc)
     def _():
         again = pltpu.make_async_copy(x_hbm, mem, load_sem.at[8])
         again.start()
-        for bs in (short, long):
+        for bs in (long, short):
             self_project(bs)
             attend_forward(bs, q_ref, k_ref, v_ref, own_lens, diagonal, None, obuf)
-            if bs == short:
+            if bs == long:
                 loads[2].wait()
             self_output(bs)
-            if bs == short:
-                loads[3].wait()
-                loads[4].wait()
-            ffn_forward(bs, grad)
+            ffn_forward(bs, grad, bs == long, bs == long)
             mem_copy[bs[0]].start()
         transposed_active(both)
         for k in range(4):
@@ -500,15 +508,11 @@
         for bs in (short, long):
             gm_copy[bs[0]].wait_recv()
             norm_backward(bs, u_ffn, up, ffn_gain, ffn_at + 1, grad, gr.at[0])
+            gr_first[bs[0]].start()
             if bs == short:
-                ffn_inner(bs, 0, slots)
+                ffn_inner(bs, 0, slots, False)
                 ffn_input(bs)
-        gr_copy[0].start()
-        ffn_inner(long, 0, 2)
-        wait_active()
-        first_sends()
-        ffn_inner(long, 2, slots)
-        ffn_input(long)
+        ffn_inner(long, 0, 1, True)
 
     @pl.when(is_dec)
     def _():
@@ -526,7 +530,7 @@
         loads[2].wait()
         self_output(both)
         wx_forward(2)
-        for cp in loads[3:]:
+        for cp in loads[5:]:
             cp.wait()
 
         def cross_query(at):
@@ -544,23 +548,47 @@
         for h in range(WX_CHUNKS):
             wx_near[h].wait()
             wx_far[h].wait()
-        for bs in (short, long):
+        for bs in (long, short):
             mem_copy[bs[0]].wait_recv()
             cross_forward(bs)
-            ffn_forward(bs, hw)
-            transposed_active(bs)
-            norm_backward(bs, u_ffn, up, ffn_gain, ffn_at + 1, grad, gr.at[0])
-            ffn_inner(bs, 0, slots)
-            ffn_input(bs)
-            cross_backward(bs)
-        gr_copy[0].start()
+        lt_copy[7].start()
+        ffn_forward(both, hw, True, True)
+        transposed_active(both)
         for k in range(4):
             lt_copy[k].start()
+        norm_backward(both, u_ffn, up, ffn_gain, ffn_at + 1, grad, gr.at[0])
+        gr_first[0].start()
+        gr_first[1].start()
+        ffn_inner(both, 0, slots, True)
+        ffn_input(both)
+        for bs in (short, long):
+            cross_backward(bs)
         transposed(6, both, hlow)
         lt_copy[6].start()
-        lt_copy[7].start()
-        wait_active()
-        first_sends()
+
+    wait_active()
+
+    def first_sends(k):
+        send_piece(2 + k, 2 + k, 0)
+        send_piece(k, k, 0, True)
+    loop(0, 2, first_sends)
+
+    @pl.when(is_enc)
+    def _():
+        ffn_inner(long, 1, slots, True)
+    lt_copy[6].wait()
+
+    def inner_sends(j):
+        remote(gr.at[1 + j], grp.at[1 + j], gr_send.at[1 + j], gr_recv.at[1 + j], core_id).wait()
+        send_piece(4 + j, 6, 1 + j)
+    loop(0, slots, inner_sends)
+
+    @pl.when(is_enc)
+    def _():
+        ffn_input(long)
+
+    @pl.when(is_dec)
+    def _():
         gr_copy[5].start()
         gr_copy[6].start()
         by_tiles(cross_input)
@@ -570,10 +598,6 @@
 
     rows_copy = pltpu.make_async_copy(xb, out_rows, io_sem.at[0])
     rows_copy.start()
-    lt_copy[6].wait()
-    for j in range(slots):
-        gr_copy[1 + j].wait()
-    loop(4, 8, lambda i: send_piece(i, 6, i - 3))
 
     norm_backward(both, u_self, grad, 2 * st, bias_at + 3, hw, gr.at[7])
     gr_copy[7].start()
@@ -581,9 +605,13 @@
     def self_up(at):
         obuf[:, at] = dot_nt(gr[7], wo[at, :]).astype(bf16)
     by_tiles(self_up)
-    loop(2, 3, lambda i: keep_piece(i, i, 0))
-    loop(0, 1, lambda i: keep_piece(i, i, 0, True))
-    attend_backward(both, q_ref, k_ref, v_ref, own_lens, diagonal)
+
+    def keep_and_attend(k, carry):
+        keep_piece(2 + k, 2 + k, 0)
+        keep_piece(k, k, 0, True)
+        attend_backward(both, q_ref, k_ref, v_ref, own_lens, diagonal, k * 3, k * 3 + 3)
+        return carry
+    lax.fori_loop(0, 2, keep_and_attend, 0)
     for j in range(3):
         gr_copy[8 + j].start()
 
@@ -591,10 +619,6 @@
     def _():
         gk_copy[0].start()
         gk_copy[1].start()
-    loop(3, 4, lambda i: keep_piece(i, i, 0))
-    loop(1, 2, lambda i: keep_piece(i, i, 0, True))
-    loop(2, 3, lambda i: pass_piece(i))
-    loop(0, 1, lambda i: pass_piece(i, True))
 
     def self_input(at):
         total = hw[:, at]
@@ -604,7 +628,7 @@
     by_tiles(self_input)
     grad_copy = pltpu.make_async_copy(hw, out_grad, io_sem.at[1])
     grad_copy.start()
-    loop(4, 5, lambda i: keep_piece(i, 6, i - 3))
+    loop(2, 4, pass_piece)
     for i in (4, 5, 7):
         lt_copy[i].wait()
 
@@ -613,32 +637,23 @@
         lt_copy[8].wait()
     for i in range(7, 11):
         gr_copy[i].wait()
-    first_left = 7 + st
-    rest = ((8, 5, 7), (9, 4, 8), (10, 4, 9), (11, 4, 10), (12, 7, 5), (13, first_left, 6))
-
     col_sum(gr.at[0], ffn_at)
     loop(0, slots, lambda j: col_sum(gr.at[1 + j], ffn_at - 4 + j))
     col_sum(gr.at[7], bias_at + 2)
     col_sum(gr.at[8], bias_at)
     col_sum(gr.at[10], bias_at + 1)
-    v_copy = [remote(vbuf.at[2 * k], vbuf.at[2 * k + 1], v_send.at[k], v_recv.at[k], dev)
+    own_half = pl.ds(pl.multiple_of(c * half, half), half)
+    other_half = pl.ds(pl.multiple_of((1 - c) * half, half), half)
+    v_copy = [remote(vg.at[:, other_half] if k == 0 else vbuf.at[2 * k], vbuf.at[2 * k + 1], v_send.at[k], v_recv.at[k], dev)
               for k, dev in enumerate((core_id, y_id, near_id, far_id, x_id))]
-    vbuf[0] = vg[...]
+    v_last = remote(vboth.at[:, :, own_half], vboth.at[:, :, own_half], v_send.at[5], v_recv.at[5], core_id)
+    vbuf[0] = vg[:, own_half]
 
     def v_next(k):
         v_copy[k].wait()
         vbuf[2 * k + 2] = vbuf[2 * k] + vbuf[2 * k + 1]
         v_copy[k + 1].start()
     v_copy[0].start()
-    for i, left, slot in rest[:2]:
-        send_piece(i, left, slot)
-    v_next(0)
-    for i, left, slot in rest[2:4]:
-        send_piece(i, left, slot)
-    loop(3, 4, lambda i: pass_piece(i))
-    loop(1, 2, lambda i: pass_piece(i, True))
-    loop(5, 6, lambda i: keep_piece(i, 6, i - 3))
-    loop(4, 5, lambda i: pass_piece(i))
 
     @pl.when(is_enc)
     def _():
@@ -646,30 +661,68 @@
         gk_copy[1].wait_recv()
         gr_copy[5].start()
         gr_copy[6].start()
-    loop(6, 7, lambda i: keep_piece(i, 6, i - 3))
+    v_next(0)
+
+    def attention_piece(k):
+        return 8 + k, 5 - (k + 3) // 4, 7 + k
+
+    def cross_piece(k):
+        return 12 + k // 2, 7 + st * (k // 2), 5 + k // 2, False, k % 2
+
+    def middle(k):
+        send_piece(*attention_piece(k))
+        keep_piece(4 + k, 6, 1 + k)
+
+        @pl.when(k > 0)
+        def _():
+            pass_piece(3 + k)
+    loop(0, 4, middle)
     for i in range(5, 7):
         gr_copy[i].wait()
-    for i, left, slot in rest[4:]:
-        send_piece(i, left, slot)
-    loop(5, 6, lambda i: pass_piece(i))
-    loop(7, 8, lambda i: keep_piece(i, 6, i - 3))
-    loop(6, 7, lambda i: pass_piece(i))
-    for k, (i, left, slot) in enumerate(rest):
-        keep_piece(i, left, slot)
-        pass_piece(i - 1)
-        if 2 <= k <= 4:
-            v_next(k - 1)
-    pass_piece(13)
+    loop(0, 4, lambda k: send_piece(*cross_piece(k)))
+    v_next(1)
+
+    def later(k):
+        keep_piece(*attention_piece(k))
+        pass_piece(7 + k)
+    loop(0, 4, later)
+    v_next(2)
+    loop(0, 2, lambda i: pass_piece(i, True))
+
+    def ends(k):
+        i, left, slot, z_first, h = cross_piece(k)
+        keep_piece(i, left, slot, z_first, h)
+
+        @pl.when(k == 0)
+        def _():
+            pass_piece(11)
+
+        @pl.when(k > 0)
+        def _():
+            pass_piece(12 + (k - 1) // 2, False, (k + 1) % 2)
+
+        @pl.when(k == 2)
+        def _():
+            v_next(3)
+    loop(0, 4, ends)
+    pass_piece(13, False, 1)
     v_copy[4].wait()
-    out_vec[...] = vbuf[8] + vbuf[9]
-
-    def finish(i, z_first=False):
-        third_copy(i, z_first).wait()
-        own_copy(i, z_first).wait()
+    vboth[st, :, own_half] = vbuf[8]
+    vboth[1 - st, :, own_half] = vbuf[9]
+    v_last.start()
+    v_last.wait()
+    vec_copy = pltpu.make_async_copy(vboth, out_vec, io_sem.at[2])
+    vec_copy.start()
+
+    def finish(i, z_first=False, h=None):
+        third_copy(i, z_first, h).wait()
+        own_copy(i, z_first, h).wait()
     loop(0, 2, lambda i: finish(i, True))
-    loop(2, PIECES, finish)
+    loop(2, 12, finish)
+    loop(0, 4, lambda k: finish(12 + k // 2, False, k % 2))
     rows_copy.wait()
     grad_copy.wait()
+    vec_copy.wait()
 
     @pl.when(is_enc)
     def _():
@@ -686,42 +739,46 @@
 
 
 def last_kernel(width, rows_in, grad_in, own, parts, vec_sum, rows_out, grad_out, *refs):
-    outs, (rows_buf, grad_buf, own_buf, part_buf, sums, in_sem, through_sem, out_sem) = refs[:8], refs[8:]
-    into = [pltpu.make_async_copy(rows_in, rows_buf, through_sem.at[0]), pltpu.make_async_copy(grad_in, grad_buf, through_sem.at[1])]
-    through = [pltpu.make_async_copy(rows_buf, rows_out, out_sem.at[PIECES]),
-               pltpu.make_async_copy(grad_buf, grad_out, out_sem.at[PIECES + 1])]
-    for cp in into:
+    outs, (vec_buf, rows_buf, grad_buf, own_buf, part_buf, sums, in_sem, through_sem, out_sem) = refs[:8], refs[8:]
+    group = PIECES // 2
+    loads = []
+    for g in range(2):
+        at = pl.ds(g * group, group)
+        loads.append((pltpu.make_async_copy(own.at[at], own_buf.at[at], in_sem.at[g, 0]),
+                      pltpu.make_async_copy(parts.at[at], part_buf.at[at], in_sem.at[g, 1])))
+    vec_load = pltpu.make_async_copy(vec_sum, vec_buf, through_sem.at[2])
+    into = [pltpu.make_async_copy(grad_in, grad_buf, through_sem.at[0]), pltpu.make_async_copy(rows_in, rows_buf, through_sem.at[1])]
+    for cp in (*loads[0], into[0], *loads[1], into[1], vec_load):
         cp.start()
-    loads = [(pltpu.make_async_copy(own.at[i], own_buf.at[i], in_sem.at[i, 0]),
-              pltpu.make_async_copy(parts.at[i], part_buf.at[i], in_sem.at[i, 1])) for i in range(PIECES)]
-    for pair in loads:
-        for cp in pair:
-            cp.start()
+    stores = []
+
+    def store(src, dst):
+        stores.append(pltpu.make_async_copy(src, dst, out_sem.at[len(stores)]))
+        stores[-1].start()
+    for g in range(2):
+        for cp in loads[g]:
+            cp.wait()
+        for i in range(g * group, (g + 1) * group):
+            sums[i] = own_buf[i].astype(f32) + part_buf[i].astype(f32)
+            if i < 4:
+                store(sums.at[i], outs[0].at[pl.ds(i * PIECE, PIECE), :])
+            elif i < 8:
+                store(sums.at[i], outs[1].at[:, pl.ds((i - 4) * width, width)])
+            elif i == 8:
+                store(sums.at[i], outs[4])
+            elif i == 11:
+                store(sums.at[pl.ds(9, 3)], outs[5])
+            elif i > 11:
+                store(sums.at[i], outs[i - 10])
+        into[g].wait()
+        store(rows_buf if g else grad_buf, rows_out if g else grad_out)
+    vec_load.wait()
     shift = lax.rem(width - lax.axis_index("dp") * PIECE, width)
-    turned = pltpu.roll(vec_sum[...], shift, 1)
-    outs[6][...] = turned[:5, :PIECE]
-    outs[7][...] = turned[5:29, :PIECE]
-    for cp, out in zip(into, through):
-        cp.wait()
-        out.start()
-    stores = []
-    for i in range(PIECES):
-        for cp in loads[i]:
-            cp.wait()
-        sums[i] = own_buf[i].astype(f32) + part_buf[i].astype(f32)
-        if i < 4:
-            target = outs[0].at[pl.ds(i * PIECE, PIECE), :]
-        elif i < 8:
-            target = outs[1].at[:, pl.ds((i - 4) * width, width)]
-        elif i == 8:
-            target = outs[4]
-        elif i < 12:
-            target = outs[5].at[i - 9]
-        else:
-            target = outs[i - 10]
-        stores.append(pltpu.make_async_copy(sums.at[i], target, out_sem.at[i]))
-        stores[-1].start()
-    for cp in stores + through:
+    for s, (g0, g1, b0, b1) in enumerate(((0, 2, 0, 10), (2, 5, 10, 24))):
+        turned = pltpu.roll(vec_buf[s], shift, 1)
+        outs[6][pl.ds(g0, g1 - g0), :] = turned[:g1 - g0, :PIECE]
+        outs[7][pl.ds(b0, b1 - b0), :] = turned[3:3 + b1 - b0, :PIECE]
+    for cp in stores:
         cp.wait()
 
 
@@ -741,10 +798,10 @@
             jax.ShapeDtypeStruct((ROWS, width), f32),
             jax.ShapeDtypeStruct((PIECES, PIECE, width), bf16),
             jax.ShapeDtypeStruct((PIECES, PIECE, width), bf16),
-            jax.ShapeDtypeStruct(small, f32),
+            jax.ShapeDtypeStruct((2, VEC_ROWS, width), f32),
         ],
         in_specs=[pl.BlockSpec(memory_space=pltpu.SMEM), vmem, vmem] + [any_space] * 8,
-        out_specs=[any_space] * 4 + [vmem],
+        out_specs=[any_space] * 5,
         scratch_shapes=[
             pltpu.VMEM(small, f32), pltpu.VMEM((2, hidden), f32),
             pltpu.VMEM(wproj.shape, bf16), pltpu.VMEM(wo.shape, bf16), pltpu.VMEM(wfirst.shape, bf16),
@@ -771,11 +828,12 @@
             pltpu.VMEM((PIECES, 2, 2, PIECE, width), bf16),
             pltpu.VMEM((PIECES, 2, PIECE, width), bf16),
             pltpu.VMEM((ROWS, width), bf16),
-            pltpu.VMEM(small, f32),
-            pltpu.VMEM((10,) + small, f32),
+            pltpu.VMEM((VEC_ROWS, width), f32),
+            pltpu.VMEM((10, VEC_ROWS, half), f32),
+            pltpu.VMEM((2, VEC_ROWS, width), f32),
             dma((9,)), dma((4 * WX_CHUNKS,)), dma((4 * WX_CHUNKS,)), dma((2,)), dma((2,)), dma((2,)), dma((2,)), dma((2,)), dma((2,)),
-            dma((9,)), dma((9,)), dma((11,)), dma((11,)),
-            dma((PIECES, 3)), dma((PIECES, 3)), dma((PIECES,)), dma((2,)), dma((5,)), dma((5,)),
+            dma((9,)), dma((9,)), dma((12,)), dma((12,)),
+            dma((PIECES, 6)), dma((PIECES, 6)), dma((PIECES, 2)), dma((3,)), dma((6,)), dma((6,)),
         ],
         compiler_params=pltpu.CompilerParams(collective_id=0, has_side_effects=True, vmem_limit_bytes=VMEM_LIMIT),
         name="step",
@@ -786,12 +844,12 @@
         functools.partial(last_kernel, width),
         out_shape=[jax.ShapeDtypeStruct((ROWS, width), bf16), jax.ShapeDtypeStruct((ROWS, width), f32)]
         + [jax.ShapeDtypeStruct(shape, f32) for shape in shapes],
-        in_specs=[any_space] * 4 + [vmem],
+        in_specs=[any_space] * 5,
         out_specs=[any_space] * 8 + [vmem] * 2,
         scratch_shapes=[
-            pltpu.VMEM((ROWS, width), bf16), pltpu.VMEM((ROWS, width), f32),
+            pltpu.VMEM((2, VEC_ROWS, width), f32), pltpu.VMEM((ROWS, width), bf16), pltpu.VMEM((ROWS, width), f32),
             pltpu.VMEM((PIECES, PIECE, width), bf16), pltpu.VMEM((PIECES, PIECE, width), bf16),
-            pltpu.VMEM((PIECES, PIECE, width), f32), dma((PIECES, 2)), dma((2,)), dma((PIECES + 2,)),
+            pltpu.VMEM((PIECES, PIECE, width), f32), dma((2, 2)), dma((3,)), dma((PIECES + 2,)),
         ],
         compiler_params=pltpu.CompilerParams(vmem_limit_bytes=VMEM_LIMIT),
         name="last",

time: 191 us -> 170 us (0.89)
  Pallas kernels: 190 us -> 169 us
    pallas_call x1, Pallas kernels: 184 us -> 165 us  [whole_step(): pl.pallas_call(functools.partial(step_kernel, width, hidden), out_shape=[...]
where the time goes in v4:
time: 170 us
  Pallas kernels  169 us (99%)
    pallas_call x1, Pallas kernels, whole_step(): pl.pallas_call(functools.partial(step_kernel, width, hidden), out_shape=[...  165 us
    pallas_call x1, Pallas kernels, whole_step(): pl.pallas_call(functools.partial(last_kernel, width), out_shape=[jax.Shap...  4.02 us

profile of v4, /device:TPU:0, one launch (start us, length us, event | category | flops | bytes accessed | tf_op | source)
XLA Modules:
  0.0 169.8 jit_solution(14008585983502162483)
XLA Ops:
  0.6 164.9 %step.1 = (bf16[384,768]{1,0:T(8,128)(2,1)}, f32[384,768]{1,0:T(8,128)}, bf16[14,48,768]{2,1,0:T(8,128)(2,1)}, bf16[14,48,768]{2,1,0:T(8,128)(2,1)}, f32[2,24,768]{2,1,0:T(8,128)}) custom-call(s32[2,1,2]{2,1,0:T(1,128)} %lengths.1, bf16[5,768]{1,0:T(8,128)(2,1)} %gains.1, bf16[24,768]{1,0:T(8,128)(2,1)} %biases.1, bf16[384,768]{1,0:T(8,128)(2,1)} %bitcast.21, ...), custom_call_target="tpu_custom_call" | custom-call | tf_op jit(solution)/shard_map/step/pallas_call | solution.py:794
  165.6 4.0 %last.1 = (bf16[384,768]{1,0:T(8,128)(2,1)}, f32[384,768]{1,0:T(8,128)}, f32[192,768]{1,0:T(8,128)}, f32[48,3072]{1,0:T(8,128)}, f32[48,768]{1,0:T(8,128)}, /*in...) custom-call(bf16[384,768]{1,0:T(8,128)(2,1)} %get-tuple-element.25.rows_in, ...), custom_call_target="tpu_custom_call" | custom-call | tf_op jit(solution)/shard_map/last/pallas_call | solution.py:843

commit v5 on v4

--- a/solution.py
+++ b/solution.py
@@ -15,7 +15,6 @@
 PIECES = 14
 VEC_ROWS = 24
 SEND_SLOTS = 8
-WX_CHUNKS = 4
 MESH = pl.DeviceIdType.MESH
 bf16, f32 = jnp.bfloat16, jnp.float32
 VMEM_LIMIT = 64 << 20
@@ -43,7 +42,7 @@
     out_rows, out_grad, out_own, out_part, out_vec,
     vec, bias_in, wproj, wo, wfirst, wsecond, win, wout, wx,
     xb, up, mem, obuf, hlow, dg, kv, acc, grad, hw, u_self, u_cross, u_ffn, gr, grp, lt, ltp, one_send, one_recv, two_recv, gmem, vg, vbuf, vboth,
-    load_sem, wx_send, wx_recv, mem_send, mem_recv, gm_send, gm_recv, gk_send, gk_recv, lt_send, lt_recv, gr_send, gr_recv,
+    load_sem, wx_send, wx_recv, mem_send, mem_recv, gm_send, gm_recv, gv_send, gv_recv, lt_send, lt_recv, gr_send, gr_recv,
     sem_send, sem_recv, own_sem, io_sem, v_send, v_recv,
 ):
     st = lax.axis_index("stream")
@@ -63,6 +62,7 @@
         return {"dp": other * 4 + y * 2 + c}
     near_id = z_id(zh * 2 + 1 - zl)
     far_id = z_id((1 - zh) * 2 + zl)
+    over_id = {"stream": 1 - st, **far_id}
 
     def remote(src, dst, ss, rs, dev):
         return pltpu.make_async_remote_copy(
@@ -79,7 +79,7 @@
     loads[1].start()
 
     barrier = pltpu.get_barrier_semaphore()
-    peers = [core_id, y_id, x_id, near_id, far_id]
+    peers = [core_id, y_id, x_id, near_id, far_id, over_id]
     for p in peers:
         pl.semaphore_signal(barrier, inc=1, device_id=p, device_id_type=MESH)
 
@@ -91,34 +91,40 @@
         for s in range(2):
             bias_in[pl.ds(s, 1), pl.ds(i * width, width)] = vec[pl.ds(9 + 14 * s + i, 1), :]
     vg[...] = jnp.zeros_like(vg)
-    pl.semaphore_wait(barrier, len(peers))
-
     half = width // 2
-    chunk = half // WX_CHUNKS
-    quarter = y * 2 + c
-    far = (1 - y) * 2 + c
+    chunks = width // 4 // PIECE
+
+    def wx_block(yy, zz, cc, h):
+        return wx.at[yy, pl.ds((zz * 2 + cc) * chunks * PIECE + h * PIECE, PIECE)]
+
+    def wx_copy(src, dst, k, dev):
+        return remote(src, dst, wx_send.at[k], wx_recv.at[k], dev)
 
     def wx_from(source, h):
-        return remote(source.at[pl.ds(c * half + h * chunk, chunk)], wx.at[quarter, pl.ds(h * chunk, chunk)],
-                      wx_send.at[h], wx_recv.at[h], x_id)
-
-    def wx_pass(at, h, sem, dev):
-        ref = wx.at[at, pl.ds(h * chunk, chunk)]
-        return remote(ref, ref, wx_send.at[sem * WX_CHUNKS + h], wx_recv.at[sem * WX_CHUNKS + h], dev)
-    wx_first = [wx_from(wfirst_hbm, h) for h in range(WX_CHUNKS)]
-    wx_y = [wx_pass(quarter, h, 1, y_id) for h in range(WX_CHUNKS)]
-    wx_near = [wx_pass(quarter, h, 2, core_id) for h in range(WX_CHUNKS)]
-    wx_far = [wx_pass(far, h, 3, core_id) for h in range(WX_CHUNKS)]
-
-    @pl.when(is_enc & (y == 0))
-    def _():
-        for h in range(WX_CHUNKS):
-            wx_first[h].start()
-
-    @pl.when(is_enc & (y == 1))
-    def _():
-        for h in range(WX_CHUNKS):
-            wx_from(wsecond_hbm, h).start()
+        return wx_copy(source.at[pl.ds((zl * 2 + c) * chunks * PIECE + h * PIECE, PIECE)], wx_block(y, zl, c, h), h, x_id)
+    wx_in = [wx_from(wfirst_hbm, h) for h in range(chunks)]
+    wx_y = [wx_copy(wx_block(y, zl, c, h), wx_block(y, zl, c, h), chunks + h, y_id) for h in range(chunks)]
+    wx_z = [wx_copy(wx_block(y, zl, c, h), wx_block(y, zl, c, h), 2 * chunks + h, near_id) for h in range(chunks)]
+    wx_on = [wx_copy(wx_block(1 - y, zl, c, h), wx_block(1 - y, zl, c, h), 3 * chunks + h, near_id) if h < chunks // 2 else
+             wx_copy(wx_block(y, 1 - zl, c, h), wx_block(y, 1 - zl, c, h), 3 * chunks + h, y_id) for h in range(chunks)]
+
+    def wx_whole(yy, zz):
+        return wx.at[yy, pl.ds((zz * 2 + c) * chunks * PIECE, chunks * PIECE)]
+    wx_core = [wx_copy(wx_whole(yy, zz), wx_whole(yy, zz), 4 * chunks + k, core_id)
+               for k, (yy, zz) in enumerate(((y, zl), (1 - y, zl), (y, 1 - zl), (1 - y, 1 - zl)))]
+
+    def wx_start():
+        pl.semaphore_wait(barrier, len(peers))
+
+        @pl.when(is_enc & (y == 0))
+        def _():
+            for h in range(chunks):
+                wx_in[h].start()
+
+        @pl.when(is_enc & (y == 1))
+        def _():
+            for h in range(chunks):
+                wx_from(wsecond_hbm, h).start()
     loads[0].wait()
     loads[1].wait()
     for cp in loads[2:]:
@@ -142,8 +148,7 @@
         return pl.ds(*span(bs))
     mem_copy = [remote(xb.at[at_rows((b,))], mem.at[at_rows((b,))], mem_send.at[b], mem_recv.at[b], x_id) for b in range(2)]
     gm_copy = [remote(gmem.at[at_rows((b,))], up.at[at_rows((b,))], gm_send.at[b], gm_recv.at[b], x_id) for b in range(2)]
-    gk_copy = [remote(kv.at[0], gr.at[6], gk_send.at[0], gk_recv.at[0], x_id),
-               remote(kv.at[1], gr.at[5], gk_send.at[1], gk_recv.at[1], x_id)]
+    gv_copy = remote(kv.at[1], gr.at[5], gv_send, gv_recv, x_id)
 
     gr_first = [remote(gr.at[0, at_rows((b,))], grp.at[0, at_rows((b,))], gr_send.at[11 * b], gr_recv.at[11 * b], core_id)
                 for b in range(2)]
@@ -163,13 +168,16 @@
         r0, n = span(bs)
         lt[i, :, :, :, :, :, pl.ds(r0, n)] = ref[pl.ds(r0, n), :].T.reshape(2, 2, 2, 2, PIECE, n)
 
+    def transposed_slot(bs, j):
+        r0, n = span(bs)
+        turned = gr[1 + j, pl.ds(r0, n), :].T.reshape(2, 2, 4, PIECE, n)
+        for k in range(4):
+            lt[k, j // 2, j % 2, :, :, :, pl.ds(r0, n)] = turned[:, :, k]
+
     def transposed_active(bs):
-        r0, n = span(bs)
 
         def step(j, carry):
-            turned = gr[1 + j, pl.ds(r0, n), :].T.reshape(2, 2, 4, PIECE, n)
-            for k in range(4):
-                lt[k, j // 2, j % 2, :, :, :, pl.ds(r0, n)] = turned[:, :, k]
+            transposed_slot(bs, j)
             return carry
         lax.fori_loop(0, slots, step, 0)
 
@@ -236,7 +244,7 @@
             return carry
         lax.fori_loop(lo, width // (2 * HDIM * pairs) if hi is None else hi, step, 0)
 
-    def attend_forward(bs, q_ref, k_ref, v_ref, lengths_at, diagonal, bias_row, out_ref):
+    def attend_forward(bs, q_ref, k_ref, v_ref, lengths_at, diagonal, bias_row, out_ref, lo=0, hi=None):
         def body(units):
             work = []
             for b, at in units:
@@ -254,7 +262,7 @@
                 if bias_row is not None:
                     att = att + vec[pl.ds(bias_row, 1), at]
                 out_ref[pl.ds(r0, n), at] = att.astype(bf16)
-        head_loop(bs, body)
+        head_loop(bs, body, lo, hi)
 
     def attend_backward(bs, q_ref, k_ref, v_ref, lengths_at, diagonal, lo=0, hi=None):
         scale = HDIM ** -0.5
@@ -316,7 +324,7 @@
         by_tiles(tile)
         norm_forward(bs, xb, u_self, bias_at + 2, 2 * st, bias_at + 3, hlow, grad)
 
-    def ffn_forward(bs, residual, wait_in, wait_out):
+    def ffn_forward(bs, residual, wait_in, wait_out, turn=False):
         r0, n = span(bs)
         rows = pl.ds(r0, n)
 
@@ -342,6 +350,9 @@
         if wait_out:
             loads[4].wait()
         by_tiles(ffn_out)
+        if turn:
+            for j in range(slots):
+                transposed_slot(bs, j)
         norm_forward(bs, residual, u_ffn, ffn_at, ffn_gain, ffn_at + 1, xb, None)
 
     def ffn_inner(bs, lo, hi, last):
@@ -375,7 +386,7 @@
         def memory_kv(which, carry):
             for t in range(tiles):
                 at = pl.ds(t * 256, 256)
-                value = dot_nn(mem[rows, pl.ds(0, half)], wx[2 * which, :, at]) + dot_nn(mem[rows, pl.ds(half, half)], wx[2 * which + 1, :, at])
+                value = dot_nn(mem[rows, :], wx[which, :, at])
                 kv[which, rows, at] = value.astype(bf16)
             return carry
         lax.fori_loop(0, 2, memory_kv, 0)
@@ -398,7 +409,7 @@
 
         def memory_half(h, carry):
             at = cols(h, half)
-            gmem[rows, at] = (dot_nt(kv[0, rows, :], wx[h]) + dot_nt(kv[1, rows, :], wx[2 + h])).astype(bf16)
+            gmem[rows, at] = (dot_nt(kv[0, rows, :], wx[0, at, :]) + dot_nt(kv[1, rows, :], wx[1, at, :])).astype(bf16)
             return carry
         lax.fori_loop(0, 2, memory_half, 0)
         gm_copy[bs[0]].start()
@@ -409,9 +420,11 @@
     def lanes_of(h):
         return pl.ds(0, width) if h is None else cols(h, half)
 
+    def unit(i, h):
+        return i if h is None else 15 + 2 * (i - 12) + h
+
     def sems(i, stage, h):
-        k = 2 * stage + (0 if h is None else h)
-        return sem_send.at[i, k], sem_recv.at[i, k]
+        return sem_send.at[unit(i, h), stage], sem_recv.at[unit(i, h), stage]
 
     def first_copy(i, z_first, h):
         at = lanes_of(h)
@@ -430,7 +443,7 @@
 
     def own_copy(i, z_first, h):
         at = lanes_of(h)
-        return pltpu.make_async_copy(two_recv.at[i, y if z_first else zh, :, at], out_own.at[i, :, at], own_sem.at[i, 0 if h is None else h])
+        return pltpu.make_async_copy(two_recv.at[i, y if z_first else zh, :, at], out_own.at[i, :, at], own_sem.at[unit(i, h)])
 
     def product(left, slot, z_first, other, at):
         if z_first:
@@ -463,14 +476,23 @@
         piece_tiles(h, tile)
         second_copy(i, z_first, h).start()
 
-    def pass_piece(i, z_first=False, h=None):
+    def merge_piece(i, z_first=False, h=None):
         second_copy(i, z_first, h).wait()
         at = lanes_of(h)
         for k in range(2):
             mine = one_recv[i, zh, k, :, at] if z_first else one_recv[i, k, zl, :, at]
             two_recv[i, k, :, at] = (two_recv[i, k, :, at].astype(f32) + mine.astype(f32)).astype(bf16)
+
+    def pass_piece(i, z_first=False, h=None):
+        merge_piece(i, z_first, h)
         third_copy(i, z_first, h).start()
         own_copy(i, z_first, h).start()
+
+    extra = PIECES
+    extra_part = remote(two_recv.at[extra, 1 - zh], out_part.at[13], sem_send.at[extra, 2], sem_recv.at[13, 2], over_id)
+    extra_own = remote(two_recv.at[extra, zh], out_own.at[13], sem_send.at[13, 0], sem_recv.at[13, 0], x_id)
+    extra_left = remote(lt.at[0, :, :, :, 1 - c], ltp.at[0], lt_send.at[0], lt_recv.at[0], core_id)
+    extra_right = remote(gr.at[0], grp.at[0], gr_send.at[0], gr_recv.at[0], core_id)
 
     def loop(lo, hi, fn):
         def step(i, carry):
@@ -490,6 +512,8 @@
         again.start()
         for bs in (long, short):
             self_project(bs)
+            if bs == long:
+                wx_start()
             attend_forward(bs, q_ref, k_ref, v_ref, own_lens, diagonal, None, obuf)
             if bs == long:
                 loads[2].wait()
@@ -517,43 +541,58 @@
     @pl.when(is_dec)
     def _():
         self_project(both)
+        wx_start()
         transposed(4, both, xb)
         lt_copy[4].start()
 
         def wx_forward(h):
-            wx_first[h].wait_recv()
+            wx_in[h].wait_recv()
             wx_y[h].start()
-            wx_near[h].start()
+            wx_z[h].start()
+        attend_forward(both, q_ref, k_ref, v_ref, own_lens, diagonal, None, obuf, 0, 3)
         wx_forward(0)
-        attend_forward(both, q_ref, k_ref, v_ref, own_lens, diagonal, None, obuf)
+        attend_forward(both, q_ref, k_ref, v_ref, own_lens, diagonal, None, obuf, 3, 6)
         wx_forward(1)
         loads[2].wait()
         self_output(both)
         wx_forward(2)
-        for cp in loads[5:]:
-            cp.wait()
+        wx_y[0].wait()
+        wx_on[0].start()
+        loads[5].wait()
 
         def cross_query(at):
             gr[6, :, at] = (dot_nn(hlow[...], wfirst[:, at]) + vec[pl.ds(19, 1), at]).astype(bf16)
         by_tiles(cross_query)
         wx_forward(3)
+        wx_core[0].start()
         transposed(5, both, obuf)
         lt_copy[5].start()
         transposed(8, both, hlow)
         lt_copy[8].start()
+        loads[6].wait()
         cot_load.wait()
-        for h in range(WX_CHUNKS):
-            wx_y[h].wait()
-            wx_far[h].start()
-        for h in range(WX_CHUNKS):
-            wx_near[h].wait()
-            wx_far[h].wait()
+        wx_y[1].wait()
+        wx_on[1].start()
+        wx_z[0].wait()
+        wx_z[1].wait()
+        wx_z[2].wait()
+        wx_on[2].start()
+        wx_y[2].wait()
+        wx_z[3].wait()
+        wx_on[3].start()
+        wx_y[3].wait()
+        wx_core[1].start()
+        wx_core[2].start()
+        for h in range(chunks):
+            wx_on[h].wait()
+        wx_core[3].start()
+        for k in range(4):
+            wx_core[k].wait()
         for bs in (long, short):
             mem_copy[bs[0]].wait_recv()
             cross_forward(bs)
         lt_copy[7].start()
-        ffn_forward(both, hw, True, True)
-        transposed_active(both)
+        ffn_forward(both, hw, True, True, True)
         for k in range(4):
             lt_copy[k].start()
         norm_backward(both, u_ffn, up, ffn_gain, ffn_at + 1, grad, gr.at[0])
@@ -617,8 +656,7 @@
 
     @pl.when(is_dec)
     def _():
-        gk_copy[0].start()
-        gk_copy[1].start()
+        gv_copy.start()
 
     def self_input(at):
         total = hw[:, at]
@@ -649,18 +687,18 @@
     v_last = remote(vboth.at[:, :, own_half], vboth.at[:, :, own_half], v_send.at[5], v_recv.at[5], core_id)
     vbuf[0] = vg[:, own_half]
 
+    @pl.when(is_dec)
+    def _():
+        transposed(0, both, mem)
+        extra_left.start()
+        gr[0] = kv[0]
+        extra_right.start()
+
     def v_next(k):
         v_copy[k].wait()
         vbuf[2 * k + 2] = vbuf[2 * k] + vbuf[2 * k + 1]
         v_copy[k + 1].start()
     v_copy[0].start()
-
-    @pl.when(is_enc)
-    def _():
-        gk_copy[0].wait_recv()
-        gk_copy[1].wait_recv()
-        gr_copy[5].start()
-        gr_copy[6].start()
     v_next(0)
 
     def attention_piece(k):
@@ -677,15 +715,34 @@
         def _():
             pass_piece(3 + k)
     loop(0, 4, middle)
-    for i in range(5, 7):
-        gr_copy[i].wait()
-    loop(0, 4, lambda k: send_piece(*cross_piece(k)))
+
+    @pl.when(is_enc)
+    def _():
+        gv_copy.wait_recv()
+        gr_copy[5].start()
+
+    @pl.when(is_dec)
+    def _():
+        extra_left.wait()
+        extra_right.wait()
+        send_piece(extra, 0, 0)
+        gr_copy[6].wait()
     v_next(1)
+    cross_units = 2 + 2 * st
 
     def later(k):
         keep_piece(*attention_piece(k))
+
+        @pl.when(k == 0)
+        def _():
+            gr_copy[5].wait()
+            loop(0, cross_units, lambda k: send_piece(*cross_piece(k)))
         pass_piece(7 + k)
     loop(0, 4, later)
+
+    @pl.when(is_dec)
+    def _():
+        keep_piece(extra, 0, 0)
     v_next(2)
     loop(0, 2, lambda i: pass_piece(i, True))
 
@@ -701,11 +758,17 @@
         def _():
             pass_piece(12 + (k - 1) // 2, False, (k + 1) % 2)
 
-        @pl.when(k == 2)
+        @pl.when(k == 1)
         def _():
             v_next(3)
-    loop(0, 4, ends)
-    pass_piece(13, False, 1)
+
+        @pl.when(is_dec & (k == 1))
+        def _():
+            merge_piece(extra)
+            extra_part.start()
+            extra_own.start()
+    loop(0, cross_units, ends)
+    pass_piece(12 + st, False, 1)
     v_copy[4].wait()
     vboth[st, :, own_half] = vbuf[8]
     vboth[1 - st, :, own_half] = vbuf[9]
@@ -719,23 +782,27 @@
         own_copy(i, z_first, h).wait()
     loop(0, 2, lambda i: finish(i, True))
     loop(2, 12, finish)
-    loop(0, 4, lambda k: finish(12 + k // 2, False, k % 2))
+    loop(0, cross_units, lambda k: finish(12 + k // 2, False, k % 2))
     rows_copy.wait()
     grad_copy.wait()
     vec_copy.wait()
 
     @pl.when(is_enc)
     def _():
-        for h in range(WX_CHUNKS):
-            wx_first[h].wait_send()
+        for h in range(chunks):
+            wx_in[h].wait_send()
         for h in range(2):
             mem_copy[h].wait_send()
+        extra_part.wait_recv()
+        extra_own.wait_recv()
 
     @pl.when(is_dec)
     def _():
         for h in range(2):
             gm_copy[h].wait_send()
-            gk_copy[h].wait_send()
+        gv_copy.wait_send()
+        extra_part.wait_send()
+        extra_own.wait_send()
 
 
 def last_kernel(width, rows_in, grad_in, own, parts, vec_sum, rows_out, grad_out, *refs):
@@ -806,7 +873,7 @@
             pltpu.VMEM(small, f32), pltpu.VMEM((2, hidden), f32),
             pltpu.VMEM(wproj.shape, bf16), pltpu.VMEM(wo.shape, bf16), pltpu.VMEM(wfirst.shape, bf16),
             pltpu.VMEM(wsecond.shape, bf16), pltpu.VMEM(win.shape, bf16), pltpu.VMEM(wout.shape, bf16),
-            pltpu.VMEM((4, half, width), bf16),
+            pltpu.VMEM((2, width, width), bf16),
             pltpu.VMEM((ROWS, width), bf16),
             pltpu.VMEM((ROWS, width), bf16),
             pltpu.VMEM((ROWS, width), bf16),
@@ -825,15 +892,15 @@
             pltpu.VMEM((9, 2, 2, 2, 2, PIECE, ROWS), bf16),
             pltpu.VMEM((9, 2, 2, 2, PIECE, ROWS), bf16),
             pltpu.VMEM((SEND_SLOTS, 2, 2, PIECE, width), bf16),
-            pltpu.VMEM((PIECES, 2, 2, PIECE, width), bf16),
-            pltpu.VMEM((PIECES, 2, PIECE, width), bf16),
+            pltpu.VMEM((PIECES + 1, 2, 2, PIECE, width), bf16),
+            pltpu.VMEM((PIECES + 1, 2, PIECE, width), bf16),
             pltpu.VMEM((ROWS, width), bf16),
             pltpu.VMEM((VEC_ROWS, width), f32),
             pltpu.VMEM((10, VEC_ROWS, half), f32),
             pltpu.VMEM((2, VEC_ROWS, width), f32),
-            dma((9,)), dma((4 * WX_CHUNKS,)), dma((4 * WX_CHUNKS,)), dma((2,)), dma((2,)), dma((2,)), dma((2,)), dma((2,)), dma((2,)),
+            dma((9,)), dma((20,)), dma((20,)), dma((2,)), dma((2,)), dma((2,)), dma((2,)), dma, dma,
             dma((9,)), dma((9,)), dma((12,)), dma((12,)),
-            dma((PIECES, 6)), dma((PIECES, 6)), dma((PIECES, 2)), dma((3,)), dma((6,)), dma((6,)),
+            dma((19, 3)), dma((19, 3)), dma((19,)), dma((3,)), dma((6,)), dma((6,)),
         ],
         compiler_params=pltpu.CompilerParams(collective_id=0, has_side_effects=True, vmem_limit_bytes=VMEM_LIMIT),
         name="step",

time: 170 us -> 163 us (0.959)
  Pallas kernels: 169 us -> 162 us
    pallas_call x1, Pallas kernels: 165 us -> 158 us  [whole_step(): pl.pallas_call(functools.partial(step_kernel, width, hidden), out_shape=[...]
where the time goes in v5:
time: 163 us
  Pallas kernels  162 us (99%)
    pallas_call x1, Pallas kernels, whole_step(): pl.pallas_call(functools.partial(step_kernel, width, hidden), out_shape=[...  158 us
    pallas_call x1, Pallas kernels, whole_step(): pl.pallas_call(functools.partial(last_kernel, width), out_shape=[jax.Shap...  4.02 us

profile of v5, /device:TPU:0, one launch (start us, length us, event | category | flops | bytes accessed | tf_op | source)
XLA Modules:
  0.0 162.6 jit_solution(14625152607792403070)
XLA Ops:
  0.6 157.7 %step.1 = (bf16[384,768]{1,0:T(8,128)(2,1)}, f32[384,768]{1,0:T(8,128)}, bf16[14,48,768]{2,1,0:T(8,128)(2,1)}, bf16[14,48,768]{2,1,0:T(8,128)(2,1)}, f32[2,24,768]{2,1,0:T(8,128)}) custom-call(s32[2,1,2]{2,1,0:T(1,128)} %lengths.1, bf16[5,768]{1,0:T(8,128)(2,1)} %gains.1, bf16[24,768]{1,0:T(8,128)(2,1)} %biases.1, bf16[384,768]{1,0:T(8,128)(2,1)} %bitcast.21, ...), custom_call_target="tpu_custom_call" | custom-call | tf_op jit(solution)/shard_map/step/pallas_call | solution.py:861
  158.4 4.0 %last.1 = (bf16[384,768]{1,0:T(8,128)(2,1)}, f32[384,768]{1,0:T(8,128)}, f32[192,768]{1,0:T(8,128)}, f32[48,3072]{1,0:T(8,128)}, f32[48,768]{1,0:T(8,128)}, /*in...) custom-call(bf16[384,768]{1,0:T(8,128)(2,1)} %get-tuple-element.25.rows_in, ...), custom_call_target="tpu_custom_call" | custom-call | tf_op jit(solution)/shard_map/last/pallas_call | solution.py:910

commit v6 on v5

--- a/solution.py
+++ b/solution.py
@@ -71,12 +71,15 @@
     loads = [
         pltpu.make_async_copy(src, dst, load_sem.at[i])
         for i, (src, dst) in enumerate((
-            (x_hbm, xb), (wproj_hbm, wproj), (wo_hbm, wo), (win_hbm, win), (wout_hbm, wout),
+            (x_hbm, xb), (x_hbm, mem), (wo_hbm, wo), (win_hbm, win), (wout_hbm, wout),
             (wfirst_hbm, wfirst), (wsecond_hbm, wsecond)))
     ]
     cot_load = pltpu.make_async_copy(cot_hbm, up, load_sem.at[7])
+    def proj_load(which):
+        return pltpu.make_async_copy(wproj_hbm.at[which], wproj.at[which], load_sem.at[9 + which])
     loads[0].start()
-    loads[1].start()
+    for which in range(3):
+        proj_load(which).start()
 
     barrier = pltpu.get_barrier_semaphore()
     peers = [core_id, y_id, x_id, near_id, far_id, over_id]
@@ -125,10 +128,9 @@
         def _():
             for h in range(chunks):
                 wx_from(wsecond_hbm, h).start()
-    loads[0].wait()
-    loads[1].wait()
     for cp in loads[2:]:
         cp.start()
+    loads[0].wait()
 
     @pl.when(is_dec)
     def _():
@@ -147,7 +149,10 @@
     def at_rows(bs):
         return pl.ds(*span(bs))
     mem_copy = [remote(xb.at[at_rows((b,))], mem.at[at_rows((b,))], mem_send.at[b], mem_recv.at[b], x_id) for b in range(2)]
-    gm_copy = [remote(gmem.at[at_rows((b,))], up.at[at_rows((b,))], gm_send.at[b], gm_recv.at[b], x_id) for b in range(2)]
+
+    def gm_part(b, h):
+        at = cols(h, half)
+        return remote(gmem.at[at_rows((b,)), at], up.at[at_rows((b,)), at], gm_send.at[2 * b + h], gm_recv.at[2 * b + h], x_id)
     gv_copy = remote(kv.at[1], gr.at[5], gv_send, gv_recv, x_id)
 
     gr_first = [remote(gr.at[0, at_rows((b,))], grp.at[0, at_rows((b,))], gr_send.at[11 * b], gr_recv.at[11 * b], core_id)
@@ -304,10 +309,12 @@
         for t in range(tiles):
             fn(pl.ds(t * 256, 256))
 
-    def self_project(bs):
+    def self_project(bs, wait):
         rows = at_rows(bs)
 
         def project(which, carry):
+            if wait:
+                proj_load(which).wait()
             for t in range(tiles):
                 at = pl.ds(t * 256, 256)
                 value = dot_nn(xb[rows, :], wproj[which, :, at])
@@ -398,21 +405,23 @@
         norm_forward(bs, grad, u_cross, 21, 3, 22, hlow, hw)
         transposed(7, bs, obuf)
 
+    def cross_branch():
+        norm_backward(both, u_cross, grad, 3, 22, hw, gr.at[5])
+
+        def cross_up(at):
+            obuf[:, at] = dot_nt(gr[5], wsecond[at, :]).astype(bf16)
+        by_tiles(cross_up)
+
     def cross_backward(bs):
         rows = at_rows(bs)
-        norm_backward(bs, u_cross, grad, 3, 22, hw, gr.at[5])
-
-        def cross_up(at):
-            obuf[rows, at] = dot_nt(gr[5, rows, :], wsecond[at, :]).astype(bf16)
-        by_tiles(cross_up)
         attend_backward(bs, gr.at[6], kv.at[0], kv.at[1], lens[:2], 4096)
 
         def memory_half(h, carry):
             at = cols(h, half)
             gmem[rows, at] = (dot_nt(kv[0, rows, :], wx[0, at, :]) + dot_nt(kv[1, rows, :], wx[1, at, :])).astype(bf16)
+            gm_part(bs[0], h).start()
             return carry
         lax.fori_loop(0, 2, memory_half, 0)
-        gm_copy[bs[0]].start()
 
     def cross_input(at):
         grad[:, at] = hw[:, at] + dot_nt(gr[6], wfirst[at, :])
@@ -508,10 +517,10 @@
 
     @pl.when(is_enc)
     def _():
-        again = pltpu.make_async_copy(x_hbm, mem, load_sem.at[8])
+        again = loads[1]
         again.start()
         for bs in (long, short):
-            self_project(bs)
+            self_project(bs, bs == long)
             if bs == long:
                 wx_start()
             attend_forward(bs, q_ref, k_ref, v_ref, own_lens, diagonal, None, obuf)
@@ -530,7 +539,8 @@
         loads[5].wait()
         loads[6].wait()
         for bs in (short, long):
-            gm_copy[bs[0]].wait_recv()
+            for h in range(2):
+                gm_part(bs[0], h).wait_recv()
             norm_backward(bs, u_ffn, up, ffn_gain, ffn_at + 1, grad, gr.at[0])
             gr_first[bs[0]].start()
             if bs == short:
@@ -540,7 +550,7 @@
 
     @pl.when(is_dec)
     def _():
-        self_project(both)
+        self_project(both, True)
         wx_start()
         transposed(4, both, xb)
         lt_copy[4].start()
@@ -600,6 +610,7 @@
         gr_first[1].start()
         ffn_inner(both, 0, slots, True)
         ffn_input(both)
+        cross_branch()
         for bs in (short, long):
             cross_backward(bs)
         transposed(6, both, hlow)
@@ -799,7 +810,8 @@
     @pl.when(is_dec)
     def _():
         for h in range(2):
-            gm_copy[h].wait_send()
+            for b in range(2):
+                gm_part(b, h).wait_send()
         gv_copy.wait_send()
         extra_part.wait_send()
         extra_own.wait_send()
@@ -898,7 +910,7 @@
             pltpu.VMEM((VEC_ROWS, width), f32),
             pltpu.VMEM((10, VEC_ROWS, half), f32),
             pltpu.VMEM((2, VEC_ROWS, width), f32),
-            dma((9,)), dma((20,)), dma((20,)), dma((2,)), dma((2,)), dma((2,)), dma((2,)), dma, dma,
+            dma((12,)), dma((20,)), dma((20,)), dma((2,)), dma((2,)), dma((4,)), dma((4,)), dma, dma,
             dma((9,)), dma((9,)), dma((12,)), dma((12,)),
             dma((19, 3)), dma((19, 3)), dma((19,)), dma((3,)), dma((6,)), dma((6,)),
         ],

time: 163 us -> 162 us (level)
  no operation moved by 1% of the time
where the time goes in v6:
time: 162 us
  Pallas kernels  161 us (99%)
    pallas_call x1, Pallas kernels, whole_step(): pl.pallas_call(functools.partial(step_kernel, width, hidden), out_shape=[...  157 us
    pallas_call x1, Pallas kernels, whole_step(): pl.pallas_call(functools.partial(last_kernel, width), out_shape=[jax.Shap...  4.02 us

profile of v6, /device:TPU:0, one launch (start us, length us, event | category | flops | bytes accessed | tf_op | source)
XLA Modules:
  0.0 161.8 jit_solution(1515650594066762264)
XLA Ops:
  0.6 157.0 %step.1 = (bf16[384,768]{1,0:T(8,128)(2,1)}, f32[384,768]{1,0:T(8,128)}, bf16[14,48,768]{2,1,0:T(8,128)(2,1)}, bf16[14,48,768]{2,1,0:T(8,128)(2,1)}, f32[2,24,768]{2,1,0:T(8,128)}) custom-call(s32[2,1,2]{2,1,0:T(1,128)} %lengths.1, bf16[5,768]{1,0:T(8,128)(2,1)} %gains.1, bf16[24,768]{1,0:T(8,128)(2,1)} %biases.1, bf16[384,768]{1,0:T(8,128)(2,1)} %bitcast.21, ...), custom_call_target="tpu_custom_call" | custom-call | tf_op jit(solution)/shard_map/step/pallas_call | solution.py:873
  157.6 4.0 %last.1 = (bf16[384,768]{1,0:T(8,128)(2,1)}, f32[384,768]{1,0:T(8,128)}, f32[192,768]{1,0:T(8,128)}, f32[48,3072]{1,0:T(8,128)}, f32[48,768]{1,0:T(8,128)}, /*in...) custom-call(bf16[384,768]{1,0:T(8,128)(2,1)} %get-tuple-element.25.rows_in, ...), custom_call_target="tpu_custom_call" | custom-call | tf_op jit(solution)/shard_map/last/pallas_call | solution.py:922

commit v7 on v6

--- a/solution.py
+++ b/solution.py
@@ -205,7 +205,7 @@
             out_low[rows, :] = h.astype(bf16)
         row_loop(bs, 32, body, 4)
 
-    def norm_backward(bs, sum_ref, source, gain, shift, out_wide, slot):
+    def norm_backward(bs, sum_ref, source, gain, shift, out_wide, slot, again=None):
         r0, n = span(bs)
 
         def step(i, carry):
@@ -220,6 +220,8 @@
             gu = (t - jnp.mean(t, axis=-1, keepdims=True) - uhat * jnp.mean(t * uhat, axis=-1, keepdims=True)) * inv
             out_wide[rows, :] = gu
             slot[rows, :] = gu.astype(bf16)
+            if again is not None:
+                again[rows, :] = gu.astype(bf16)
             return (carry[0] + jnp.sum((r * uhat).reshape(4, 8, width), axis=0),
                     carry[1] + jnp.sum(r.reshape(4, 8, width), axis=0))
         zero = jnp.zeros((8, width), f32)
@@ -285,6 +287,7 @@
                     ups.append(dot_nt(jnp.where(lanes, go2, zero), v2))
             probs = [softmax(s) for s in scores]
             gs = [(p * (gp - jnp.sum(p * gp, axis=-1, keepdims=True))).astype(bf16) for p, gp in zip(probs, ups)]
+            results = []
             for i, (b, at) in enumerate(units):
                 r0, n = buckets[b]
                 rows = pl.ds(r0, n)
@@ -294,9 +297,14 @@
                 gv = [dot_tn(probs[u].astype(bf16), go2) for u in two]
                 gq = [dot_nn(gs[u], k2) for u in two]
                 gk = [dot_tn(gs[u], q2) for u in two]
-                q_ref[rows, at] = (jnp.where(first, gq[0], gq[1]) * scale).astype(bf16)
-                k_ref[rows, at] = (jnp.where(first, gk[0], gk[1]) * scale).astype(bf16)
-                v_ref[rows, at] = jnp.where(first, gv[0], gv[1]).astype(bf16)
+                results.append(((jnp.where(first, gq[0], gq[1]) * scale).astype(bf16),
+                                (jnp.where(first, gk[0], gk[1]) * scale).astype(bf16),
+                                jnp.where(first, gv[0], gv[1]).astype(bf16)))
+            for (b, at), (gq, gk, gv) in zip(units, results):
+                rows = pl.ds(*buckets[b])
+                q_ref[rows, at] = gq
+                k_ref[rows, at] = gk
+                v_ref[rows, at] = gv
         head_loop(bs, body, lo, hi)
 
     q_ref, k_ref, v_ref = gr.at[8], gr.at[9], gr.at[10]
@@ -370,7 +378,7 @@
             for t in range(tiles):
                 at = pl.ds(t * 256, 256)
                 wide = pl.ds(pl.multiple_of(j * width + t * 256, 256), 256)
-                value = dot_nt(gr[0, rows, :], wout[wide, :])
+                value = dot_nt(obuf[rows, :], wout[wide, :])
                 gr[1 + j, rows, at] = (value * dg[j, rows, at].astype(f32)).astype(bf16)
             if last:
                 remote(gr.at[1 + j], grp.at[1 + j], gr_send.at[1 + j], gr_recv.at[1 + j], core_id).start()
@@ -541,7 +549,7 @@
         for bs in (short, long):
             for h in range(2):
                 gm_part(bs[0], h).wait_recv()
-            norm_backward(bs, u_ffn, up, ffn_gain, ffn_at + 1, grad, gr.at[0])
+            norm_backward(bs, u_ffn, up, ffn_gain, ffn_at + 1, grad, gr.at[0], obuf)
             gr_first[bs[0]].start()
             if bs == short:
                 ffn_inner(bs, 0, slots, False)
@@ -605,7 +613,7 @@
         ffn_forward(both, hw, True, True, True)
         for k in range(4):
             lt_copy[k].start()
-        norm_backward(both, u_ffn, up, ffn_gain, ffn_at + 1, grad, gr.at[0])
+        norm_backward(both, u_ffn, up, ffn_gain, ffn_at + 1, grad, gr.at[0], obuf)
         gr_first[0].start()
         gr_first[1].start()
         ffn_inner(both, 0, slots, True)

time: 162 us -> 159 us (0.981)
  Pallas kernels: 161 us -> 158 us
    pallas_call x1, Pallas kernels: 157 us -> 154 us  [whole_step(): pl.pallas_call(functools.partial(step_kernel, width, hidden), out_shape=[...]
where the time goes in v7:
time: 159 us
  Pallas kernels  158 us (99%)
    pallas_call x1, Pallas kernels, whole_step(): pl.pallas_call(functools.partial(step_kernel, width, hidden), out_shape=[...  154 us
    pallas_call x1, Pallas kernels, whole_step(): pl.pallas_call(functools.partial(last_kernel, width), out_shape=[jax.Shap...  4.02 us

profile of v7, /device:TPU:0, one launch (start us, length us, event | category | flops | bytes accessed | tf_op | source)
XLA Modules:
  0.0 158.9 jit_solution(9372102079986472349)
XLA Ops:
  0.6 154.0 %step.1 = (bf16[384,768]{1,0:T(8,128)(2,1)}, f32[384,768]{1,0:T(8,128)}, bf16[14,48,768]{2,1,0:T(8,128)(2,1)}, bf16[14,48,768]{2,1,0:T(8,128)(2,1)}, f32[2,24,768]{2,1,0:T(8,128)}) custom-call(s32[2,1,2]{2,1,0:T(1,128)} %lengths.1, bf16[5,768]{1,0:T(8,128)(2,1)} %gains.1, bf16[24,768]{1,0:T(8,128)(2,1)} %biases.1, bf16[384,768]{1,0:T(8,128)(2,1)} %bitcast.21, ...), custom_call_target="tpu_custom_call" | custom-call | tf_op jit(solution)/shard_map/step/pallas_call | solution.py:881
  154.7 4.0 %last.1 = (bf16[384,768]{1,0:T(8,128)(2,1)}, f32[384,768]{1,0:T(8,128)}, f32[192,768]{1,0:T(8,128)}, f32[48,3072]{1,0:T(8,128)}, f32[48,768]{1,0:T(8,128)}, /*in...) custom-call(bf16[384,768]{1,0:T(8,128)(2,1)} %get-tuple-element.25.rows_in, ...), custom_call_target="tpu_custom_call" | custom-call | tf_op jit(solution)/shard_map/last/pallas_call | solution.py:930

commit v8 on v7

--- a/solution.py
+++ b/solution.py
@@ -232,6 +232,8 @@
     def masked_scores(q_half, k2, n, length, diagonal):
         s = dot_nt(q_half, k2)
         column = lax.broadcasted_iota(jnp.int32, (n, n), 1)
+        if diagonal is None:
+            return jnp.where(column < length, s, -1e30)
         row = lax.broadcasted_iota(jnp.int32, (n, n), 0)
         return jnp.where((column < length) & (column <= row + diagonal), s, -1e30)
 
@@ -243,8 +245,8 @@
         lane = lax.broadcasted_iota(jnp.int32, (n, 2 * HDIM), 1)
         return lane < HDIM
 
-    def head_loop(bs, body, lo=0, hi=None):
-        pairs = {short: 3, long: 2, both: 1}[bs]
+    def head_loop(bs, body, lo=0, hi=None, more=False):
+        pairs = {short: 6 if more else 3, long: 3 if more else 2, both: 1}[bs]
 
         def step(p, carry):
             body([(b, pl.ds(pl.multiple_of((p * pairs + i) * 2 * HDIM, 2 * HDIM), 2 * HDIM)) for b in bs for i in range(pairs)])
@@ -269,7 +271,7 @@
                 if bias_row is not None:
                     att = att + vec[pl.ds(bias_row, 1), at]
                 out_ref[pl.ds(r0, n), at] = att.astype(bf16)
-        head_loop(bs, body, lo, hi)
+        head_loop(bs, body, lo, hi, True)
 
     def attend_backward(bs, q_ref, k_ref, v_ref, lengths_at, diagonal, lo=0, hi=None):
         scale = HDIM ** -0.5
@@ -405,7 +407,7 @@
                 kv[which, rows, at] = value.astype(bf16)
             return carry
         lax.fori_loop(0, 2, memory_kv, 0)
-        attend_forward(bs, gr.at[6], kv.at[0], kv.at[1], lens[:2], 4096, 20, obuf)
+        attend_forward(bs, gr.at[6], kv.at[0], kv.at[1], lens[:2], None, 20, obuf)
 
         def cross_out(at):
             acc[rows, at] = dot_nn(obuf[rows, :], wsecond[:, at])
@@ -422,7 +424,7 @@
 
     def cross_backward(bs):
         rows = at_rows(bs)
-        attend_backward(bs, gr.at[6], kv.at[0], kv.at[1], lens[:2], 4096)
+        attend_backward(bs, gr.at[6], kv.at[0], kv.at[1], lens[:2], None)
 
         def memory_half(h, carry):
             at = cols(h, half)
@@ -531,7 +533,7 @@
             self_project(bs, bs == long)
             if bs == long:
                 wx_start()
-            attend_forward(bs, q_ref, k_ref, v_ref, own_lens, diagonal, None, obuf)
+            attend_forward(bs, q_ref, k_ref, v_ref, own_lens, None, None, obuf)
             if bs == long:
                 loads[2].wait()
             self_output(bs)

time: 159 us -> 158 us (level)
  no operation moved by 1% of the time
where the time goes in v8:
time: 158 us
  Pallas kernels  157 us (99%)
    pallas_call x1, Pallas kernels, whole_step(): pl.pallas_call(functools.partial(step_kernel, width, hidden), out_shape=[...  153 us
    pallas_call x1, Pallas kernels, whole_step(): pl.pallas_call(functools.partial(last_kernel, width), out_shape=[jax.Shap...  4.02 us

profile of v8, /device:TPU:0, one launch (start us, length us, event | category | flops | bytes accessed | tf_op | source)
XLA Modules:
  0.0 157.9 jit_solution(5141072973670328141)
XLA Ops:
  0.6 153.1 %step.1 = (bf16[384,768]{1,0:T(8,128)(2,1)}, f32[384,768]{1,0:T(8,128)}, bf16[14,48,768]{2,1,0:T(8,128)(2,1)}, bf16[14,48,768]{2,1,0:T(8,128)(2,1)}, f32[2,24,768]{2,1,0:T(8,128)}) custom-call(s32[2,1,2]{2,1,0:T(1,128)} %lengths.1, bf16[5,768]{1,0:T(8,128)(2,1)} %gains.1, bf16[24,768]{1,0:T(8,128)(2,1)} %biases.1, bf16[384,768]{1,0:T(8,128)(2,1)} %bitcast.21, ...), custom_call_target="tpu_custom_call" | custom-call | tf_op jit(solution)/shard_map/step/pallas_call | solution.py:883
  153.7 4.0 %last.1 = (bf16[384,768]{1,0:T(8,128)(2,1)}, f32[384,768]{1,0:T(8,128)}, f32[192,768]{1,0:T(8,128)}, f32[48,3072]{1,0:T(8,128)}, f32[48,768]{1,0:T(8,128)}, /*in...) custom-call(bf16[384,768]{1,0:T(8,128)(2,1)} %get-tuple-element.25.rows_in, ...), custom_call_target="tpu_custom_call" | custom-call | tf_op jit(solution)/shard_map/last/pallas_call | solution.py:932
